TPU v7x, 512 devices: a whole 4x8x8 slice. The times are simulated.
512 devices in a mesh: section: 16 (over x_lo, z), dp: 16 (over y, x_hi), hid: 2 (over core).
Axes of the slice: x: 4 (x_hi: 2, x_lo: 2; x = x_hi * 2 + x_lo), y: 8, z: 8, core: 2. Of those that a mesh axis runs over, the one named last changes fastest.
Arguments:
- forward_input: bfloat16 [16, 3072, 2048], P('section', 'dp'), may hold values from -6 to 6
- backward_input: bfloat16 [16, 3072, 2048], P('section', 'dp'), may hold values from -6 to 6
- output_grad: bfloat16 [16, 3072, 2048], P('section', 'dp'), may hold values from -8 to 8
- norm_gain: float32 [16, 2048], P('section'), may hold values from 0.5 to 1.5
- in_weight: float32 [16, 2, 2048, 512], P('section', None, 'dp', 'hid'), may hold values from -0.125 to 0.125
- out_weight: float32 [16, 512, 2048], P('section', 'hid', 'dp'), may hold values from -0.25 to 0.25
- in_codes: int32 [16, 2, 2048, 512], P('section', None, 'dp', 'hid'), may hold values from 0 to 32511
- out_codes: int32 [16, 512, 2048], P('section', 'hid', 'dp'), may hold values from 0 to 32511
- in_scales: float32 [16, 2, 2, 2048, 2], P('section', None, None, 'dp', 'hid'), may hold values from 0.005 to 0.05
- out_scales: float32 [16, 2, 2, 2048], P('section', None, 'hid', 'dp'), may hold values from 0.005 to 0.05
- section_lags: int32 [16], P('section'), may hold values from 1 to 4
Outputs:
- next_input: bfloat16 [16, 3072, 2048], P('section', 'dp')
- input_grad: bfloat16 [16, 3072, 2048], P('section', 'dp')
- in_update: float32 [16, 2, 2048, 512], P('section', None, 'dp', 'hid')
- out_update: float32 [16, 512, 2048], P('section', 'hid', 'dp')
Inputs may be any that keep to these rules, and one draw needn't show every extreme that they name: `in_codes`: each code holds a first-moment code of 0 to 126 times 256 plus a second-moment code of 0 to 255. `out_codes`: each code holds a first-moment code of 0 to 126 times 256 plus a second-moment code of 0 to 255.
All inputs are finite; a program needn't handle non-finite values.
Results may differ from a plain program's by a relative error of at most 0.012.
Values may be sent and summed in bfloat16 or wider, within the bound.
No kernel may reach another device: no remote copies, remote signals or barrier semaphores. Data moves between devices by JAX's collectives and lax.ppermute only.
A program may use at most 64 MiB of HBM per device.

v0:
```python
import jax
import jax.numpy as jnp
from jax import lax
from jax.sharding import Mesh
from jax.sharding import PartitionSpec as P

QB = 256
STEP = 1000
DP = ("dp_0", "dp_1")


BETA_ONE = 0.9
BETA_TWO = 0.999
ADAM_EPS = 1e-08
NORM_EPS = 1e-06
LEARN_RATE = 0.003


def in_order(pieces, dim):
    pieces = jnp.moveaxis(pieces, 0, dim)
    lengths = pieces.shape
    return pieces.reshape(*lengths[:dim], lengths[dim] * lengths[dim + 1], *lengths[dim + 2 :])


def gather_together(arrays, axis, dims):
    flat = jnp.concatenate([a.reshape(-1) for a in arrays])
    lines, at, outs = (lax.all_gather(flat, axis), 0, [])
    for a, dim in zip(arrays, dims):
        pieces = lines[:, at : at + a.size].reshape(-1, *a.shape)
        outs.append(in_order(pieces, dim))
        at += a.size
    return tuple(outs)


def copy_for_each(x, axis):
    copies = jnp.broadcast_to(x, (lax.axis_size(axis), *x.shape))
    return lax.all_to_all(copies, axis, split_axis=0, concat_axis=0, tiled=True)


def taken_together(x, axis):
    everything = copy_for_each(x, axis)
    return jnp.sum(everything.astype(jnp.float32), axis=0)


def passed_along(block, axis, distance):
    devices = range(lax.axis_size(axis))
    route = [(i - distance, i) for i in devices if i - distance in devices]
    return lax.ppermute(block, axis, route)


def sum_by_axis(x, axes, dim):
    if not axes:
        return x
    nearer = lax.psum_scatter(x, axes[0], scatter_dimension=dim, tiled=True)
    return sum_by_axis(nearer, axes[1:], dim)


def dequant(codes, first_scale, second_scale):
    high = (codes // 256).astype(jnp.float32)
    low = (codes % 256).astype(jnp.float32)
    moment_m = first_scale * (high - 63.0) / 63.0
    moment_v = jnp.square(second_scale * (0.25 + 0.75 * low / 255.0))
    return (moment_m, moment_v)


def direction(moment_m, moment_v, count):
    return (
        moment_m
        / (1.0 - BETA_ONE**count)
        / (jnp.sqrt(moment_v / (1.0 - BETA_TWO**count)) + ADAM_EPS)
    )


def normalize(inputs, gain):
    values = inputs.astype(jnp.float32)
    factor = lax.rsqrt(jnp.mean(values * values, axis=-1, keepdims=True) + NORM_EPS)
    return ((values * factor * gain).astype(jnp.bfloat16), factor, values)


def local(
    forward_input,
    backward_input,
    output_grad,
    norm_gain,
    in_weight,
    out_weight,
    in_codes,
    out_codes,
    in_scales,
    out_scales,
    section_lags,
):
    lag_value = section_lags[0].astype(jnp.float32)
    gain = norm_gain[0]
    m_in, v_in = dequant(
        in_codes[0],
        jnp.repeat(in_scales[0, 0], QB, axis=-1),
        jnp.repeat(in_scales[0, 1], QB, axis=-1),
    )
    m_out, v_out = dequant(
        out_codes[0],
        jnp.repeat(out_scales[0, 0], QB, axis=0),
        jnp.repeat(out_scales[0, 1], QB, axis=0),
    )
    pred_in = (in_weight[0] - LEARN_RATE * lag_value * direction(m_in, v_in, STEP - 1)).astype(
        jnp.bfloat16
    )
    pred_out = (out_weight[0] - LEARN_RATE * lag_value * direction(m_out, v_out, STEP - 1)).astype(
        jnp.bfloat16
    )
    full_in, full_out = gather_together((pred_in, pred_out), DP, (1, 1))
    normed, factor, values = normalize(forward_input[0], gain)
    gate_val = jnp.dot(normed, full_in[0], preferred_element_type=jnp.float32)
    up_val = jnp.dot(normed, full_in[1], preferred_element_type=jnp.float32)
    hidden = (gate_val * jax.nn.sigmoid(gate_val) * up_val).astype(jnp.bfloat16)
    partial_value = jnp.dot(hidden, full_out, preferred_element_type=jnp.float32)
    back_in, back_out = (full_in, full_out)
    out_cot = output_grad[0]
    normed_b, factor_b, values_b = normalize(backward_input[0], gain)
    gate_b = jnp.dot(normed_b, back_in[0], preferred_element_type=jnp.float32)
    up_b = jnp.dot(normed_b, back_in[1], preferred_element_type=jnp.float32)
    sig_b = jax.nn.sigmoid(gate_b)
    hidden_b = (gate_b * sig_b * up_b).astype(jnp.bfloat16)
    grad_h = jnp.dot(out_cot, back_out.T, preferred_element_type=jnp.float32)
    grad_gate = (grad_h * up_b * sig_b * (1.0 + gate_b * (1.0 - sig_b))).astype(jnp.bfloat16)
    grad_up = (grad_h * gate_b * sig_b).astype(jnp.bfloat16)
    grad_part = jnp.dot(grad_gate, back_in[0].T, preferred_element_type=jnp.float32) + jnp.dot(
        grad_up, back_in[1].T, preferred_element_type=jnp.float32
    )
    summed, grad_n = (
        taken_together(partial_value.astype(jnp.bfloat16), "hid").astype(jnp.float32),
        taken_together(grad_part.astype(jnp.bfloat16), "hid").astype(jnp.float32),
    )
    ahead = (values + summed).astype(jnp.bfloat16)
    next_rows = passed_along(ahead, "section", 1)
    scaled = gain * grad_n
    grad_x = (
        out_cot.astype(jnp.float32)
        + factor_b * scaled
        - values_b * factor_b**3 * jnp.mean(scaled * values_b, axis=-1, keepdims=True)
    )
    back_rows = passed_along(grad_x.astype(jnp.bfloat16), "section", -1)
    local_in = jnp.stack(
        [
            jnp.dot(normed_b.T, grad_gate, preferred_element_type=jnp.float32),
            jnp.dot(normed_b.T, grad_up, preferred_element_type=jnp.float32),
        ]
    )
    local_out = jnp.dot(hidden_b.T, out_cot, preferred_element_type=jnp.float32)
    sum_in, sum_out = (
        sum_by_axis(local_in.astype(jnp.bfloat16), DP, 1).astype(jnp.float32),
        sum_by_axis(local_out.astype(jnp.bfloat16), DP, 1).astype(jnp.float32),
    )
    rows_all = out_cot.shape[0] * lax.axis_size(DP)
    grad_in = sum_in / rows_all
    grad_out = sum_out / rows_all
    new_m_in = BETA_ONE * m_in + (1.0 - BETA_ONE) * grad_in
    new_v_in = BETA_TWO * v_in + (1.0 - BETA_TWO) * grad_in * grad_in
    new_m_out = BETA_ONE * m_out + (1.0 - BETA_ONE) * grad_out
    new_v_out = BETA_TWO * v_out + (1.0 - BETA_TWO) * grad_out * grad_out
    in_update = direction(new_m_in, new_v_in, STEP)
    out_update = direction(new_m_out, new_v_out, STEP)
    return (next_rows[None], back_rows[None], in_update[None], out_update[None])


def solution(mesh):
    split = Mesh(
        mesh.devices.reshape(mesh.shape["section"], 8, 2, mesh.shape["hid"]),
        ("section", "dp_0", "dp_1", "hid"),
    )
    return jax.shard_map(
        local,
        mesh=split,
        in_specs=(
            P("section", DP, None),
            P("section", DP, None),
            P("section", DP, None),
            P("section", None),
            P("section", None, DP, "hid"),
            P("section", "hid", DP),
            P("section", None, DP, "hid"),
            P("section", "hid", DP),
            P("section", None, None, DP, "hid"),
            P("section", None, "hid", DP),
            P("section"),
        ),
        out_specs=(
            P("section", DP, None),
            P("section", DP, None),
            P("section", None, DP, "hid"),
            P("section", "hid", DP),
        ),
        check_vma=False,
    )
```

profile of v0, /device:TPU:1, one launch (start us, length us, event | category | flops | bytes accessed | tf_op | source)
XLA Modules:
  0.0 263.6 jit_solution(4497651772757236221)
XLA Ops:
  8.0 0.7 slice_bitcast_fusion.2
  8.6 0.7 fusion.129
  10.9 0.7 pad_maximum_fusion.1
  12.5 99.0 %all-gather.3.cloned.1.call-done = bf16[1572864]{0:T(1024)(128)(2,1)} async-done(((bf16[98304]{0:T(1024)(128)(2,1)}), bf16[1572864]{0:T(1024)(128)(2,1)}) %all-gather.3.cloned.1.call-update) | async-done | bytes 3145744 | tf_op jit(solution)/shard_map/all_gather | solution.py:27
  111.4 2.8 %reshape.162 = bf16[16,98304]{1,0:T(8,128)(2,1)S(1)} reshape(bf16[1572864]{0:T(1024)(128)(2,1)} %all-gather.3.cloned.1.call-done) | data formatting | bytes 6291456 | tf_op jit(solution)/shard_map/all_gather | solution.py:27
  115.1 0.9 copy-done.1
  117.5 1.5 convolution_convert_fusion
  122.7 1.5 pad_maximum_fusion
  124.3 1.5 fusion.9
  125.8 1.6 fusion.71
  127.4 2.6 convolution_convert_fusion.3
  130.0 1.4 broadcast_in_dim.12
  131.3 7.9 %all-to-all-start = ((bf16[2,192,2048]{2,1,0:T(8,128)(2,1)}), bf16[2,192,2048]{2,1,0:T(8,128)(2,1)S(1)}, u32[]{:S(2)}, u32[]{:S(2)}) async-start(bf16[2,192,2048]{2,1,0:T(8,128)(2,1)} %broadcast_in_dim.12), calls=%async_computation | async-start | bytes 3145728 | tf_op jit(solution)/shard_map/all_to_all | solution.py:37
  139.3 1.8 fusion.130
  141.1 1.4 fusion
  142.5 2.5 broadcast_in_dim.27
  145.0 4.7 %all-to-all-start.1 = ((bf16[2,192,2048]{2,1,0:T(8,128)(2,1)}), bf16[2,192,2048]{2,1,0:T(8,128)(2,1)}, u32[]{:S(2)}, u32[]{:S(2)}) async-start(bf16[2,192,2048]{2,1,0:T(8,128)(2,1)} %broadcast_in_dim.27), calls=%async_computation.1 | async-start | bytes 3145728 | tf_op jit(solution)/shard_map/all_to_all | solution.py:37
  150.0 0.8 copy-done.7
  150.8 1.1 fusion.10
  151.9 3.3 %collective-permute-start = (bf16[192,2048]{1,0:T(8,128)(2,1)}, bf16[192,2048]{1,0:T(8,128)(2,1)S(1)}, u32[]{:S(2)}, u32[]{:S(2)}) collective-permute-start(bf16[192,2048]{1,0:T(8,128)(2,1)} %fusion.10), channel_id=1, source_target_pairs={{0,32},{32,64},{64,96},{96,128},{128,160},{160,192},{192,224},{224... | collective-permute-start | bytes 2359304 | tf_op jit(solution)/shard_map/ppermute | solution.py:48
  155.2 1.9 convert_reduce_fusion
  157.5 0.8 copy-done.10
  158.8 1.3 collective-permute-start.1
  160.2 1.7 copy.18
  161.9 42.0 %reduce-scatter.7.cloned.1.call-done = bf16[2,256,256]{2,1,0:T(8,128)(2,1)} async-done(((bf16[2,2048,256]{2,1,0:T(8,128)(2,1)}), bf16[2,256,256]{2,1,0:T(8,128)(2,1)}) %reduce-scatter.7.cloned.1.call-update) | async-done | bytes 262160 | tf_op jit(solution)/shard_map/reduce_scatter | solution.py:54
  204.0 25.9 %reduce-scatter.13.cloned.1.call-done = bf16[128,256]{1,0:T(8,128)(2,1)} async-done(((bf16[256,256]{1,0:T(8,128)(2,1)}), bf16[128,256]{1,0:T(8,128)(2,1)}) %reduce-scatter.13.cloned.1.call-update) | async-done | bytes 65552
  229.9 0.9 copy.19
  230.8 0.9 fusion.119
  231.7 21.5 %reduce-scatter.9.cloned.1.call-done = bf16[2,128,256]{2,1,0:T(8,128)(2,1)} async-done(((bf16[2,256,256]{2,1,0:T(8,128)(2,1)}), bf16[2,128,256]{2,1,0:T(8,128)(2,1)}) %reduce-scatter.9.cloned.1.call-update) | async-done | bytes 131088 | tf_op jit(solution)/shard_map/reduce_scatter | solution.py:54
  253.2 2.1 fusion.62
  255.3 0.9 copy.29
  256.2 0.9 copy.30
  (98 shorter events, 9.6 us)
Async XLA Ops:
  7.2 2.7 %copy-start.15 = (f32[1,2,128,256]{3,2,1,0:T(8,128)S(1)}, f32[1,2,128,256]{3,2,1,0:T(8,128)}, u32[]{:S(2)}) copy-start(f32[1,2,128,256]{3,2,1,0:T(8,128)} %param.15) | copy-start | bytes 786436
  7.2 2.8 %copy-start.12 = (s32[1,2,128,256]{3,2,1,0:T(8,128)S(1)}, s32[1,2,128,256]{3,2,1,0:T(8,128)}, u32[]{:S(2)}) copy-start(s32[1,2,128,256]{3,2,1,0:T(8,128)} %param.17) | copy-start | bytes 786436
  7.2 3.0 %copy-start.14 = (s32[1,256,128]{2,1,0:T(8,128)S(1)}, s32[1,256,128]{2,1,0:T(8,128)}, u32[]{:S(2)}) copy-start(s32[1,256,128]{2,1,0:T(8,128)} %param.18) | copy-start | bytes 393220
  7.2 3.0 %copy-start.18 = (f32[1,256,128]{2,1,0:T(8,128)S(1)}, f32[1,256,128]{2,1,0:T(8,128)}, u32[]{:S(2)}) copy-start(f32[1,256,128]{2,1,0:T(8,128)} %param.16) | copy-start | bytes 393220
  7.2 104.2 %all-gather.3.cloned.1.call-start = ((), (), s32[]{:S(2)}) async-start(), calls=%async_computation.9 | async-start | bytes 3342336 | tf_op jit(solution)/shard_map/all_gather | solution.py:27
  8.6 2.2 copy-start.23
  8.6 2.2 copy-start.25
  9.8 1.8 copy-start
  11.6 148.6 %reduce-scatter.11.cloned.1.call-start = ((), (), s32[]{:S(2)}) async-start(), calls=%async_computation.8 | async-start | bytes 1179648 | tf_op jit(solution)/shard_map/reduce_scatter | solution.py:54
  12.4 109.6 %copy-start.28 = (f32[192]{0:T(256)}, f32[192]{0:T(256)S(1)}, u32[]{:S(2)}) copy-start(f32[192]{0:T(256)S(1)} %get-tuple-element.11) | copy-start | bytes 2308
  115.1 1.8 copy-start.3
  115.1 1.8 copy-start.5
  116.4 1.1 copy-start.8
  119.0 84.9 %reduce-scatter.7.cloned.1.call-start = ((), (), s32[]{:S(2)}) async-start(), calls=%async_computation.6 | async-start | bytes 2359296 | tf_op jit(solution)/shard_map/reduce_scatter | solution.py:54
  119.4 1.2 copy-start.17
  119.9 2.2 copy-start.11
  119.9 1.6 copy-start.2
  120.9 1.2 copy-start.19
  120.9 1.2 copy-start.21
  124.2 1.6 copy-start.6
  124.2 3.1 %copy-start.4 = (bf16[1,16,128,256]{3,2,0,1:T(8,128)(2,1)S(1)}, bf16[1,16,128,256]{3,2,0,1:T(8,128)(2,1)}, u32[]{:S(2)}) copy-start(bf16[1,16,128,256]{3,2,0,1:T(8,128)(2,1)} %copy-done.3) | copy-start | bytes 3145732
  131.3 11.1 %all-to-all-start = ((bf16[2,192,2048]{2,1,0:T(8,128)(2,1)}), bf16[2,192,2048]{2,1,0:T(8,128)(2,1)S(1)}, u32[]{:S(2)}, u32[]{:S(2)}) async-start(bf16[2,192,2048]{2,1,0:T(8,128)(2,1)} %broadcast_in_dim.12), calls=%async_computation | async-start | bytes 3145728 | tf_op jit(solution)/shard_map/all_to_all | solution.py:37
  139.3 1.8 copy-start.20
  145.0 10.2 %all-to-all-start.1 = ((bf16[2,192,2048]{2,1,0:T(8,128)(2,1)}), bf16[2,192,2048]{2,1,0:T(8,128)(2,1)}, u32[]{:S(2)}, u32[]{:S(2)}) async-start(bf16[2,192,2048]{2,1,0:T(8,128)(2,1)} %broadcast_in_dim.27), calls=%async_computation.1 | async-start | bytes 3145728 | tf_op jit(solution)/shard_map/all_to_all | solution.py:37
  149.7 1.1 copy-start.7
  149.7 80.2 %reduce-scatter.13.cloned.1.call-start = ((), (), s32[]{:S(2)}) async-start(), calls=%async_computation.10 | async-start | bytes 196608
  151.9 52.1 %collective-permute-start = (bf16[192,2048]{1,0:T(8,128)(2,1)}, bf16[192,2048]{1,0:T(8,128)(2,1)S(1)}, u32[]{:S(2)}, u32[]{:S(2)}) collective-permute-start(bf16[192,2048]{1,0:T(8,128)(2,1)} %fusion.10), channel_id=1, source_target_pairs={{0,32},{32,64},{64,96},{96,128},{128,160},{160,192},{192,224},{224... | collective-permute-start | bytes 2359304 | tf_op jit(solution)/shard_map/ppermute | solution.py:48
  158.3 72.5 %copy-start.24 = (f32[128]{0:T(128)S(1)}, f32[128]{0:T(128)}, u32[]{:S(2)}) copy-start(f32[128]{0:T(128)} %copy-done.23) | copy-start | bytes 1540
  158.3 72.5 %copy-start.26 = (f32[128]{0:T(128)S(1)}, f32[128]{0:T(128)}, u32[]{:S(2)}) copy-start(f32[128]{0:T(128)} %copy-done.25) | copy-start | bytes 1540
  158.3 94.9 %copy-start.13 = (s32[1,2,128,256]{3,2,1,0:T(8,128)S(1)}, s32[1,2,128,256]{3,2,1,0:T(8,128)}, u32[]{:S(2)}) copy-start(s32[1,2,128,256]{3,2,1,0:T(8,128)} %param.17) | copy-start | bytes 786436
  158.8 45.1 %collective-permute-start.1 = (bf16[192,2048]{1,0:T(8,128)(2,1)S(1)}, bf16[192,2048]{1,0:T(8,128)(2,1)S(1)}, u32[]{:S(2)}, u32[]{:S(2)}) collective-permute-start(bf16[192,2048]{1,0:T(8,128)(2,1)S(1)} %fusion.16), channel_id=1, source_target_pairs={{32,0},{64,32},{96,64},{128,96},{160,128},{192,160},{224,192},{256... | collective-permute-start | bytes 2359304 | tf_op jit(solution)/shard_map/ppermute | solution.py:48
  161.8 91.4 %reduce-scatter.9.cloned.1.call-start = ((), (), s32[]{:S(2)}) async-start(), calls=%async_computation.7 | async-start | bytes 393216 | tf_op jit(solution)/shard_map/reduce_scatter | solution.py:54
  (7 other events, 7.5 us)
Sparse Core Ops, SparseCore 0:
  11.8 99.6 all-gather.2
  119.1 36.8 reduce-scatter.10
  158.9 44.9 reduce-scatter.6
  207.1 22.6 reduce-scatter.12
  232.5 20.6 reduce-scatter.8
where the time goes:
time: 264 us
  waiting for transfers between devices  188 us (71%)
  local copies, waits for them, and re-layouts  19.1 us (7%)
  starting transfers between devices  17.4 us (7%)
  between operations  15.1 us (6%)
  other arithmetic  12.4 us (5%)
  matrix products  11.2 us (4%)
    all_gather x1, waiting for transfers between devices, gather_together(): lines, at, outs = (lax.all_gather(flat, axis), 0, [])  99 us
    reduce_scatter x3, waiting for transfers between devices, sum_by_axis(): nearer = lax.psum_scatter(x, axes[0], scatter_dimension=dim, tiled=True)  63.5 us
    unnamed x6, waiting for transfers between devices  26 us
    all_to_all x2, starting transfers between devices, copy_for_each(): return lax.all_to_all(copies, axis, split_axis=0, concat_axis=0, tiled=True)  12.6 us
    unnamed x71, local copies, waits for them, and re-layouts  10 us
  transfers between devices with their start and end apart: 9, of which 4 were waited for; matrix products, arithmetic and copies ran while one was open for 10% of the time, Pallas kernels for 0%

commit v1 on v0

v1 whole, which is shorter than its diff:
```python
import functools

import jax
import jax.numpy as jnp
from jax import lax
from jax.experimental import pallas as pl
from jax.experimental.pallas import tpu as pltpu
from jax.sharding import Mesh
from jax.sharding import PartitionSpec as P

STEP = 1000
DP = ("y", "xh")
BETA_ONE = 0.9
BETA_TWO = 0.999
ADAM_EPS = 1e-08
NORM_EPS = 1e-06
LEARN_RATE = 0.003

F32 = jnp.float32
BF16 = jnp.bfloat16
VM = pl.BlockSpec(memory_space=pltpu.VMEM)
SM = pl.BlockSpec(memory_space=pltpu.SMEM)
NT = (((1,), (1,)), ((), ()))


def call(body, out, args, scratch=(), flops=0, n_smem=0, name=None):
    moved = sum(a.size * a.dtype.itemsize for a in (*args, *out))
    return pl.pallas_call(
        body,
        out_shape=tuple(jax.ShapeDtypeStruct(o.shape, o.dtype) for o in out),
        in_specs=[SM] * n_smem + [VM] * (len(args) - n_smem),
        out_specs=tuple(VM for _ in out),
        scratch_shapes=list(scratch),
        cost_estimate=pl.CostEstimate(flops=flops, bytes_accessed=moved, transcendentals=0),
        name=name,
    )(*args)


def struct(shape, dtype=BF16):
    return jax.ShapeDtypeStruct(shape, dtype)


def column(row, n):
    return jnp.broadcast_to(row, (n, row.shape[1])).T


def moments(codes, scale_m, scale_v):
    high = (codes >> 8).astype(F32)
    low = (codes & 255).astype(F32)
    return scale_m * (high - 63.0) / 63.0, scale_v * (0.25 + 0.75 * low / 255.0)


def predicted(weight, codes, scale_m, scale_v, rate):
    m, root = moments(codes, scale_m, scale_v)
    c1 = 1.0 - BETA_ONE ** (STEP - 1)
    c2 = (1.0 - BETA_TWO ** (STEP - 1)) ** 0.5
    return weight - rate * (m / c1 / (root / c2 + ADAM_EPS))


def predict_body(lag_ref, w_in, c_in, s_in, w_out, c_out, s_out, send):
    rate = LEARN_RATE * lag_ref[0].astype(F32)
    parts = []
    for i in range(2):
        sm = column(s_in[i : i + 1, :], 128)
        sv = column(s_in[2 + i : 3 + i, :], 128)
        parts.append([
            predicted(w_in[i, :, h * 128 : h * 128 + 128], c_in[i, :, h * 128 : h * 128 + 128], sm, sv, rate)
            for h in range(2)
        ])
    down = []
    for h in range(2):
        rows = slice(h * 128, h * 128 + 128)
        down.append(predicted(w_out[rows, :], c_out[rows, :], s_out[0:1, :], s_out[1:2, :], rate).T)
    parts.append(down)
    for i in range(3):
        for h in range(2):
            piece = parts[i][h].astype(BF16)
            for j in range(8):
                send[2 * j + h, :, i * 128 : i * 128 + 128] = piece


def rms(x):
    return lax.rsqrt(jnp.mean(x * x, axis=-1, keepdims=True) + NORM_EPS)


def gather_body(normed_arrays, k_ref, gain_ref, *refs):
    n = len(normed_arrays)
    ins, outs = refs[: 3 * n], refs[3 * n :]
    k = k_ref[0]
    gain = gain_ref[...]
    for a, norm in enumerate(normed_arrays):
        own, near, far = ins[3 * a : 3 * a + 3]
        out = outs[a]

        def step(i, carry, own=own, near=near, far=far, out=out, norm=norm):
            r = pl.multiple_of(i * 16, 16)
            rk = pl.multiple_of(k * 96 + i * 16, 16)
            rm = pl.multiple_of((1 - k) * 96 + i * 16, 16)
            for b, v in enumerate((own[pl.ds(rk, 16), :], own[pl.ds(rm, 16), :], near[pl.ds(r, 16), :], far[pl.ds(r, 16), :])):
                if norm:
                    x = v.astype(F32)
                    v = (x * rms(x) * gain).astype(BF16)
                out[pl.ds(pl.multiple_of(b * 96 + i * 16, 16), 16), :] = v
            return carry

        lax.fori_loop(0, 6, step, 0)


def backward_body(nb, dy, w, grads, dgu, gu_acc, dh_acc, left):
    gu_acc[...] = jnp.zeros_like(gu_acc)
    dh_acc[...] = jnp.zeros_like(dh_acc)

    def contract(j, carry):
        d = pl.ds(pl.multiple_of(j * 512, 512), 512)
        gu_acc[...] += jnp.dot(nb[:, d], w[d, 0:256], preferred_element_type=F32)
        dh_acc[...] += jnp.dot(dy[:, d], w[d, 256:384], preferred_element_type=F32)
        return carry

    lax.fori_loop(0, 4, contract, 0)
    for b in range(3):
        rows = slice(b * 128, b * 128 + 128)
        g, u, dh = gu_acc[rows, 0:128], gu_acc[rows, 128:256], dh_acc[rows, :]
        s = jax.nn.sigmoid(g)
        gs = g * s
        dg = dh * u * s * (1.0 + g * (1.0 - s))
        du = dh * gs
        dgu[rows, 0:128] = dg.astype(BF16)
        dgu[rows, 128:256] = du.astype(BF16)
        left[0:128, rows] = dg.T.astype(BF16)
        left[128:256, rows] = du.T.astype(BF16)
        left[256:384, rows] = (gs * u).T.astype(BF16)

    def expand(j, carry):
        d = pl.ds(pl.multiple_of(j * 256, 256), 256)
        a = jnp.dot(left[0:256, :], nb[:, d], preferred_element_type=F32).astype(BF16)
        b = jnp.dot(left[256:384, :], dy[:, d], preferred_element_type=F32).astype(BF16)
        for h in range(2):
            lanes = slice(h * 128, h * 128 + 128)
            grads[2 * j + h, 0:256, :] = a[:, lanes]
            grads[2 * j + h, 256:384, :] = b[:, lanes]
        return carry

    lax.fori_loop(0, 8, expand, 0)


def project(left, w, first, last, keep, send):
    def step(j, carry):
        d = pl.ds(pl.multiple_of(j * 256, 256), 256)
        r = lax.dot_general(left[...], w[d, first:last], NT, preferred_element_type=F32).astype(BF16)
        keep[0:96, d] = r[0:96]
        send[0:96, d] = r[96:192]
        keep[96:192, d] = r[192:288]
        send[96:192, d] = r[288:384]
        return carry

    lax.fori_loop(0, 8, step, 0)


def cotangent_body(dgu, w, keep, send):
    project(dgu, w, 0, 256, keep, send)


def forward_body(nf, w, keep, send, gu_acc, hidden):
    gu_acc[...] = jnp.zeros_like(gu_acc)

    def contract(j, carry):
        d = pl.ds(pl.multiple_of(j * 512, 512), 512)
        gu_acc[...] += jnp.dot(nf[:, d], w[d, 0:256], preferred_element_type=F32)
        return carry

    lax.fori_loop(0, 4, contract, 0)
    for b in range(3):
        rows = slice(b * 128, b * 128 + 128)
        g, u = gu_acc[rows, 0:128], gu_acc[rows, 128:256]
        hidden[rows, :] = (g * jax.nn.sigmoid(g) * u).astype(BF16)
    project(hidden, w, 256, 384, keep, send)


def pair_body(keep, recv, out):
    out[...] = (keep[96:192, :].astype(F32) + recv[96:192, :].astype(F32)).astype(BF16)


def total(keep, recv, other, rows):
    return keep[rows, :].astype(F32) + recv[rows, :].astype(F32) + other[rows, :].astype(F32)


def ahead_body(k_ref, x, keep, recv, other, out):
    k = k_ref[0]

    def step(i, carry):
        rows = pl.ds(pl.multiple_of(i * 16, 16), 16)
        mine = pl.ds(pl.multiple_of(k * 96 + i * 16, 16), 16)
        out[rows, :] = (x[mine, :].astype(F32) + total(keep, recv, other, rows)).astype(BF16)
        return carry

    lax.fori_loop(0, 6, step, 0)


def back_body(k_ref, gain_ref, x_ref, dy, keep, recv, other, out):
    k = k_ref[0]
    gain = gain_ref[...]

    def step(i, carry):
        rows = pl.ds(pl.multiple_of(i * 16, 16), 16)
        mine = pl.ds(pl.multiple_of(k * 96 + i * 16, 16), 16)
        x = x_ref[mine, :].astype(F32)
        r = rms(x)
        a = gain * total(keep, recv, other, rows)
        dot = jnp.mean(a * x, axis=-1, keepdims=True)
        out[rows, :] = (dy[mine, :].astype(F32) + r * a - x * (r * r * r * dot)).astype(BF16)
        return carry

    lax.fori_loop(0, 6, step, 0)


def stepped(m, root, grad):
    m2 = BETA_ONE * m + (1.0 - BETA_ONE) * grad
    v2 = BETA_TWO * (root * root) + (1.0 - BETA_TWO) * grad * grad
    return m2 / (1.0 - BETA_ONE**STEP) / (jnp.sqrt(v2 / (1.0 - BETA_TWO**STEP)) + ADAM_EPS)


def update_body(rows_all, recv, c_in, s_in, c_out, s_out, in_update, out_update):
    def summed(h, rows):
        acc = recv[h, rows, :].astype(F32)
        for j in range(1, 8):
            acc = acc + recv[2 * j + h, rows, :].astype(F32)
        return acc / rows_all

    for i in range(2):
        sm = column(s_in[i : i + 1, :], 128)
        sv = column(s_in[2 + i : 3 + i, :], 128)
        for h in range(2):
            lanes = slice(h * 128, h * 128 + 128)
            m, root = moments(c_in[i, :, lanes], sm, sv)
            in_update[i, :, lanes] = stepped(m, root, summed(h, slice(i * 128, i * 128 + 128)).T)
    for h in range(2):
        rows = slice(h * 128, h * 128 + 128)
        m, root = moments(c_out[rows, :], s_out[0:1, :], s_out[1:2, :])
        out_update[rows, :] = stepped(m, root, summed(h, slice(256, 384)))


def local(fwd, bwd, cot, gain, w_in, w_out, c_in, c_out, s_in, s_out, lags):
    x_f, x_b, dy = fwd[0], bwd[0], cot[0]
    c_in, c_out = c_in[0], c_out[0]
    s_in, s_out = s_in.reshape(4, 128), s_out.reshape(2, 128)
    k = lax.axis_index("hid")
    k_arr = k.astype(jnp.int32).reshape(1)
    swap = [(0, 1), (1, 0)]
    sections = lax.axis_size("section")

    def half(x):
        return lax.dynamic_slice_in_dim(x, k * 96, 96, 0)

    def across(x):
        return lax.ppermute(x, "xh", swap)

    def on_chip(x):
        return lax.ppermute(x, "hid", swap)

    def exchange(x):
        return lax.all_to_all(x, DP, 0, 0, tiled=True)

    (send,) = call(
        predict_body, [struct((16, 128, 384))],
        [lags, w_in[0], c_in, s_in, w_out[0], c_out, s_out], n_smem=1, name="predict",
    )
    weights = exchange(send).reshape(2048, 384)

    near_b, near_y, near_f = across(half(x_b)), across(half(dy)), across(half(x_f))
    far_b, far_y, far_f = on_chip(near_b), on_chip(near_y), on_chip(near_f)
    tokens = struct((384, 2048))
    nb, dyc = call(
        functools.partial(gather_body, (True, False)), [tokens, tokens],
        [k_arr, gain, x_b, near_b, far_b, dy, near_y, far_y], n_smem=1, name="gather_b",
    )
    (nf,) = call(
        functools.partial(gather_body, (True,)), [tokens],
        [k_arr, gain, x_f, near_f, far_f], n_smem=1, name="gather_f",
    )

    grads, dgu = call(
        backward_body, [struct((16, 384, 128)), struct((384, 256))], [nb, dyc, weights],
        scratch=[pltpu.VMEM((384, 256), F32), pltpu.VMEM((384, 128), F32), pltpu.VMEM((384, 384), BF16)],
        flops=4 * 384 * 384 * 2048, name="backward",
    )
    received = exchange(grads)

    part = struct((192, 2048))
    piece = struct((96, 2048))
    e_keep, e_send = call(cotangent_body, [part, part], [dgu, weights], flops=2 * 384 * 256 * 2048, name="cotangent")
    e_recv = on_chip(e_send)
    (e_pair,) = call(pair_body, [piece], [e_keep, e_recv], name="pair_e")
    e_other = across(e_pair)
    (back,) = call(back_body, [piece], [k_arr, gain, x_b, dy, e_keep, e_recv, e_other], n_smem=1, name="back")

    q_keep, q_send = call(
        forward_body, [part, part], [nf, weights],
        scratch=[pltpu.VMEM((384, 256), F32), pltpu.VMEM((384, 128), BF16)],
        flops=2 * 384 * 384 * 2048, name="forward",
    )
    q_recv = on_chip(q_send)
    (q_pair,) = call(pair_body, [piece], [q_keep, q_recv], name="pair_q")
    q_other = across(q_pair)
    (ahead,) = call(ahead_body, [piece], [k_arr, x_f, q_keep, q_recv, q_other], n_smem=1, name="ahead")

    def relay(x, distance):
        moves = [(s, s + distance) for s in range(sections) if 0 <= s + distance < sections]
        same = [(2 * s + h, 2 * t + h) for s, t in moves for h in range(2)]
        cross = [(2 * s + h, 2 * t + 1 - h) for s, t in moves for h in range(2)]
        axes = ("section", "hid")
        a, b = lax.ppermute(x, axes, same), lax.ppermute(x, axes, cross)
        first = jnp.where(k == 0, a, b)
        second = jnp.where(k == 0, b, a)
        return jnp.concatenate([first, second], axis=0)

    back_rows = relay(back, -1)
    next_rows = relay(ahead, 1)

    rows_all = dy.shape[0] * lax.axis_size(DP)
    in_update, out_update = call(
        functools.partial(update_body, float(rows_all)),
        [struct((2, 128, 256), F32), struct((256, 128), F32)],
        [received, c_in, s_in, c_out, s_out], name="update",
    )
    return next_rows[None], back_rows[None], in_update[None], out_update[None]


def solution(mesh):
    split = Mesh(
        mesh.devices.reshape(mesh.shape["section"], 8, 2, mesh.shape["hid"]),
        ("section", "y", "xh", "hid"),
    )
    return jax.shard_map(
        local,
        mesh=split,
        in_specs=(
            P("section", DP, None),
            P("section", DP, None),
            P("section", DP, None),
            P("section", None),
            P("section", None, DP, "hid"),
            P("section", "hid", DP),
            P("section", None, DP, "hid"),
            P("section", "hid", DP),
            P("section", None, None, DP, "hid"),
            P("section", None, "hid", DP),
            P("section"),
        ),
        out_specs=(
            P("section", DP, None),
            P("section", DP, None),
            P("section", None, DP, "hid"),
            P("section", "hid", DP),
        ),
        check_vma=False,
    )
```

time: 264 us -> 187 us (0.71)
  the two profiles are of different devices: /device:TPU:1 before, /device:TPU:3 now
where the time goes in v1:
time: 187 us; the launch traced here: 186 us
  starting transfers between devices  80.8 us (43%)
  waiting for transfers between devices  51.8 us (28%)
  Pallas kernels  42.3 us (23%)
  local copies, waits for them, and re-layouts  7.39 us (4%)
  other arithmetic  1.98 us (1%)
    pallas_call x11, Pallas kernels, call(): pl.pallas_call(body, out_shape=tuple((jax.ShapeDtypeStruct(o.shape, o.dty...  42.3 us
    ppermute x5, waiting for transfers between devices, across(): return lax.ppermute(x, 'xh', swap)  34.4 us
    ppermute x5, starting transfers between devices, on_chip(): return lax.ppermute(x, 'hid', swap)  25.3 us
    ppermute x4, starting transfers between devices, relay(): a, b = (lax.ppermute(x, axes, same), lax.ppermute(x, axes, cross))  19.7 us
    ppermute x5, starting transfers between devices, across(): return lax.ppermute(x, 'xh', swap)  18.6 us
    ppermute x4, waiting for transfers between devices, relay(): a, b = (lax.ppermute(x, axes, same), lax.ppermute(x, axes, cross))  17.4 us
    all_to_all x2, starting transfers between devices, exchange(): return lax.all_to_all(x, DP, 0, 0, tiled=True)  17.2 us
    unnamed x30, local copies, waits for them, and re-layouts  7.29 us
  transfers between devices with their start and end apart: 16, of which 7 were waited for; matrix products, arithmetic and copies ran while one was open for 1% of the time, Pallas kernels for 20%

profile of v1, /device:TPU:3, one launch (start us, length us, event | category | flops | bytes accessed | tf_op | source)
XLA Modules:
  0.0 185.8 jit_solution(18269272091255682124)
XLA Ops:
  1.3 2.8 %predict.1 = bf16[16,128,384]{2,1,0:T(8,128)(2,1)} custom-call(s32[1]{0:T(128)S(6)} %copy.15.lag_ref, f32[2,128,256]{2,1,0:T(8,128)} %bitcast.36, s32[2,128,256]{2,1,0:T(8,128)} %bitcast.32, f32[4,128]{1,0:T(4,128)} %bitcast.38, f32[256,128]{1,0:T(8,128)} %bitcast.37, s32[256,128]{1,0:T(8,128)} %bitcast.34, f32[2,128]{1,0:T(2,128)} %bitcast.40), custom_call_target="tpu_custom_call" | custom-call | bytes 2362372 | tf_op jit(solution)/shard_map/predict/pallas_call | solution.py:28
  4.1 8.6 %all-to-all-start = ((bf16[16,128,384]{2,1,0:T(8,128)(2,1)}), bf16[16,128,384]{2,1,0:T(8,128)(2,1)S(1)}, u32[]{:S(2)}, u32[]{:S(2)}) async-start(bf16[16,128,384]{2,1,0:T(8,128)(2,1)} %predict.1), calls=%async_computation | async-start | bytes 3145728 | tf_op jit(solution)/shard_map/all_to_all | solution.py:261
  12.8 4.9 %collective-permute-start.6 = (bf16[96,2048]{1,0:T(8,128)(2,1)S(1)}, bf16[96,2048]{1,0:T(8,128)(2,1)S(1)}, u32[]{:S(2)}, u32[]{:S(2)}) collective-permute-start(bf16[96,2048]{1,0:T(8,128)(2,1)S(1)} %dynamic-slice_bitcast_fusion.1), channel_id=1, source_target_pairs={{0,2},{2,0},{1,3},{3,1},{4,6},{6,4},{5,7},{7,5},{8,10},{10,8},{9,1... | collective-permute-start | bytes 1179656 | tf_op jit(solution)/shard_map/ppermute | solution.py:255
  17.7 2.0 %collective-permute-start.8 = (bf16[96,2048]{1,0:T(8,128)(2,1)S(1)}, bf16[96,2048]{1,0:T(8,128)(2,1)S(1)}, u32[]{:S(2)}, u32[]{:S(2)}) collective-permute-start(bf16[96,2048]{1,0:T(8,128)(2,1)S(1)} %dynamic-slice_bitcast_fusion), channel_id=1, source_target_pairs={{0,2},{2,0},{1,3},{3,1},{4,6},{6,4},{5,7},{7,5},{8,10},{10,8},{9,1... | collective-permute-start | bytes 1179656 | tf_op jit(solution)/shard_map/ppermute | solution.py:255
  19.8 4.8 %collective-permute-start = (bf16[96,2048]{1,0:T(8,128)(2,1)S(1)}, bf16[96,2048]{1,0:T(8,128)(2,1)S(1)}, u32[]{:S(2)}, u32[]{:S(2)}) collective-permute-start(bf16[96,2048]{1,0:T(8,128)(2,1)S(1)} %dynamic-slice_bitcast_fusion.2), channel_id=1, source_target_pairs={{0,2},{2,0},{1,3},{3,1},{4,6},{6,4},{5,7},{7,5},{8,10},{10,8},{9,1... | collective-permute-start | bytes 1179656 | tf_op jit(solution)/shard_map/ppermute | solution.py:255
  24.6 2.5 %collective-permute-done.6.refs_1_ = bf16[96,2048]{1,0:T(8,128)(2,1)S(1)} collective-permute-done((bf16[96,2048]{1,0:T(8,128)(2,1)S(1)}, bf16[96,2048]{1,0:T(8,128)(2,1)S(1)}, u32[]{:S(2)}, u32[]{:S(2)}) %collective-permute-start.6) | collective-permute-done | bytes 393248 | tf_op jit(solution)/shard_map/ppermute | solution.py:255
  27.1 4.4 %collective-permute-start.7 = (bf16[96,2048]{1,0:T(8,128)(2,1)S(1)}, bf16[96,2048]{1,0:T(8,128)(2,1)S(1)}, u32[]{:S(2)}, u32[]{:S(2)}) collective-permute-start(bf16[96,2048]{1,0:T(8,128)(2,1)S(1)} %collective-permute-done.6.refs_1_), channel_id=1, source_target_pairs={{0,1},{1,0},{2,3},{3,2},{4,5},{5,4},{6,7},{7,6},{8,9},{9,8},{10,11... | collective-permute-start | bytes 1179656 | tf_op jit(solution)/shard_map/ppermute | solution.py:258
  31.5 9.0 %collective-permute-done.8.refs_4_ = bf16[96,2048]{1,0:T(8,128)(2,1)S(1)} collective-permute-done((bf16[96,2048]{1,0:T(8,128)(2,1)S(1)}, bf16[96,2048]{1,0:T(8,128)(2,1)S(1)}, u32[]{:S(2)}, u32[]{:S(2)}) %collective-permute-start.8) | collective-permute-done | bytes 393248 | tf_op jit(solution)/shard_map/ppermute | solution.py:255
  40.6 13.0 %collective-permute-start.9 = (bf16[96,2048]{1,0:T(8,128)(2,1)S(1)}, bf16[96,2048]{1,0:T(8,128)(2,1)S(1)}, u32[]{:S(2)}, u32[]{:S(2)}) collective-permute-start(bf16[96,2048]{1,0:T(8,128)(2,1)S(1)} %collective-permute-done.8.refs_4_), channel_id=1, source_target_pairs={{0,1},{1,0},{2,3},{3,2},{4,5},{5,4},{6,7},{7,6},{8,9},{9,8},{10,11... | collective-permute-start | bytes 1179656 | tf_op jit(solution)/shard_map/ppermute | solution.py:258
  53.6 5.0 %collective-permute-done.refs_1_ = bf16[96,2048]{1,0:T(8,128)(2,1)S(1)} collective-permute-done((bf16[96,2048]{1,0:T(8,128)(2,1)S(1)}, bf16[96,2048]{1,0:T(8,128)(2,1)S(1)}, u32[]{:S(2)}, u32[]{:S(2)}) %collective-permute-start) | collective-permute-done | bytes 393248 | tf_op jit(solution)/shard_map/ppermute | solution.py:255
  58.6 3.2 %collective-permute-start.1 = (bf16[96,2048]{1,0:T(8,128)(2,1)S(1)}, bf16[96,2048]{1,0:T(8,128)(2,1)S(1)}, u32[]{:S(2)}, u32[]{:S(2)}) collective-permute-start(bf16[96,2048]{1,0:T(8,128)(2,1)S(1)} %collective-permute-done.refs_1_), channel_id=1, source_target_pairs={{0,1},{1,0},{2,3},{3,2},{4,5},{5,4},{6,7},{7,6},{8,9},{9,8},{10,11... | collective-permute-start | bytes 1179656 | tf_op jit(solution)/shard_map/ppermute | solution.py:258
  62.8 4.6 %gather_b.1 = (bf16[384,2048]{1,0:T(8,128)(2,1)}, bf16[384,2048]{1,0:T(8,128)(2,1)}) custom-call(s32[1]{0:T(128)} %bitcast.k_ref, f32[1,2048]{1,0:T(1,128)} %gain_ref.5, bf16[192,2048]{1,0:T(8,128)(2,1)} %bitcast.26, bf16[96,2048]{1,0:T(8,128)(2,1)} %copy-done.9, bf16[96,2048]{1,0:T(8,128)(2,1)} %copy-done.12, bf16[192,2048]{1,0:T(8,128)(2,1)} %bitcast.28, ...), custom_call_target="tpu_custom_call" | custom-call | bytes 6299652 | tf_op jit(solution)/shard_map/gather_b/pallas_call | solution.py:28
  68.6 7.3 %backward.1 = (bf16[16,384,128]{2,1,0:T(8,128)(2,1)}, bf16[384,256]{1,0:T(8,128)(2,1)}) custom-call(bf16[384,2048]{1,0:T(8,128)(2,1)} %get-tuple-element.16.nb, bf16[384,2048]{1,0:T(8,128)(2,1)} %get-tuple-element.17.dy, bf16[2048,384]{1,0:T(8,128)(2,1)} %bitcast.23), custom_call_target="tpu_custom_call" | custom-call | flops 1207959552 | bytes 6488064 | tf_op jit(solution)/shard_map/backward/pallas_call | solution.py:28
  75.9 4.6 %cotangent.1 = (bf16[192,2048]{1,0:T(8,128)(2,1)}, bf16[192,2048]{1,0:T(8,128)(2,1)}) custom-call(bf16[384,256]{1,0:T(8,128)(2,1)} %get-tuple-element.18.dgu, bf16[2048,384]{1,0:T(8,128)(2,1)} %bitcast.24), custom_call_target="tpu_custom_call" | custom-call | flops 402653184 | bytes 3342336 | tf_op jit(solution)/shard_map/cotangent/pallas_call | solution.py:28
  82.5 8.6 %all-to-all-start.1 = ((bf16[16,384,128]{2,1,0:T(8,128)(2,1)}), bf16[16,384,128]{2,1,0:T(8,128)(2,1)S(1)}, u32[]{:S(2)}, u32[]{:S(2)}) async-start(bf16[16,384,128]{2,1,0:T(8,128)(2,1)} %get-tuple-element.21), calls=%async_computation.1 | async-start | bytes 3145728 | tf_op jit(solution)/shard_map/all_to_all | solution.py:261
  91.8 3.5 %gather_f.1.nf = bf16[384,2048]{1,0:T(8,128)(2,1)} custom-call(s32[1]{0:T(128)} %bitcast.k_ref, f32[1,2048]{1,0:T(1,128)} %gain_ref.5, bf16[192,2048]{1,0:T(8,128)(2,1)} %bitcast.30, bf16[96,2048]{1,0:T(8,128)(2,1)} %copy-done.8, bf16[96,2048]{1,0:T(8,128)(2,1)} %copy-done.10), custom_call_target="tpu_custom_call" | custom-call | bytes 3153924 | tf_op jit(solution)/shard_map/gather_f/pallas_call | solution.py:28
  95.3 5.8 %forward.1 = (bf16[192,2048]{1,0:T(8,128)(2,1)}, bf16[192,2048]{1,0:T(8,128)(2,1)}) custom-call(bf16[384,2048]{1,0:T(8,128)(2,1)} %gather_f.1.nf, bf16[2048,384]{1,0:T(8,128)(2,1)} %bitcast.25), custom_call_target="tpu_custom_call" | custom-call | flops 603979776 | bytes 4718592 | tf_op jit(solution)/shard_map/forward/pallas_call | solution.py:28
  101.2 2.7 %collective-permute-start.2 = (bf16[192,2048]{1,0:T(8,128)(2,1)}, bf16[192,2048]{1,0:T(8,128)(2,1)S(1)}, u32[]{:S(2)}, u32[]{:S(2)}) collective-permute-start(bf16[192,2048]{1,0:T(8,128)(2,1)} %get-tuple-element.15), channel_id=1, source_target_pairs={{0,1},{1,0},{2,3},{3,2},{4,5},{5,4},{6,7},{7,6},{8,9},{9,8},{10,11... | collective-permute-start | bytes 2359304 | tf_op jit(solution)/shard_map/ppermute | solution.py:258
  104.7 2.2 %pair_e.1 = bf16[96,2048]{1,0:T(8,128)(2,1)} custom-call(bf16[192,2048]{1,0:T(8,128)(2,1)} %get-tuple-element.19.keep, bf16[192,2048]{1,0:T(8,128)(2,1)} %copy-done.5), custom_call_target="tpu_custom_call" | custom-call | bytes 1966080 | tf_op jit(solution)/shard_map/pair_e/pallas_call | solution.py:28
  107.0 5.0 %collective-permute-start.11 = (bf16[96,2048]{1,0:T(8,128)(2,1)}, bf16[96,2048]{1,0:T(8,128)(2,1)S(1)}, u32[]{:S(2)}, u32[]{:S(2)}) collective-permute-start(bf16[96,2048]{1,0:T(8,128)(2,1)} %pair_e.1), channel_id=1, source_target_pairs={{0,2},{2,0},{1,3},{3,1},{4,6},{6,4},{5,7},{7,5},{8,10},{10,8},{9,1... | collective-permute-start | bytes 1179656 | tf_op jit(solution)/shard_map/ppermute | solution.py:255
  112.9 2.2 %pair_q.1 = bf16[96,2048]{1,0:T(8,128)(2,1)} custom-call(bf16[192,2048]{1,0:T(8,128)(2,1)} %get-tuple-element.14.keep, bf16[192,2048]{1,0:T(8,128)(2,1)} %copy-done.6), custom_call_target="tpu_custom_call" | custom-call | bytes 1966080 | tf_op jit(solution)/shard_map/pair_q/pallas_call | solution.py:28
  117.0 17.8 %collective-permute-done.11.other = bf16[96,2048]{1,0:T(8,128)(2,1)S(1)} collective-permute-done((bf16[96,2048]{1,0:T(8,128)(2,1)}, bf16[96,2048]{1,0:T(8,128)(2,1)S(1)}, u32[]{:S(2)}, u32[]{:S(2)}) %collective-permute-start.11) | collective-permute-done | bytes 393248 | tf_op jit(solution)/shard_map/ppermute | solution.py:255
  135.6 3.6 %back.1 = bf16[96,2048]{1,0:T(8,128)(2,1)} custom-call(s32[1]{0:T(128)} %bitcast.k_ref, f32[1,2048]{1,0:T(1,128)} %gain_ref.5, bf16[192,2048]{1,0:T(8,128)(2,1)} %bitcast.27, bf16[192,2048]{1,0:T(8,128)(2,1)} %bitcast.29, bf16[192,2048]{1,0:T(8,128)(2,1)} %get-tuple-element.19.keep, bf16[192,2048]{1,0:T(8,128)(2,1)} %copy-done.5, bf16[96,2048]{1,0:T(8,128)(2,1)} %copy-done.7), custom_call_target="tpu_custom_call" | custom-call | bytes 3940356 | tf_op jit(solution)/shard_map/back/pallas_call | solution.py:28
  139.2 11.5 %collective-permute-start.12 = (bf16[96,2048]{1,0:T(8,128)(2,1)}, bf16[96,2048]{1,0:T(8,128)(2,1)S(1)}, u32[]{:S(2)}, u32[]{:S(2)}) collective-permute-start(bf16[96,2048]{1,0:T(8,128)(2,1)} %back.1), channel_id=1, source_target_pairs={{32,0},{33,1},{64,32},{65,33},{96,64},{97,65},{128,96},{129,97},{1... | collective-permute-start | bytes 1179656 | tf_op jit(solution)/shard_map/ppermute | solution.py:311
  150.8 3.1 %collective-permute-start.13 = (bf16[96,2048]{1,0:T(8,128)(2,1)}, bf16[96,2048]{1,0:T(8,128)(2,1)S(1)}, u32[]{:S(2)}, u32[]{:S(2)}) collective-permute-start(bf16[96,2048]{1,0:T(8,128)(2,1)} %back.1), channel_id=1, source_target_pairs={{32,1},{33,0},{64,33},{65,32},{96,65},{97,64},{128,97},{129,96},{1... | collective-permute-start | bytes 1179656 | tf_op jit(solution)/shard_map/ppermute | solution.py:311
  154.7 2.7 %ahead.1 = bf16[96,2048]{1,0:T(8,128)(2,1)} custom-call(s32[1]{0:T(128)} %bitcast.k_ref, bf16[192,2048]{1,0:T(8,128)(2,1)} %bitcast.31, bf16[192,2048]{1,0:T(8,128)(2,1)} %get-tuple-element.14.keep, bf16[192,2048]{1,0:T(8,128)(2,1)} %copy-done.6, bf16[96,2048]{1,0:T(8,128)(2,1)} %copy-done.13), custom_call_target="tpu_custom_call" | custom-call | bytes 3145732 | tf_op jit(solution)/shard_map/ahead/pallas_call | solution.py:28
  157.3 3.1 %collective-permute-start.4 = (bf16[96,2048]{1,0:T(8,128)(2,1)}, bf16[96,2048]{1,0:T(8,128)(2,1)S(1)}, u32[]{:S(2)}, u32[]{:S(2)}) collective-permute-start(bf16[96,2048]{1,0:T(8,128)(2,1)} %ahead.1), channel_id=1, source_target_pairs={{0,32},{1,33},{32,64},{33,65},{64,96},{65,97},{96,128},{97,129},{1... | collective-permute-start | bytes 1179656 | tf_op jit(solution)/shard_map/ppermute | solution.py:311
  160.4 1.9 %collective-permute-start.5 = (bf16[96,2048]{1,0:T(8,128)(2,1)}, bf16[96,2048]{1,0:T(8,128)(2,1)S(1)}, u32[]{:S(2)}, u32[]{:S(2)}) collective-permute-start(bf16[96,2048]{1,0:T(8,128)(2,1)} %ahead.1), channel_id=1, source_target_pairs={{0,33},{1,32},{32,65},{33,64},{64,97},{65,96},{96,129},{97,128},{1... | collective-permute-start | bytes 1179656 | tf_op jit(solution)/shard_map/ppermute | solution.py:311
  162.4 4.8 %collective-permute-done.13 = bf16[96,2048]{1,0:T(8,128)(2,1)S(1)} collective-permute-done((bf16[96,2048]{1,0:T(8,128)(2,1)}, bf16[96,2048]{1,0:T(8,128)(2,1)S(1)}, u32[]{:S(2)}, u32[]{:S(2)}) %collective-permute-start.13) | collective-permute-done | bytes 393248 | tf_op jit(solution)/shard_map/ppermute | solution.py:311
  168.2 4.1 %collective-permute-done.4 = bf16[96,2048]{1,0:T(8,128)(2,1)S(1)} collective-permute-done((bf16[96,2048]{1,0:T(8,128)(2,1)}, bf16[96,2048]{1,0:T(8,128)(2,1)S(1)}, u32[]{:S(2)}, u32[]{:S(2)}) %collective-permute-start.4) | collective-permute-done | bytes 393248 | tf_op jit(solution)/shard_map/ppermute | solution.py:311
  172.3 8.5 %collective-permute-done.5 = bf16[96,2048]{1,0:T(8,128)(2,1)S(1)} collective-permute-done((bf16[96,2048]{1,0:T(8,128)(2,1)}, bf16[96,2048]{1,0:T(8,128)(2,1)S(1)}, u32[]{:S(2)}, u32[]{:S(2)}) %collective-permute-start.5) | collective-permute-done | bytes 393248 | tf_op jit(solution)/shard_map/ppermute | solution.py:311
  183.0 2.9 %update.1 = (f32[2,128,256]{2,1,0:T(8,128)}, f32[256,128]{1,0:T(8,128)}) custom-call(bf16[16,384,128]{2,1,0:T(8,128)(2,1)} %copy-done.1, s32[2,128,256]{2,1,0:T(8,128)} %bitcast.33, f32[4,128]{1,0:T(4,128)} %bitcast.39, s32[256,128]{1,0:T(8,128)} %bitcast.35, f32[2,128]{1,0:T(2,128)} %bitcast.41), custom_call_target="tpu_custom_call" | custom-call | bytes 2362368 | tf_op jit(solution)/shard_map/update/pallas_call | solution.py:28
  (48 shorter events, 13.2 us)
Async XLA Ops:
  4.1 8.6 %copy-start.2 = (bf16[1,192,2048]{2,1,0:T(8,128)(2,1)S(1)}, bf16[1,192,2048]{2,1,0:T(8,128)(2,1)}, u32[]{:S(2)}) copy-start(bf16[1,192,2048]{2,1,0:T(8,128)(2,1)} %param.12) | copy-start | bytes 2359300
  4.1 13.6 %copy-start.3 = (bf16[1,192,2048]{2,1,0:T(8,128)(2,1)S(1)}, bf16[1,192,2048]{2,1,0:T(8,128)(2,1)}, u32[]{:S(2)}) copy-start(bf16[1,192,2048]{2,1,0:T(8,128)(2,1)} %param.13) | copy-start | bytes 2359300
  4.1 63.3 %all-to-all-start = ((bf16[16,128,384]{2,1,0:T(8,128)(2,1)}), bf16[16,128,384]{2,1,0:T(8,128)(2,1)S(1)}, u32[]{:S(2)}, u32[]{:S(2)}) async-start(bf16[16,128,384]{2,1,0:T(8,128)(2,1)} %predict.1), calls=%async_computation | async-start | bytes 3145728 | tf_op jit(solution)/shard_map/all_to_all | solution.py:261
  12.7 7.0 %copy-start.4 = (bf16[1,192,2048]{2,1,0:T(8,128)(2,1)S(1)}, bf16[1,192,2048]{2,1,0:T(8,128)(2,1)}, u32[]{:S(2)}) copy-start(bf16[1,192,2048]{2,1,0:T(8,128)(2,1)} %param.11) | copy-start | bytes 2359300
  12.8 14.3 %collective-permute-start.6 = (bf16[96,2048]{1,0:T(8,128)(2,1)S(1)}, bf16[96,2048]{1,0:T(8,128)(2,1)S(1)}, u32[]{:S(2)}, u32[]{:S(2)}) collective-permute-start(bf16[96,2048]{1,0:T(8,128)(2,1)S(1)} %dynamic-slice_bitcast_fusion.1), channel_id=1, source_target_pairs={{0,2},{2,0},{1,3},{3,1},{4,6},{6,4},{5,7},{7,5},{8,10},{10,8},{9,1... | collective-permute-start | bytes 1179656 | tf_op jit(solution)/shard_map/ppermute | solution.py:255
  17.7 22.8 %collective-permute-start.8 = (bf16[96,2048]{1,0:T(8,128)(2,1)S(1)}, bf16[96,2048]{1,0:T(8,128)(2,1)S(1)}, u32[]{:S(2)}, u32[]{:S(2)}) collective-permute-start(bf16[96,2048]{1,0:T(8,128)(2,1)S(1)} %dynamic-slice_bitcast_fusion), channel_id=1, source_target_pairs={{0,2},{2,0},{1,3},{3,1},{4,6},{6,4},{5,7},{7,5},{8,10},{10,8},{9,1... | collective-permute-start | bytes 1179656 | tf_op jit(solution)/shard_map/ppermute | solution.py:255
  19.8 38.8 %collective-permute-start = (bf16[96,2048]{1,0:T(8,128)(2,1)S(1)}, bf16[96,2048]{1,0:T(8,128)(2,1)S(1)}, u32[]{:S(2)}, u32[]{:S(2)}) collective-permute-start(bf16[96,2048]{1,0:T(8,128)(2,1)S(1)} %dynamic-slice_bitcast_fusion.2), channel_id=1, source_target_pairs={{0,2},{2,0},{1,3},{3,1},{4,6},{6,4},{5,7},{7,5},{8,10},{10,8},{9,1... | collective-permute-start | bytes 1179656 | tf_op jit(solution)/shard_map/ppermute | solution.py:255
  27.1 35.5 %copy-start.9 = (bf16[96,2048]{1,0:T(8,128)(2,1)}, bf16[96,2048]{1,0:T(8,128)(2,1)S(1)}, u32[]{:S(2)}) copy-start(bf16[96,2048]{1,0:T(8,128)(2,1)S(1)} %collective-permute-done.6.refs_1_) | copy-start | bytes 1179652
  27.1 34.7 %collective-permute-start.7 = (bf16[96,2048]{1,0:T(8,128)(2,1)S(1)}, bf16[96,2048]{1,0:T(8,128)(2,1)S(1)}, u32[]{:S(2)}, u32[]{:S(2)}) collective-permute-start(bf16[96,2048]{1,0:T(8,128)(2,1)S(1)} %collective-permute-done.6.refs_1_), channel_id=1, source_target_pairs={{0,1},{1,0},{2,3},{3,2},{4,5},{5,4},{6,7},{7,6},{8,9},{9,8},{10,11... | collective-permute-start | bytes 1179656 | tf_op jit(solution)/shard_map/ppermute | solution.py:258
  40.6 22.1 %copy-start.11 = (bf16[96,2048]{1,0:T(8,128)(2,1)}, bf16[96,2048]{1,0:T(8,128)(2,1)S(1)}, u32[]{:S(2)}) copy-start(bf16[96,2048]{1,0:T(8,128)(2,1)S(1)} %collective-permute-done.8.refs_4_) | copy-start | bytes 1179652
  40.6 21.3 %collective-permute-start.9 = (bf16[96,2048]{1,0:T(8,128)(2,1)S(1)}, bf16[96,2048]{1,0:T(8,128)(2,1)S(1)}, u32[]{:S(2)}, u32[]{:S(2)}) collective-permute-start(bf16[96,2048]{1,0:T(8,128)(2,1)S(1)} %collective-permute-done.8.refs_4_), channel_id=1, source_target_pairs={{0,1},{1,0},{2,3},{3,2},{4,5},{5,4},{6,7},{7,6},{8,9},{9,8},{10,11... | collective-permute-start | bytes 1179656 | tf_op jit(solution)/shard_map/ppermute | solution.py:258
  58.6 8.8 %copy-start.8 = (bf16[96,2048]{1,0:T(8,128)(2,1)}, bf16[96,2048]{1,0:T(8,128)(2,1)S(1)}, u32[]{:S(2)}) copy-start(bf16[96,2048]{1,0:T(8,128)(2,1)S(1)} %collective-permute-done.refs_1_) | copy-start | bytes 1179652
  58.6 32.5 %collective-permute-start.1 = (bf16[96,2048]{1,0:T(8,128)(2,1)S(1)}, bf16[96,2048]{1,0:T(8,128)(2,1)S(1)}, u32[]{:S(2)}, u32[]{:S(2)}) collective-permute-start(bf16[96,2048]{1,0:T(8,128)(2,1)S(1)} %collective-permute-done.refs_1_), channel_id=1, source_target_pairs={{0,1},{1,0},{2,3},{3,2},{4,5},{5,4},{6,7},{7,6},{8,9},{9,8},{10,11... | collective-permute-start | bytes 1179656 | tf_op jit(solution)/shard_map/ppermute | solution.py:258
  61.8 0.9 copy-start.12
  61.9 0.8 copy-start.14
  67.4 1.2 copy-start
  80.6 23.3 %collective-permute-start.10 = (bf16[192,2048]{1,0:T(8,128)(2,1)}, bf16[192,2048]{1,0:T(8,128)(2,1)S(1)}, u32[]{:S(2)}, u32[]{:S(2)}) collective-permute-start(bf16[192,2048]{1,0:T(8,128)(2,1)} %get-tuple-element.20), channel_id=1, source_target_pairs={{0,1},{1,0},{2,3},{3,2},{4,5},{5,4},{6,7},{7,6},{8,9},{9,8},{10,11... | collective-permute-start | bytes 2359304 | tf_op jit(solution)/shard_map/ppermute | solution.py:258
  82.5 99.3 %all-to-all-start.1 = ((bf16[16,384,128]{2,1,0:T(8,128)(2,1)}), bf16[16,384,128]{2,1,0:T(8,128)(2,1)S(1)}, u32[]{:S(2)}, u32[]{:S(2)}) async-start(bf16[16,384,128]{2,1,0:T(8,128)(2,1)} %get-tuple-element.21), calls=%async_computation.1 | async-start | bytes 3145728 | tf_op jit(solution)/shard_map/all_to_all | solution.py:261
  91.1 0.7 copy-start.10
  101.2 10.9 %collective-permute-start.2 = (bf16[192,2048]{1,0:T(8,128)(2,1)}, bf16[192,2048]{1,0:T(8,128)(2,1)S(1)}, u32[]{:S(2)}, u32[]{:S(2)}) collective-permute-start(bf16[192,2048]{1,0:T(8,128)(2,1)} %get-tuple-element.15), channel_id=1, source_target_pairs={{0,1},{1,0},{2,3},{3,2},{4,5},{5,4},{6,7},{7,6},{8,9},{9,8},{10,11... | collective-permute-start | bytes 2359304 | tf_op jit(solution)/shard_map/ppermute | solution.py:258
  103.9 0.9 copy-start.5
  107.0 27.9 %collective-permute-start.11 = (bf16[96,2048]{1,0:T(8,128)(2,1)}, bf16[96,2048]{1,0:T(8,128)(2,1)S(1)}, u32[]{:S(2)}, u32[]{:S(2)}) collective-permute-start(bf16[96,2048]{1,0:T(8,128)(2,1)} %pair_e.1), channel_id=1, source_target_pairs={{0,2},{2,0},{1,3},{3,1},{4,6},{6,4},{5,7},{7,5},{8,10},{10,8},{9,1... | collective-permute-start | bytes 1179656 | tf_op jit(solution)/shard_map/ppermute | solution.py:255
  112.0 0.9 copy-start.6
  115.1 38.8 %collective-permute-start.3 = (bf16[96,2048]{1,0:T(8,128)(2,1)}, bf16[96,2048]{1,0:T(8,128)(2,1)S(1)}, u32[]{:S(2)}, u32[]{:S(2)}) collective-permute-start(bf16[96,2048]{1,0:T(8,128)(2,1)} %pair_q.1), channel_id=1, source_target_pairs={{0,2},{2,0},{1,3},{3,1},{4,6},{6,4},{5,7},{7,5},{8,10},{10,8},{9,1... | collective-permute-start | bytes 1179656 | tf_op jit(solution)/shard_map/ppermute | solution.py:255
  134.9 0.7 copy-start.7
  139.2 23.1 %collective-permute-start.12 = (bf16[96,2048]{1,0:T(8,128)(2,1)}, bf16[96,2048]{1,0:T(8,128)(2,1)S(1)}, u32[]{:S(2)}, u32[]{:S(2)}) collective-permute-start(bf16[96,2048]{1,0:T(8,128)(2,1)} %back.1), channel_id=1, source_target_pairs={{32,0},{33,1},{64,32},{65,33},{96,64},{97,65},{128,96},{129,97},{1... | collective-permute-start | bytes 1179656 | tf_op jit(solution)/shard_map/ppermute | solution.py:311
  150.8 16.4 %collective-permute-start.13 = (bf16[96,2048]{1,0:T(8,128)(2,1)}, bf16[96,2048]{1,0:T(8,128)(2,1)S(1)}, u32[]{:S(2)}, u32[]{:S(2)}) collective-permute-start(bf16[96,2048]{1,0:T(8,128)(2,1)} %back.1), channel_id=1, source_target_pairs={{32,1},{33,0},{64,33},{65,32},{96,65},{97,64},{128,97},{129,96},{1... | collective-permute-start | bytes 1179656 | tf_op jit(solution)/shard_map/ppermute | solution.py:311
  153.9 0.7 copy-start.13
  157.3 15.0 %collective-permute-start.4 = (bf16[96,2048]{1,0:T(8,128)(2,1)}, bf16[96,2048]{1,0:T(8,128)(2,1)S(1)}, u32[]{:S(2)}, u32[]{:S(2)}) collective-permute-start(bf16[96,2048]{1,0:T(8,128)(2,1)} %ahead.1), channel_id=1, source_target_pairs={{0,32},{1,33},{32,64},{33,65},{64,96},{65,97},{96,128},{97,129},{1... | collective-permute-start | bytes 1179656 | tf_op jit(solution)/shard_map/ppermute | solution.py:311
  160.4 20.4 %collective-permute-start.5 = (bf16[96,2048]{1,0:T(8,128)(2,1)}, bf16[96,2048]{1,0:T(8,128)(2,1)S(1)}, u32[]{:S(2)}, u32[]{:S(2)}) collective-permute-start(bf16[96,2048]{1,0:T(8,128)(2,1)} %ahead.1), channel_id=1, source_target_pairs={{0,33},{1,32},{32,65},{33,64},{64,97},{65,96},{96,129},{97,128},{1... | collective-permute-start | bytes 1179656 | tf_op jit(solution)/shard_map/ppermute | solution.py:311
  181.8 1.2 copy-start.1

commit v2 on v1

v2 whole, which is shorter than its diff:
```python
import functools

import jax
import jax.numpy as jnp
from jax import lax
from jax.experimental import pallas as pl
from jax.experimental.pallas import tpu as pltpu
from jax.sharding import Mesh
from jax.sharding import PartitionSpec as P

STEP = 1000
DP = ("y", "xh")
BETA_ONE = 0.9
BETA_TWO = 0.999
ADAM_EPS = 1e-08
NORM_EPS = 1e-06
LEARN_RATE = 0.003

F32 = jnp.float32
BF16 = jnp.bfloat16
VM = pl.BlockSpec(memory_space=pltpu.VMEM)
HB = pl.BlockSpec(memory_space=pltpu.HBM)
SM = pl.BlockSpec(memory_space=pltpu.SMEM)
NT = (((1,), (1,)), ((), ()))


def call(body, out, args, scratch=(), flops=0, n_smem=0, hbm_in=(), hbm_out=(), alias=None):
    moved = sum(a.size * a.dtype.itemsize for a in (*args, *out))
    args = [pltpu.with_memory_space_constraint(a, pltpu.HBM) if i in hbm_in else a for i, a in enumerate(args)]
    specs = [HB if i in hbm_in else SM if i < n_smem else VM for i in range(len(args))]
    return pl.pallas_call(
        body,
        out_shape=tuple((pltpu.HBM if i in hbm_out else jax.ShapeDtypeStruct)(o.shape, o.dtype) for i, o in enumerate(out)),
        in_specs=specs,
        out_specs=tuple(HB if i in hbm_out else VM for i in range(len(out))),
        scratch_shapes=list(scratch),
        input_output_aliases=alias or {},
        compiler_params=pltpu.CompilerParams(vmem_limit_bytes=20 * 2**20),
        cost_estimate=pl.CostEstimate(flops=flops, bytes_accessed=moved, transcendentals=0),
    )(*args)


def struct(shape, dtype=BF16):
    return jax.ShapeDtypeStruct(shape, dtype)


def column(row, n):
    return jnp.broadcast_to(row, (n, row.shape[1])).T


def moments(codes, scale_m, scale_v):
    high = (codes >> 8).astype(F32)
    low = (codes & 255).astype(F32)
    return scale_m * (high - 63.0) / 63.0, scale_v * (0.25 + 0.75 * low / 255.0)


def predicted(weight, codes, scale_m, scale_v, rate):
    m, root = moments(codes, scale_m, scale_v)
    c1 = 1.0 - BETA_ONE ** (STEP - 1)
    c2 = (1.0 - BETA_TWO ** (STEP - 1)) ** 0.5
    return weight - rate * (m / c1 / (root / c2 + ADAM_EPS))


def predict_body(lag_ref, x_ref, *refs):
    hbm, give, send = refs[:6], refs[6], refs[7]
    w_in, c_in, s_in, w_out, c_out, s_out = refs[8:14]
    blocks_ref, in_sem, out_sem = refs[14:]
    xh = x_ref[0]
    loads = [pltpu.make_async_copy(hbm[i], refs[8 + i], in_sem.at[i]) for i in range(6)]
    for load in loads:
        load.start()
    for load in loads:
        load.wait()
    rate = LEARN_RATE * lag_ref[0].astype(F32)
    sm = [column(s_in[i : i + 1, :], 128) for i in range(2)]
    sv = [column(s_in[2 + i : 3 + i, :], 128) for i in range(2)]
    for h in range(2):
        lanes = slice(h * 128, h * 128 + 128)
        for i in range(2):
            piece = predicted(w_in[i, :, lanes], c_in[i, :, lanes], sm[i], sv[i], rate)
            blocks_ref[h, :, i * 128 : i * 128 + 128] = piece.astype(BF16)
        piece = predicted(w_out[lanes, :], c_out[lanes, :], s_out[0:1, :], s_out[1:2, :], rate)
        blocks_ref[h, :, 256:384] = piece.T.astype(BF16)
    give[...] = blocks_ref[1 - xh]
    stores = [pltpu.make_async_copy(blocks_ref.at[xh], send.at[j, xh], out_sem.at[j]) for j in range(8)]
    for store in stores:
        store.start()
    for store in stores:
        store.wait()


def halves_body(k_ref, *refs):
    rows = pl.ds(pl.multiple_of(k_ref[0] * 96, 32), 96)
    loads = [pltpu.make_async_copy(refs[i].at[rows, :], refs[3 + i], refs[6].at[i]) for i in range(3)]
    for load in loads:
        load.start()
    for load in loads:
        load.wait()


def fill_body(x_ref, other, _, send, sem):
    stores = [pltpu.make_async_copy(other, send.at[j, 1 - x_ref[0]], sem.at[j]) for j in range(8)]
    for store in stores:
        store.start()
    for store in stores:
        store.wait()


def rms(x):
    return lax.rsqrt(jnp.mean(x * x, axis=-1, keepdims=True) + NORM_EPS)


def normed_hbm_body(gain_ref, own, near, far, out, rows):
    normed_body(gain_ref, own, near, far, rows)
    pltpu.sync_copy(rows, out)


def normed_body(gain_ref, own, near, far, out):
    gain = gain_ref[...]

    def step(i, carry):
        r = pl.multiple_of(i * 16, 16)
        for start, ref, at in ((0, own, r), (96, own, 96 + r), (192, near, r), (288, far, r)):
            x = ref[pl.ds(pl.multiple_of(at, 16), 16), :].astype(F32)
            out[pl.ds(pl.multiple_of(start + r, 16), 16), :] = (x * rms(x) * gain).astype(BF16)
        return carry

    lax.fori_loop(0, 6, step, 0)


def blocks(k):
    first = pl.multiple_of(96 * k, 32)
    second = pl.multiple_of(96 - 96 * k, 32)
    return ((0, first), (96, second), (192, 192), (288, 288))


def backward_body(k_ref, nb_hbm, own, near, far, w, grads, dgu, gu_acc, dh_acc, left, dy, nb, ordered, out, in_sem, sem):
    chunks = [slice(j * 512, j * 512 + 512) for j in range(4)]
    nb_loads = [pltpu.make_async_copy(nb_hbm.at[:, c], nb.at[:, c], in_sem.at[3 + j]) for j, c in enumerate(chunks)]
    loads = [
        pltpu.make_async_copy(own, dy.at[0:192, :], in_sem.at[0]),
        pltpu.make_async_copy(near, dy.at[192:288, :], in_sem.at[1]),
        pltpu.make_async_copy(far, dy.at[288:384, :], in_sem.at[2]),
    ]
    for load in nb_loads + loads:
        load.start()
    gu_acc[...] = jnp.zeros_like(gu_acc)
    dh_acc[...] = jnp.zeros_like(dh_acc)
    for load, d in zip(nb_loads, chunks):
        load.wait()
        gu_acc[...] += jnp.dot(nb[:, d], w[d, 0:256], preferred_element_type=F32)
    for load in loads:
        load.wait()

    def contract_dy(j, carry):
        d = pl.ds(pl.multiple_of(j * 512, 512), 512)
        dh_acc[...] += jnp.dot(dy[:, d], w[d, 256:384], preferred_element_type=F32)
        return carry

    lax.fori_loop(0, 4, contract_dy, 0)
    for b in range(3):
        rows = slice(b * 128, b * 128 + 128)
        g, u, dh = gu_acc[rows, 0:128], gu_acc[rows, 128:256], dh_acc[rows, :]
        s = jax.nn.sigmoid(g)
        gs = g * s
        dg = dh * u * s * (1.0 + g * (1.0 - s))
        du = dh * gs
        gu_acc[rows, 0:128] = dg
        gu_acc[rows, 128:256] = du
        left[0:128, rows] = dg.T.astype(BF16)
        left[128:256, rows] = du.T.astype(BF16)
        left[256:384, rows] = (gs * u).T.astype(BF16)

    def expand(j, carry):
        d = pl.ds(pl.multiple_of(j * 256, 256), 256)
        a = jnp.dot(left[0:256, :], nb[:, d], preferred_element_type=F32).astype(BF16)
        b = jnp.dot(left[256:384, :], dy[:, d], preferred_element_type=F32).astype(BF16)
        for h in range(2):
            lanes = slice(h * 128, h * 128 + 128)
            out[2 * j + h, 0:256, :] = a[:, lanes]
            out[2 * j + h, 256:384, :] = b[:, lanes]
        pair = pl.ds(2 * j, 2)
        pltpu.make_async_copy(out.at[pair], grads.at[pair], sem.at[j]).start()
        return carry

    lax.fori_loop(0, 8, expand, 0)
    for at, start in blocks(k_ref[0]):
        ordered[at : at + 96, :] = gu_acc[pl.ds(start, 96), :].astype(BF16)
    pltpu.sync_copy(ordered, dgu)
    for j in range(8):
        pair = pl.ds(2 * j, 2)
        pltpu.make_async_copy(out.at[pair], grads.at[pair], sem.at[j]).wait()


def project(left, w, first, last, keep, send):
    def step(j, carry):
        d = pl.ds(pl.multiple_of(j * 256, 256), 256)
        r = lax.dot_general(left[...], w[d, first:last], NT, preferred_element_type=F32).astype(BF16)
        keep[0:96, d] = r[0:96]
        send[0:96, d] = r[96:192]
        keep[96:192, d] = r[192:288]
        send[96:192, d] = r[288:384]
        return carry

    lax.fori_loop(0, 8, step, 0)


def cotangent_body(dgu_hbm, w, keep, send, dgu):
    pltpu.sync_copy(dgu_hbm, dgu)
    project(dgu, w, 0, 256, keep, send)


def forward_body(k_ref, nf_hbm, w, keep, send, gu_acc, hidden, nf, sem):
    chunks = [slice(j * 512, j * 512 + 512) for j in range(4)]
    loads = [pltpu.make_async_copy(nf_hbm.at[:, c], nf.at[:, c], sem.at[j]) for j, c in enumerate(chunks)]
    for load in loads:
        load.start()
    for j, d in enumerate(chunks):
        loads[j].wait()
        part = jnp.dot(nf[:, d], w[d, 0:256], preferred_element_type=F32)
        gu_acc[...] = part if j == 0 else gu_acc[...] + part
    for at, start in blocks(k_ref[0]):
        rows = pl.ds(start, 96)
        g, u = gu_acc[rows, 0:128], gu_acc[rows, 128:256]
        hidden[at : at + 96, :] = (g * jax.nn.sigmoid(g) * u).astype(BF16)
    project(hidden, w, 256, 384, keep, send)


def total(keep, recv, start):
    rows = pl.ds(pl.multiple_of(start, 16), 16)
    return keep[rows, :].astype(F32) + recv[rows, :].astype(F32)


def ahead_body(k_ref, x, keep, recv, own_out, pair_out):
    k = k_ref[0]

    def step(i, carry):
        r = i * 16
        rows = pl.ds(pl.multiple_of(r, 16), 16)
        mine = pl.ds(pl.multiple_of(k * 96 + r, 16), 16)
        own_out[rows, :] = (x[mine, :].astype(F32) + total(keep, recv, r)).astype(BF16)
        pair_out[rows, :] = total(keep, recv, 96 + r).astype(BF16)
        return carry

    lax.fori_loop(0, 6, step, 0)


def back_body(k_ref, gain_ref, x_own, x_near, dy, keep, recv, own_out, pair_out):
    k = k_ref[0]
    gain = gain_ref[...]

    def through_norm(x, e):
        r = rms(x)
        a = gain * e
        return r * a - x * (r * r * r * jnp.mean(a * x, axis=-1, keepdims=True))

    def step(i, carry):
        r = i * 16
        rows = pl.ds(pl.multiple_of(r, 16), 16)
        mine = pl.ds(pl.multiple_of(k * 96 + r, 16), 16)
        own = through_norm(x_own[mine, :].astype(F32), total(keep, recv, r))
        own_out[rows, :] = (dy[mine, :].astype(F32) + own).astype(BF16)
        pair_out[rows, :] = through_norm(x_near[rows, :].astype(F32), total(keep, recv, 96 + r)).astype(BF16)
        return carry

    lax.fori_loop(0, 6, step, 0)


def rejoin_body(k_ref, *refs):
    pieces, outs, sem = refs[:4], refs[4:6], refs[6]
    stores = []
    for i in range(4):
        at = k_ref[0] if i % 2 == 0 else 1 - k_ref[0]
        rows = pl.ds(pl.multiple_of(at * 96, 32), 96)
        stores.append(pltpu.make_async_copy(pieces[i], outs[i // 2].at[rows, :], sem.at[i]))
    for store in stores:
        store.start()
    for store in stores:
        store.wait()


def add_body(a, b, out):
    out[...] = (a[...].astype(F32) + b[...].astype(F32)).astype(BF16)


def stepped(m, root, grad):
    m2 = BETA_ONE * m + (1.0 - BETA_ONE) * grad
    v2 = BETA_TWO * (root * root) + (1.0 - BETA_TWO) * grad * grad
    return m2 / (1.0 - BETA_ONE**STEP) / (jnp.sqrt(v2 / (1.0 - BETA_TWO**STEP)) + ADAM_EPS)


def sum_body(x_ref, received, own_sum, give, recv, sem):
    xh = x_ref[0]
    order = ((1 - xh, give), (xh, own_sum))
    loads = []
    for n, (d, _) in enumerate(order):
        for i in range(3):
            rows = slice(i * 128, i * 128 + 128)
            loads.append(pltpu.make_async_copy(received.at[:, d, rows, :], recv.at[:, d, rows, :], sem.at[3 * n + i]))
    for load in loads:
        load.start()
    for n, (d, out) in enumerate(order):
        for i in range(3):
            rows = slice(i * 128, i * 128 + 128)
            loads[3 * n + i].wait()
            acc = recv[0, d, rows, :].astype(F32)
            for j in range(1, 8):
                acc = acc + recv[j, d, rows, :].astype(F32)
            out[rows, :] = acc.astype(out.dtype)


def update_body(rows_all, x_ref, own_sum, other_sum, c_in, s_in, c_out, s_out, in_update, out_update):
    xh = x_ref[0]
    for h, grad in ((xh, own_sum), (1 - xh, other_sum)):
        part = pl.ds(pl.multiple_of(h * 128, 128), 128)
        for i in range(2):
            sm = column(s_in[i : i + 1, :], 128)
            sv = column(s_in[2 + i : 3 + i, :], 128)
            m, root = moments(c_in[i, :, part], sm, sv)
            g = grad[i * 128 : i * 128 + 128, :].astype(F32) / rows_all
            in_update[i, :, part] = stepped(m, root, g.T)
        m, root = moments(c_out[part, :], s_out[0:1, :], s_out[1:2, :])
        out_update[part, :] = stepped(m, root, grad[256:384, :].astype(F32) / rows_all)


def tick(fwd, bwd, cot, gain, w_in, w_out, c_in, c_out, s_in, s_out, lags):
    x_f, x_b, dy = fwd[0], bwd[0], cot[0]
    c_in, c_out = c_in[0], c_out[0]
    s_in, s_out = s_in.reshape(4, 128), s_out.reshape(2, 128)
    k = lax.axis_index("hid")
    k_arr = k.astype(jnp.int32).reshape(1)
    x_arr = lax.axis_index("xh").astype(jnp.int32).reshape(1)
    swap = [(0, 1), (1, 0)]
    sections = lax.axis_size("section")

    def across(x):
        return lax.ppermute(x, "xh", swap)

    def on_chip(x):
        return lax.ppermute(x, "hid", swap)

    def exchange(x):
        return lax.all_to_all(x, "y", 0, 0, tiled=True)

    def after(x, other):
        return lax.optimization_barrier((x, other))[0]

    tokens, part, piece = struct((384, 2048)), struct((192, 2048)), struct((96, 2048))
    quarter = struct((128, 384))
    give, mine = call(
        predict_body, [quarter, struct((8, 2, 128, 384))],
        [lags, x_arr, w_in[0], c_in, s_in, w_out[0], c_out, s_out],
        scratch=[
            pltpu.VMEM((2, 128, 256), F32), pltpu.VMEM((2, 128, 256), jnp.int32), pltpu.VMEM((4, 128), F32),
            pltpu.VMEM((256, 128), F32), pltpu.VMEM((256, 128), jnp.int32), pltpu.VMEM((2, 128), F32),
            pltpu.VMEM((2, 128, 384), BF16), pltpu.SemaphoreType.DMA((6,)), pltpu.SemaphoreType.DMA((8,)),
        ],
        n_smem=2, hbm_in=range(2, 8), hbm_out=(1,),
    )
    other = across(give)
    half_b, half_y, half_f = call(
        halves_body, [piece, piece, piece], [k_arr, after(x_b, give), dy, x_f],
        scratch=[pltpu.SemaphoreType.DMA((3,))], n_smem=1, hbm_in=(1, 2, 3),
    )
    (send,) = call(
        fill_body, [struct((8, 2, 128, 384))], [x_arr, other, mine],
        scratch=[pltpu.SemaphoreType.DMA((8,))], n_smem=1, hbm_in=(2,), hbm_out=(0,), alias={2: 0},
    )
    weights = exchange(send).reshape(2048, 384)

    near_b = across(half_b)
    near_y = across(half_y)
    far_b = on_chip(near_b)
    far_y = on_chip(near_y)
    near_f = across(half_f)
    far_f = on_chip(near_f)
    (nb,) = call(normed_hbm_body, [tokens], [gain, x_b, near_b, far_b], hbm_out=(0,), scratch=[pltpu.VMEM((384, 2048), BF16)])
    (nf,) = call(
        normed_hbm_body, [tokens], [gain, x_f, near_f, far_f],
        hbm_out=(0,), scratch=[pltpu.VMEM((384, 2048), BF16)],
    )

    grads, dgu = call(
        backward_body, [struct((16, 384, 128)), struct((384, 256))], [k_arr, nb, dy, near_y, far_y, weights],
        scratch=[
            pltpu.VMEM((384, 256), F32), pltpu.VMEM((384, 128), F32),
            pltpu.VMEM((384, 384), BF16), pltpu.VMEM((384, 2048), BF16),
            pltpu.VMEM((384, 2048), BF16), pltpu.VMEM((384, 256), BF16),
            pltpu.VMEM((16, 384, 128), BF16), pltpu.SemaphoreType.DMA((7,)), pltpu.SemaphoreType.DMA((8,)),
        ],
        flops=4 * 384 * 384 * 2048, n_smem=1, hbm_in=(1, 2, 3, 4), hbm_out=(0, 1),
    )
    received = exchange(grads.reshape(8, 2, 384, 128))
    own_sum, give = call(
        sum_body, [struct((384, 128), F32), struct((384, 128))], [x_arr, received],
        scratch=[pltpu.VMEM((8, 2, 384, 128), BF16), pltpu.SemaphoreType.DMA((6,))],
        n_smem=1, hbm_in=(1,),
    )
    other_sum = across(give)

    q_keep, q_send = call(
        forward_body, [part, part], [k_arr, after(nf, dgu), weights],
        scratch=[
            pltpu.VMEM((384, 256), F32), pltpu.VMEM((384, 128), BF16),
            pltpu.VMEM((384, 2048), BF16), pltpu.SemaphoreType.DMA((4,)),
        ],
        flops=2 * 384 * 384 * 2048, n_smem=1, hbm_in=(1,),
    )
    q_recv = on_chip(q_send)
    e_keep, e_send = call(
        cotangent_body, [part, part], [after(dgu, q_send), weights],
        scratch=[pltpu.VMEM((384, 256), BF16)], flops=2 * 384 * 256 * 2048, hbm_in=(0,),
    )
    e_recv = on_chip(e_send)
    ahead = call(ahead_body, [piece, piece], [k_arr, x_f, q_keep, q_recv], n_smem=1)
    back = call(back_body, [piece, piece], [k_arr, gain, x_b, near_b, dy, e_keep, e_recv], n_smem=1)

    def relay(pieces, distance):
        moves = [(s, s + distance) for s in range(sections) if 0 <= s + distance < sections]
        same = [(2 * s + h, 2 * t + h) for s, t in moves for h in range(2)]
        cross = [(2 * s + h, 2 * t + 1 - h) for s, t in moves for h in range(2)]
        axes = ("section", "xh")
        own, pair = lax.ppermute(pieces[0], axes, same), lax.ppermute(pieces[1], axes, cross)
        (mine,) = call(add_body, [piece], [own, pair])
        return mine, on_chip(mine)

    next_halves = relay(ahead, 1)
    back_halves = relay(back, -1)
    next_rows, back_rows = call(
        rejoin_body, [part, part], [k_arr, *next_halves, *back_halves],
        scratch=[pltpu.SemaphoreType.DMA((4,))], n_smem=1, hbm_out=(0, 1),
    )

    rows_all = dy.shape[0] * lax.axis_size(DP)
    in_update, out_update = call(
        functools.partial(update_body, float(rows_all)),
        [struct((2, 128, 256), F32), struct((256, 128), F32)],
        [x_arr, own_sum, other_sum, c_in, s_in, c_out, s_out], n_smem=1,
    )
    return next_rows[None], back_rows[None], in_update[None], out_update[None]


def solution(mesh):
    split = Mesh(
        mesh.devices.reshape(mesh.shape["section"], 8, 2, mesh.shape["hid"]),
        ("section", "y", "xh", "hid"),
    )
    return jax.shard_map(
        tick,
        mesh=split,
        in_specs=(
            P("section", DP, None),
            P("section", DP, None),
            P("section", DP, None),
            P("section", None),
            P("section", None, DP, "hid"),
            P("section", "hid", DP),
            P("section", None, DP, "hid"),
            P("section", "hid", DP),
            P("section", None, None, DP, "hid"),
            P("section", None, "hid", DP),
            P("section"),
        ),
        out_specs=(
            P("section", DP, None),
            P("section", DP, None),
            P("section", None, DP, "hid"),
            P("section", "hid", DP),
        ),
        check_vma=False,
    )
```

time: 187 us -> 156 us (0.83)
  the two profiles are of different devices: /device:TPU:3 before, /device:TPU:10 now
where the time goes in v2:
time: 156 us; the launch traced here: 155 us
  starting transfers between devices  66.9 us (43%)
  waiting for transfers between devices  59.3 us (38%)
  Pallas kernels  27.5 us (18%)
  between operations  1.65 us (1%)
    ppermute x5, waiting for transfers between devices, across(): return lax.ppermute(x, 'xh', swap)  30.3 us
    pallas_call x15, Pallas kernels, call(): pl.pallas_call(body, out_shape=tuple(((pltpu.HBM if i in hbm_out else jax...  27.5 us
    ppermute x5, starting transfers between devices, across(): return lax.ppermute(x, 'xh', swap)  18.5 us
    ppermute x2, waiting for transfers between devices, relay(): lax.ppermute(pieces[1], axes, cross)  15.4 us
    ppermute x2, starting transfers between devices, relay(): lax.ppermute(pieces[0], axes, same)  15.2 us
    ppermute x7, starting transfers between devices, on_chip(): return lax.ppermute(x, 'hid', swap)  14 us
    all_to_all x2, starting transfers between devices, exchange(): return lax.all_to_all(x, 'y', 0, 0, tiled=True)  13.3 us
    all_to_all x2, waiting for transfers between devices, exchange(): return lax.all_to_all(x, 'y', 0, 0, tiled=True)  11 us
  transfers between devices with their start and end apart: 18, of which 10 were waited for; matrix products, arithmetic and copies ran while one was open for 0% of the time, Pallas kernels for 11%

profile of v2, /device:TPU:10, one launch (start us, length us, event | category | flops | bytes accessed | tf_op | source)
XLA Modules:
  0.0 155.5 jit_solution(101439515440474735)
XLA Ops:
  1.3 2.4 %shard_map.138 = (bf16[128,384]{1,0:T(8,128)(2,1)S(1)}, bf16[8,2,128,384]{3,2,1,0:T(8,128)(2,1)}) custom-call(s32[1]{0:T(128)S(6)} %copy.17.lag_ref, s32[1]{0:T(128)} %bitcast.3.x_ref, f32[2,128,256]{2,1,0:T(8,128)} %bitcast.38, s32[2,128,256]{2,1,0:T(8,128)} %bitcast.29, f32[4,128]{1,0:T(4,128)} %bitcast.33, f32[256,128]{1,0:T(8,128)} %bitcast.39, ...), custom_call_target="tpu_custom_call" | custom-call | bytes 2460680 | tf_op jit(solution)/shard_map/pallas_call | solution.py:31
  3.7 4.1 %collective-permute-start.6 = (bf16[128,384]{1,0:T(8,128)(2,1)S(1)}, bf16[128,384]{1,0:T(8,128)(2,1)S(1)}, u32[]{:S(2)}, u32[]{:S(2)}) collective-permute-start(bf16[128,384]{1,0:T(8,128)(2,1)S(1)} %get-tuple-element.28), channel_id=1, source_target_pairs={{0,2},{2,0},{1,3},{3,1},{4,6},{6,4},{5,7},{7,5},{8,10},{10,8},{9,1... | collective-permute-start | bytes 294920 | tf_op jit(solution)/shard_map/ppermute | solution.py:337
  7.8 3.9 %collective-permute-done.6.other = bf16[128,384]{1,0:T(8,128)(2,1)S(1)} collective-permute-done((bf16[128,384]{1,0:T(8,128)(2,1)S(1)}, bf16[128,384]{1,0:T(8,128)(2,1)S(1)}, u32[]{:S(2)}, u32[]{:S(2)}) %collective-permute-start.6) | collective-permute-done | bytes 98336 | tf_op jit(solution)/shard_map/ppermute | solution.py:337
  12.7 7.6 %all-to-all-start = ((bf16[8,2,128,384]{3,2,1,0:T(8,128)(2,1)}), bf16[8,2,128,384]{3,2,1,0:T(8,128)(2,1)S(1)}, u32[]{:S(2)}, u32[]{:S(2)}) async-start(bf16[8,2,128,384]{3,2,1,0:T(8,128)(2,1)} %shard_map.142), calls=%async_computation | async-start | bytes 3145728 | tf_op jit(solution)/shard_map/all_to_all | solution.py:343
  21.6 4.0 %collective-permute-start.2 = (bf16[96,2048]{1,0:T(8,128)(2,1)S(1)}, bf16[96,2048]{1,0:T(8,128)(2,1)S(1)}, u32[]{:S(2)}, u32[]{:S(2)}) collective-permute-start(bf16[96,2048]{1,0:T(8,128)(2,1)S(1)} %get-tuple-element.31), channel_id=1, source_target_pairs={{0,2},{2,0},{1,3},{3,1},{4,6},{6,4},{5,7},{7,5},{8,10},{10,8},{9,1... | collective-permute-start | bytes 1179656 | tf_op jit(solution)/shard_map/ppermute | solution.py:337
  25.7 3.3 %collective-permute-start.4 = (bf16[96,2048]{1,0:T(8,128)(2,1)S(1)}, bf16[96,2048]{1,0:T(8,128)(2,1)S(1)}, u32[]{:S(2)}, u32[]{:S(2)}) collective-permute-start(bf16[96,2048]{1,0:T(8,128)(2,1)S(1)} %get-tuple-element.32), channel_id=1, source_target_pairs={{0,2},{2,0},{1,3},{3,1},{4,6},{6,4},{5,7},{7,5},{8,10},{10,8},{9,1... | collective-permute-start | bytes 1179656 | tf_op jit(solution)/shard_map/ppermute | solution.py:337
  29.0 8.0 %collective-permute-done.2.near.x_near = bf16[96,2048]{1,0:T(8,128)(2,1)S(1)} collective-permute-done((bf16[96,2048]{1,0:T(8,128)(2,1)S(1)}, bf16[96,2048]{1,0:T(8,128)(2,1)S(1)}, u32[]{:S(2)}, u32[]{:S(2)}) %collective-permute-start.2) | collective-permute-done | bytes 393248 | tf_op jit(solution)/shard_map/ppermute | solution.py:337
  37.0 1.9 %collective-permute-start.3 = (bf16[96,2048]{1,0:T(8,128)(2,1)S(1)}, bf16[96,2048]{1,0:T(8,128)(2,1)S(1)}, u32[]{:S(2)}, u32[]{:S(2)}) collective-permute-start(bf16[96,2048]{1,0:T(8,128)(2,1)S(1)} %collective-permute-done.2.near.x_near), channel_id=1, source_target_pairs={{0,1},{1,0},{2,3},{3,2},{4,5},{5,4},{6,7},{7,6},{8,9},{9,8},{10,11... | collective-permute-start | bytes 1179656 | tf_op jit(solution)/shard_map/ppermute | solution.py:340
  38.9 3.7 %collective-permute-done.4.near = bf16[96,2048]{1,0:T(8,128)(2,1)S(1)} collective-permute-done((bf16[96,2048]{1,0:T(8,128)(2,1)S(1)}, bf16[96,2048]{1,0:T(8,128)(2,1)S(1)}, u32[]{:S(2)}, u32[]{:S(2)}) %collective-permute-start.4) | collective-permute-done | bytes 393248 | tf_op jit(solution)/shard_map/ppermute | solution.py:337
  42.6 1.9 %collective-permute-start.5 = (bf16[96,2048]{1,0:T(8,128)(2,1)S(1)}, bf16[96,2048]{1,0:T(8,128)(2,1)S(1)}, u32[]{:S(2)}, u32[]{:S(2)}) collective-permute-start(bf16[96,2048]{1,0:T(8,128)(2,1)S(1)} %collective-permute-done.4.near), channel_id=1, source_target_pairs={{0,1},{1,0},{2,3},{3,2},{4,5},{5,4},{6,7},{7,6},{8,9},{9,8},{10,11... | collective-permute-start | bytes 1179656 | tf_op jit(solution)/shard_map/ppermute | solution.py:340
  44.5 2.1 %shard_map.141.nb_hbm = bf16[384,2048]{1,0:T(8,128)(2,1)} custom-call(f32[1,2048]{1,0:T(1,128)S(1)} %copy-done.5, bf16[192,2048]{1,0:T(8,128)(2,1)S(1)} %bitcast.27, bf16[96,2048]{1,0:T(8,128)(2,1)S(1)} %collective-permute-done.2.near.x_near, bf16[96,2048]{1,0:T(8,128)(2,1)S(1)} %collective-permute-done.3.far), custom_call_target="tpu_custom_call" | custom-call | bytes 3153920 | tf_op jit(solution)/shard_map/pallas_call | solution.py:31
  46.7 10.9 %all-to-all-done = bf16[8,2,128,384]{3,2,1,0:T(8,128)(2,1)S(1)} async-done(((bf16[8,2,128,384]{3,2,1,0:T(8,128)(2,1)}), bf16[8,2,128,384]{3,2,1,0:T(8,128)(2,1)S(1)}, u32[]{:S(2)}, u32[]{:S(2)}) %all-to-all-start) | async-done | bytes 1572896 | tf_op jit(solution)/shard_map/all_to_all | solution.py:343
  57.6 6.3 %shard_map.143 = (bf16[16,384,128]{2,1,0:T(8,128)(2,1)}, bf16[384,256]{1,0:T(8,128)(2,1)}) custom-call(s32[1]{0:T(128)} %bitcast.k_ref, bf16[384,2048]{1,0:T(8,128)(2,1)} %shard_map.141.nb_hbm, bf16[192,2048]{1,0:T(8,128)(2,1)} %bitcast.24, bf16[96,2048]{1,0:T(8,128)(2,1)} %copy-done.9, bf16[96,2048]{1,0:T(8,128)(2,1)} %copy-done.10, ...), custom_call_target="tpu_custom_call" | custom-call | flops 1207959552 | bytes 6488068 | tf_op jit(solution)/shard_map/pallas_call | solution.py:31
  64.0 5.8 %all-to-all-start.1 = ((bf16[8,2,384,128]{3,2,1,0:T(8,128)(2,1)}), bf16[8,2,384,128]{3,2,1,0:T(8,128)(2,1)}, u32[]{:S(2)}, u32[]{:S(2)}) async-start(bf16[8,2,384,128]{3,2,1,0:T(8,128)(2,1)} %bitcast.37), calls=%async_computation.1 | async-start | bytes 3145728 | tf_op jit(solution)/shard_map/all_to_all | solution.py:343
  69.8 4.0 %collective-permute-start = (bf16[96,2048]{1,0:T(8,128)(2,1)}, bf16[96,2048]{1,0:T(8,128)(2,1)S(1)}, u32[]{:S(2)}, u32[]{:S(2)}) collective-permute-start(bf16[96,2048]{1,0:T(8,128)(2,1)} %copy-done.8), channel_id=1, source_target_pairs={{0,2},{2,0},{1,3},{3,1},{4,6},{6,4},{5,7},{7,5},{8,10},{10,8},{9,1... | collective-permute-start | bytes 1179656 | tf_op jit(solution)/shard_map/ppermute | solution.py:337
  73.8 10.3 %collective-permute-done.near = bf16[96,2048]{1,0:T(8,128)(2,1)S(1)} collective-permute-done((bf16[96,2048]{1,0:T(8,128)(2,1)}, bf16[96,2048]{1,0:T(8,128)(2,1)S(1)}, u32[]{:S(2)}, u32[]{:S(2)}) %collective-permute-start) | collective-permute-done | bytes 393248 | tf_op jit(solution)/shard_map/ppermute | solution.py:337
  84.1 1.9 %collective-permute-start.1 = (bf16[96,2048]{1,0:T(8,128)(2,1)S(1)}, bf16[96,2048]{1,0:T(8,128)(2,1)S(1)}, u32[]{:S(2)}, u32[]{:S(2)}) collective-permute-start(bf16[96,2048]{1,0:T(8,128)(2,1)S(1)} %collective-permute-done.near), channel_id=1, source_target_pairs={{0,1},{1,0},{2,3},{3,2},{4,5},{5,4},{6,7},{7,6},{8,9},{9,8},{10,11... | collective-permute-start | bytes 1179656 | tf_op jit(solution)/shard_map/ppermute | solution.py:340
  87.7 2.1 %shard_map.140.nf_hbm = bf16[384,2048]{1,0:T(8,128)(2,1)} custom-call(f32[1,2048]{1,0:T(1,128)S(1)} %copy-done.5, bf16[192,2048]{1,0:T(8,128)(2,1)S(1)} %bitcast.21, bf16[96,2048]{1,0:T(8,128)(2,1)S(1)} %collective-permute-done.near, bf16[96,2048]{1,0:T(8,128)(2,1)S(1)} %collective-permute-done.1.far), custom_call_target="tpu_custom_call" | custom-call | bytes 3153920 | tf_op jit(solution)/shard_map/pallas_call | solution.py:31
  89.8 4.0 %shard_map.144 = (bf16[192,2048]{1,0:T(8,128)(2,1)S(1)}, bf16[192,2048]{1,0:T(8,128)(2,1)S(1)}) custom-call(s32[1]{0:T(128)} %bitcast.k_ref, bf16[384,2048]{1,0:T(8,128)(2,1)} %shard_map.140.nf_hbm, bf16[2048,384]{1,0:T(8,128)(2,1)S(1)} %bitcast.18), custom_call_target="tpu_custom_call" | custom-call | flops 603979776 | bytes 4718596 | tf_op jit(solution)/shard_map/pallas_call | solution.py:31
  93.8 3.0 %shard_map.147 = (bf16[192,2048]{1,0:T(8,128)(2,1)S(1)}, bf16[192,2048]{1,0:T(8,128)(2,1)S(1)}) custom-call(bf16[384,256]{1,0:T(8,128)(2,1)} %get-tuple-element.40.dgu_hbm, bf16[2048,384]{1,0:T(8,128)(2,1)S(1)} %bitcast.19), custom_call_target="tpu_custom_call" | custom-call | flops 402653184 | bytes 3342336 | tf_op jit(solution)/shard_map/pallas_call | solution.py:31
  96.8 2.0 %collective-permute-start.11 = (bf16[192,2048]{1,0:T(8,128)(2,1)S(1)}, bf16[192,2048]{1,0:T(8,128)(2,1)S(1)}, u32[]{:S(2)}, u32[]{:S(2)}) collective-permute-start(bf16[192,2048]{1,0:T(8,128)(2,1)S(1)} %get-tuple-element.42), channel_id=1, source_target_pairs={{0,1},{1,0},{2,3},{3,2},{4,5},{5,4},{6,7},{7,6},{8,9},{9,8},{10,11... | collective-permute-start | bytes 2359304 | tf_op jit(solution)/shard_map/ppermute | solution.py:340
  98.8 2.3 %collective-permute-start.7 = (bf16[192,2048]{1,0:T(8,128)(2,1)S(1)}, bf16[192,2048]{1,0:T(8,128)(2,1)S(1)}, u32[]{:S(2)}, u32[]{:S(2)}) collective-permute-start(bf16[192,2048]{1,0:T(8,128)(2,1)S(1)} %get-tuple-element.37), channel_id=1, source_target_pairs={{0,1},{1,0},{2,3},{3,2},{4,5},{5,4},{6,7},{7,6},{8,9},{9,8},{10,11... | collective-permute-start | bytes 2359304 | tf_op jit(solution)/shard_map/ppermute | solution.py:340
  102.2 10.9 %collective-permute-start.12 = (bf16[96,2048]{1,0:T(8,128)(2,1)S(1)}, bf16[96,2048]{1,0:T(8,128)(2,1)S(1)}, u32[]{:S(2)}, u32[]{:S(2)}) collective-permute-start(bf16[96,2048]{1,0:T(8,128)(2,1)S(1)} %get-tuple-element.43), channel_id=1, source_target_pairs={{32,0},{34,2},{64,32},{66,34},{96,64},{98,66},{128,96},{130,98},{1... | collective-permute-start | bytes 1179656 | tf_op jit(solution)/shard_map/ppermute | solution.py:423
  113.1 3.4 %collective-permute-start.13 = (bf16[96,2048]{1,0:T(8,128)(2,1)S(1)}, bf16[96,2048]{1,0:T(8,128)(2,1)S(1)}, u32[]{:S(2)}, u32[]{:S(2)}) collective-permute-start(bf16[96,2048]{1,0:T(8,128)(2,1)S(1)} %get-tuple-element.44), channel_id=1, source_target_pairs={{32,2},{34,0},{64,34},{66,32},{96,66},{98,64},{128,98},{130,96},{1... | collective-permute-start | bytes 1179656 | tf_op jit(solution)/shard_map/ppermute | solution.py:423
  116.8 4.3 %collective-permute-start.8 = (bf16[96,2048]{1,0:T(8,128)(2,1)S(1)}, bf16[96,2048]{1,0:T(8,128)(2,1)S(1)}, u32[]{:S(2)}, u32[]{:S(2)}) collective-permute-start(bf16[96,2048]{1,0:T(8,128)(2,1)S(1)} %get-tuple-element.38), channel_id=1, source_target_pairs={{0,32},{2,34},{32,64},{34,66},{64,96},{66,98},{96,128},{98,130},{1... | collective-permute-start | bytes 1179656 | tf_op jit(solution)/shard_map/ppermute | solution.py:423
  121.1 2.5 %collective-permute-start.9 = (bf16[96,2048]{1,0:T(8,128)(2,1)S(1)}, bf16[96,2048]{1,0:T(8,128)(2,1)S(1)}, u32[]{:S(2)}, u32[]{:S(2)}) collective-permute-start(bf16[96,2048]{1,0:T(8,128)(2,1)S(1)} %get-tuple-element.39), channel_id=1, source_target_pairs={{0,34},{2,32},{32,66},{34,64},{64,98},{66,96},{96,130},{98,128},{1... | collective-permute-start | bytes 1179656 | tf_op jit(solution)/shard_map/ppermute | solution.py:423
  123.6 7.4 %collective-permute-done.13.b = bf16[96,2048]{1,0:T(8,128)(2,1)S(1)} collective-permute-done((bf16[96,2048]{1,0:T(8,128)(2,1)S(1)}, bf16[96,2048]{1,0:T(8,128)(2,1)S(1)}, u32[]{:S(2)}, u32[]{:S(2)}) %collective-permute-start.13) | collective-permute-done | bytes 393248 | tf_op jit(solution)/shard_map/ppermute | solution.py:423
  131.1 1.9 %collective-permute-start.14 = (bf16[96,2048]{1,0:T(8,128)(2,1)S(1)}, bf16[96,2048]{1,0:T(8,128)(2,1)S(1)}, u32[]{:S(2)}, u32[]{:S(2)}) collective-permute-start(bf16[96,2048]{1,0:T(8,128)(2,1)S(1)} %shard_map.149.refs_2_), channel_id=1, source_target_pairs={{0,1},{1,0},{2,3},{3,2},{4,5},{5,4},{6,7},{7,6},{8,9},{9,8},{10,11... | collective-permute-start | bytes 1179656 | tf_op jit(solution)/shard_map/ppermute | solution.py:340
  134.0 8.0 %collective-permute-done.9.b = bf16[96,2048]{1,0:T(8,128)(2,1)S(1)} collective-permute-done((bf16[96,2048]{1,0:T(8,128)(2,1)S(1)}, bf16[96,2048]{1,0:T(8,128)(2,1)S(1)}, u32[]{:S(2)}, u32[]{:S(2)}) %collective-permute-start.9) | collective-permute-done | bytes 393248 | tf_op jit(solution)/shard_map/ppermute | solution.py:423
  142.2 2.1 %collective-permute-start.10 = (bf16[96,2048]{1,0:T(8,128)(2,1)S(1)}, bf16[96,2048]{1,0:T(8,128)(2,1)S(1)}, u32[]{:S(2)}, u32[]{:S(2)}) collective-permute-start(bf16[96,2048]{1,0:T(8,128)(2,1)S(1)} %shard_map.146.refs_0_), channel_id=1, source_target_pairs={{0,1},{1,0},{2,3},{3,2},{4,5},{5,4},{6,7},{7,6},{8,9},{9,8},{10,11... | collective-permute-start | bytes 1179656 | tf_op jit(solution)/shard_map/ppermute | solution.py:340
  145.7 3.0 %collective-permute-start.15 = (bf16[384,128]{1,0:T(8,128)(2,1)S(1)}, bf16[384,128]{1,0:T(8,128)(2,1)S(1)}, u32[]{:S(2)}, u32[]{:S(2)}) collective-permute-start(bf16[384,128]{1,0:T(8,128)(2,1)S(1)} %get-tuple-element.49), channel_id=1, source_target_pairs={{0,2},{2,0},{1,3},{3,1},{4,6},{6,4},{5,7},{7,5},{8,10},{10,8},{9,1... | collective-permute-start | bytes 294920 | tf_op jit(solution)/shard_map/ppermute | solution.py:337
  149.9 4.4 %collective-permute-done.15.other_sum = bf16[384,128]{1,0:T(8,128)(2,1)S(1)} collective-permute-done((bf16[384,128]{1,0:T(8,128)(2,1)S(1)}, bf16[384,128]{1,0:T(8,128)(2,1)S(1)}, u32[]{:S(2)}, u32[]{:S(2)}) %collective-permute-start.15) | collective-permute-done | bytes 98336 | tf_op jit(solution)/shard_map/ppermute | solution.py:337
  (41 shorter events, 10.3 us)
Async XLA Ops:
  3.7 8.0 %collective-permute-start.6 = (bf16[128,384]{1,0:T(8,128)(2,1)S(1)}, bf16[128,384]{1,0:T(8,128)(2,1)S(1)}, u32[]{:S(2)}, u32[]{:S(2)}) collective-permute-start(bf16[128,384]{1,0:T(8,128)(2,1)S(1)} %get-tuple-element.28), channel_id=1, source_target_pairs={{0,2},{2,0},{1,3},{3,1},{4,6},{6,4},{5,7},{7,5},{8,10},{10,8},{9,1... | collective-permute-start | bytes 294920 | tf_op jit(solution)/shard_map/ppermute | solution.py:337
  12.7 44.9 %all-to-all-start = ((bf16[8,2,128,384]{3,2,1,0:T(8,128)(2,1)}), bf16[8,2,128,384]{3,2,1,0:T(8,128)(2,1)S(1)}, u32[]{:S(2)}, u32[]{:S(2)}) async-start(bf16[8,2,128,384]{3,2,1,0:T(8,128)(2,1)} %shard_map.142), calls=%async_computation | async-start | bytes 3145728 | tf_op jit(solution)/shard_map/all_to_all | solution.py:343
  20.3 24.3 %copy-start.2 = (bf16[1,192,2048]{2,1,0:T(8,128)(2,1)S(1)}, bf16[1,192,2048]{2,1,0:T(8,128)(2,1)}, u32[]{:S(2)}) copy-start(bf16[1,192,2048]{2,1,0:T(8,128)(2,1)} %param.12) | copy-start | bytes 2359300
  20.3 24.3 %copy-start.5 = (f32[1,2048]{1,0:T(1,128)S(1)}, f32[1,2048]{1,0:T(1,128)}, u32[]{:S(2)}) copy-start(f32[1,2048]{1,0:T(1,128)} %gain_ref.5) | copy-start | bytes 24580
  21.6 25.1 %copy-start.8 = (bf16[96,2048]{1,0:T(8,128)(2,1)}, bf16[96,2048]{1,0:T(8,128)(2,1)S(1)}, u32[]{:S(2)}) copy-start(bf16[96,2048]{1,0:T(8,128)(2,1)S(1)} %get-tuple-element.30) | copy-start | bytes 1179652
  21.6 15.4 %collective-permute-start.2 = (bf16[96,2048]{1,0:T(8,128)(2,1)S(1)}, bf16[96,2048]{1,0:T(8,128)(2,1)S(1)}, u32[]{:S(2)}, u32[]{:S(2)}) collective-permute-start(bf16[96,2048]{1,0:T(8,128)(2,1)S(1)} %get-tuple-element.31), channel_id=1, source_target_pairs={{0,2},{2,0},{1,3},{3,1},{4,6},{6,4},{5,7},{7,5},{8,10},{10,8},{9,1... | collective-permute-start | bytes 1179656 | tf_op jit(solution)/shard_map/ppermute | solution.py:337
  25.7 16.9 %collective-permute-start.4 = (bf16[96,2048]{1,0:T(8,128)(2,1)S(1)}, bf16[96,2048]{1,0:T(8,128)(2,1)S(1)}, u32[]{:S(2)}, u32[]{:S(2)}) collective-permute-start(bf16[96,2048]{1,0:T(8,128)(2,1)S(1)} %get-tuple-element.32), channel_id=1, source_target_pairs={{0,2},{2,0},{1,3},{3,1},{4,6},{6,4},{5,7},{7,5},{8,10},{10,8},{9,1... | collective-permute-start | bytes 1179656 | tf_op jit(solution)/shard_map/ppermute | solution.py:337
  37.0 7.5 %collective-permute-start.3 = (bf16[96,2048]{1,0:T(8,128)(2,1)S(1)}, bf16[96,2048]{1,0:T(8,128)(2,1)S(1)}, u32[]{:S(2)}, u32[]{:S(2)}) collective-permute-start(bf16[96,2048]{1,0:T(8,128)(2,1)S(1)} %collective-permute-done.2.near.x_near), channel_id=1, source_target_pairs={{0,1},{1,0},{2,3},{3,2},{4,5},{5,4},{6,7},{7,6},{8,9},{9,8},{10,11... | collective-permute-start | bytes 1179656 | tf_op jit(solution)/shard_map/ppermute | solution.py:340
  42.6 4.1 %copy-start.9 = (bf16[96,2048]{1,0:T(8,128)(2,1)}, bf16[96,2048]{1,0:T(8,128)(2,1)S(1)}, u32[]{:S(2)}) copy-start(bf16[96,2048]{1,0:T(8,128)(2,1)S(1)} %collective-permute-done.4.near) | copy-start | bytes 1179652
  42.6 4.1 %collective-permute-start.5 = (bf16[96,2048]{1,0:T(8,128)(2,1)S(1)}, bf16[96,2048]{1,0:T(8,128)(2,1)S(1)}, u32[]{:S(2)}, u32[]{:S(2)}) collective-permute-start(bf16[96,2048]{1,0:T(8,128)(2,1)S(1)} %collective-permute-done.4.near), channel_id=1, source_target_pairs={{0,1},{1,0},{2,3},{3,2},{4,5},{5,4},{6,7},{7,6},{8,9},{9,8},{10,11... | collective-permute-start | bytes 1179656 | tf_op jit(solution)/shard_map/ppermute | solution.py:340
  46.7 11.0 %copy-start.10 = (bf16[96,2048]{1,0:T(8,128)(2,1)}, bf16[96,2048]{1,0:T(8,128)(2,1)S(1)}, u32[]{:S(2)}) copy-start(bf16[96,2048]{1,0:T(8,128)(2,1)S(1)} %collective-permute-done.5.far) | copy-start | bytes 1179652
  64.0 23.7 %copy-start = (bf16[1,192,2048]{2,1,0:T(8,128)(2,1)S(1)}, bf16[1,192,2048]{2,1,0:T(8,128)(2,1)}, u32[]{:S(2)}) copy-start(bf16[1,192,2048]{2,1,0:T(8,128)(2,1)} %param.11) | copy-start | bytes 2359300
  64.0 80.2 %all-to-all-start.1 = ((bf16[8,2,384,128]{3,2,1,0:T(8,128)(2,1)}), bf16[8,2,384,128]{3,2,1,0:T(8,128)(2,1)}, u32[]{:S(2)}, u32[]{:S(2)}) async-start(bf16[8,2,384,128]{3,2,1,0:T(8,128)(2,1)} %bitcast.37), calls=%async_computation.1 | async-start | bytes 3145728 | tf_op jit(solution)/shard_map/all_to_all | solution.py:343
  69.8 14.4 %collective-permute-start = (bf16[96,2048]{1,0:T(8,128)(2,1)}, bf16[96,2048]{1,0:T(8,128)(2,1)S(1)}, u32[]{:S(2)}, u32[]{:S(2)}) collective-permute-start(bf16[96,2048]{1,0:T(8,128)(2,1)} %copy-done.8), channel_id=1, source_target_pairs={{0,2},{2,0},{1,3},{3,1},{4,6},{6,4},{5,7},{7,5},{8,10},{10,8},{9,1... | collective-permute-start | bytes 1179656 | tf_op jit(solution)/shard_map/ppermute | solution.py:337
  84.1 3.6 %collective-permute-start.1 = (bf16[96,2048]{1,0:T(8,128)(2,1)S(1)}, bf16[96,2048]{1,0:T(8,128)(2,1)S(1)}, u32[]{:S(2)}, u32[]{:S(2)}) collective-permute-start(bf16[96,2048]{1,0:T(8,128)(2,1)S(1)} %collective-permute-done.near), channel_id=1, source_target_pairs={{0,1},{1,0},{2,3},{3,2},{4,5},{5,4},{6,7},{7,6},{8,9},{9,8},{10,11... | collective-permute-start | bytes 1179656 | tf_op jit(solution)/shard_map/ppermute | solution.py:340
  93.8 7.4 %copy-start.1 = (bf16[1,192,2048]{2,1,0:T(8,128)(2,1)S(1)}, bf16[1,192,2048]{2,1,0:T(8,128)(2,1)}, u32[]{:S(2)}) copy-start(bf16[1,192,2048]{2,1,0:T(8,128)(2,1)} %param.13) | copy-start | bytes 2359300
  96.8 4.3 %collective-permute-start.11 = (bf16[192,2048]{1,0:T(8,128)(2,1)S(1)}, bf16[192,2048]{1,0:T(8,128)(2,1)S(1)}, u32[]{:S(2)}, u32[]{:S(2)}) collective-permute-start(bf16[192,2048]{1,0:T(8,128)(2,1)S(1)} %get-tuple-element.42), channel_id=1, source_target_pairs={{0,1},{1,0},{2,3},{3,2},{4,5},{5,4},{6,7},{7,6},{8,9},{9,8},{10,11... | collective-permute-start | bytes 2359304 | tf_op jit(solution)/shard_map/ppermute | solution.py:340
  98.8 17.7 %collective-permute-start.7 = (bf16[192,2048]{1,0:T(8,128)(2,1)S(1)}, bf16[192,2048]{1,0:T(8,128)(2,1)S(1)}, u32[]{:S(2)}, u32[]{:S(2)}) collective-permute-start(bf16[192,2048]{1,0:T(8,128)(2,1)S(1)} %get-tuple-element.37), channel_id=1, source_target_pairs={{0,1},{1,0},{2,3},{3,2},{4,5},{5,4},{6,7},{7,6},{8,9},{9,8},{10,11... | collective-permute-start | bytes 2359304 | tf_op jit(solution)/shard_map/ppermute | solution.py:340
  102.2 21.4 %collective-permute-start.12 = (bf16[96,2048]{1,0:T(8,128)(2,1)S(1)}, bf16[96,2048]{1,0:T(8,128)(2,1)S(1)}, u32[]{:S(2)}, u32[]{:S(2)}) collective-permute-start(bf16[96,2048]{1,0:T(8,128)(2,1)S(1)} %get-tuple-element.43), channel_id=1, source_target_pairs={{32,0},{34,2},{64,32},{66,34},{96,64},{98,66},{128,96},{130,98},{1... | collective-permute-start | bytes 1179656 | tf_op jit(solution)/shard_map/ppermute | solution.py:423
  113.1 17.9 %collective-permute-start.13 = (bf16[96,2048]{1,0:T(8,128)(2,1)S(1)}, bf16[96,2048]{1,0:T(8,128)(2,1)S(1)}, u32[]{:S(2)}, u32[]{:S(2)}) collective-permute-start(bf16[96,2048]{1,0:T(8,128)(2,1)S(1)} %get-tuple-element.44), channel_id=1, source_target_pairs={{32,2},{34,0},{64,34},{66,32},{96,66},{98,64},{128,98},{130,96},{1... | collective-permute-start | bytes 1179656 | tf_op jit(solution)/shard_map/ppermute | solution.py:423
  116.8 17.2 %collective-permute-start.8 = (bf16[96,2048]{1,0:T(8,128)(2,1)S(1)}, bf16[96,2048]{1,0:T(8,128)(2,1)S(1)}, u32[]{:S(2)}, u32[]{:S(2)}) collective-permute-start(bf16[96,2048]{1,0:T(8,128)(2,1)S(1)} %get-tuple-element.38), channel_id=1, source_target_pairs={{0,32},{2,34},{32,64},{34,66},{64,96},{66,98},{96,128},{98,130},{1... | collective-permute-start | bytes 1179656 | tf_op jit(solution)/shard_map/ppermute | solution.py:423
  121.1 20.9 %collective-permute-start.9 = (bf16[96,2048]{1,0:T(8,128)(2,1)S(1)}, bf16[96,2048]{1,0:T(8,128)(2,1)S(1)}, u32[]{:S(2)}, u32[]{:S(2)}) collective-permute-start(bf16[96,2048]{1,0:T(8,128)(2,1)S(1)} %get-tuple-element.39), channel_id=1, source_target_pairs={{0,34},{2,32},{32,66},{34,64},{64,98},{66,96},{96,130},{98,128},{1... | collective-permute-start | bytes 1179656 | tf_op jit(solution)/shard_map/ppermute | solution.py:423
  131.1 17.6 %collective-permute-start.14 = (bf16[96,2048]{1,0:T(8,128)(2,1)S(1)}, bf16[96,2048]{1,0:T(8,128)(2,1)S(1)}, u32[]{:S(2)}, u32[]{:S(2)}) collective-permute-start(bf16[96,2048]{1,0:T(8,128)(2,1)S(1)} %shard_map.149.refs_2_), channel_id=1, source_target_pairs={{0,1},{1,0},{2,3},{3,2},{4,5},{5,4},{6,7},{7,6},{8,9},{9,8},{10,11... | collective-permute-start | bytes 1179656 | tf_op jit(solution)/shard_map/ppermute | solution.py:340
  142.1 12.2 %copy-start.3 = (s32[1,2,128,256]{3,2,1,0:T(8,128)S(1)}, s32[1,2,128,256]{3,2,1,0:T(8,128)}, u32[]{:S(2)}) copy-start(s32[1,2,128,256]{3,2,1,0:T(8,128)} %param.17) | copy-start | bytes 786436
  142.1 12.2 %copy-start.4 = (s32[1,256,128]{2,1,0:T(8,128)S(1)}, s32[1,256,128]{2,1,0:T(8,128)}, u32[]{:S(2)}) copy-start(s32[1,256,128]{2,1,0:T(8,128)} %param.18) | copy-start | bytes 393220
  142.1 12.1 %copy-start.6 = (f32[1,2,2,128,1]{3,4,2,1,0:T(1,128)S(1)}, f32[1,2,2,128,1]{3,4,2,1,0:T(1,128)}, u32[]{:S(2)}) copy-start(f32[1,2,2,128,1]{3,4,2,1,0:T(1,128)} %param.19) | copy-start | bytes 6148
  142.2 12.1 %copy-start.7 = (f32[1,2,1,128]{3,2,1,0:T(1,128)S(1)}, f32[1,2,1,128]{3,2,1,0:T(1,128)}, u32[]{:S(2)}) copy-start(f32[1,2,1,128]{3,2,1,0:T(1,128)} %param.20) | copy-start | bytes 3076
  142.2 6.5 %collective-permute-start.10 = (bf16[96,2048]{1,0:T(8,128)(2,1)S(1)}, bf16[96,2048]{1,0:T(8,128)(2,1)S(1)}, u32[]{:S(2)}, u32[]{:S(2)}) collective-permute-start(bf16[96,2048]{1,0:T(8,128)(2,1)S(1)} %shard_map.146.refs_0_), channel_id=1, source_target_pairs={{0,1},{1,0},{2,3},{3,2},{4,5},{5,4},{6,7},{7,6},{8,9},{9,8},{10,11... | collective-permute-start | bytes 1179656 | tf_op jit(solution)/shard_map/ppermute | solution.py:340
  145.7 8.6 %collective-permute-start.15 = (bf16[384,128]{1,0:T(8,128)(2,1)S(1)}, bf16[384,128]{1,0:T(8,128)(2,1)S(1)}, u32[]{:S(2)}, u32[]{:S(2)}) collective-permute-start(bf16[384,128]{1,0:T(8,128)(2,1)S(1)} %get-tuple-element.49), channel_id=1, source_target_pairs={{0,2},{2,0},{1,3},{3,1},{4,6},{6,4},{5,7},{7,5},{8,10},{10,8},{9,1... | collective-permute-start | bytes 294920 | tf_op jit(solution)/shard_map/ppermute | solution.py:337

commit v3 on v2

--- a/solution.py
+++ b/solution.py
@@ -62,9 +62,9 @@
 
 
 def predict_body(lag_ref, x_ref, *refs):
-    hbm, give, send = refs[:6], refs[6], refs[7]
+    hbm, give, mine = refs[:6], refs[6], refs[7]
     w_in, c_in, s_in, w_out, c_out, s_out = refs[8:14]
-    blocks_ref, in_sem, out_sem = refs[14:]
+    in_sem = refs[14]
     xh = x_ref[0]
     loads = [pltpu.make_async_copy(hbm[i], refs[8 + i], in_sem.at[i]) for i in range(6)]
     for load in loads:
@@ -74,55 +74,48 @@
     rate = LEARN_RATE * lag_ref[0].astype(F32)
     sm = [column(s_in[i : i + 1, :], 128) for i in range(2)]
     sv = [column(s_in[2 + i : 3 + i, :], 128) for i in range(2)]
-    for h in range(2):
-        lanes = slice(h * 128, h * 128 + 128)
+    for h, out in ((1 - xh, give), (xh, mine)):
+        part = pl.ds(pl.multiple_of(h * 128, 128), 128)
         for i in range(2):
-            piece = predicted(w_in[i, :, lanes], c_in[i, :, lanes], sm[i], sv[i], rate)
-            blocks_ref[h, :, i * 128 : i * 128 + 128] = piece.astype(BF16)
-        piece = predicted(w_out[lanes, :], c_out[lanes, :], s_out[0:1, :], s_out[1:2, :], rate)
-        blocks_ref[h, :, 256:384] = piece.T.astype(BF16)
-    give[...] = blocks_ref[1 - xh]
-    stores = [pltpu.make_async_copy(blocks_ref.at[xh], send.at[j, xh], out_sem.at[j]) for j in range(8)]
-    for store in stores:
-        store.start()
-    for store in stores:
-        store.wait()
-
-
-def halves_body(k_ref, *refs):
+            piece = predicted(w_in[i, :, part], c_in[i, :, part], sm[i], sv[i], rate)
+            out[:, i * 128 : i * 128 + 128] = piece.astype(BF16)
+        piece = predicted(w_out[part, :], c_out[part, :], s_out[0:1, :], s_out[1:2, :], rate)
+        out[:, 256:384] = piece.T.astype(BF16)
+
+
+def halves_body(k_ref, x_b, dy, x_f, both, half_f, sem):
     rows = pl.ds(pl.multiple_of(k_ref[0] * 96, 32), 96)
-    loads = [pltpu.make_async_copy(refs[i].at[rows, :], refs[3 + i], refs[6].at[i]) for i in range(3)]
+    loads = [
+        pltpu.make_async_copy(x_b.at[rows, :], both.at[0:96, :], sem.at[0]),
+        pltpu.make_async_copy(dy.at[rows, :], both.at[96:192, :], sem.at[1]),
+        pltpu.make_async_copy(x_f.at[rows, :], half_f, sem.at[2]),
+    ]
     for load in loads:
         load.start()
     for load in loads:
         load.wait()
-
-
-def fill_body(x_ref, other, _, send, sem):
-    stores = [pltpu.make_async_copy(other, send.at[j, 1 - x_ref[0]], sem.at[j]) for j in range(8)]
-    for store in stores:
-        store.start()
-    for store in stores:
-        store.wait()
 
 
 def rms(x):
     return lax.rsqrt(jnp.mean(x * x, axis=-1, keepdims=True) + NORM_EPS)
 
 
-def normed_hbm_body(gain_ref, own, near, far, out, rows):
-    normed_body(gain_ref, own, near, far, rows)
-    pltpu.sync_copy(rows, out)
-
-
-def normed_body(gain_ref, own, near, far, out):
+def row_loads(parts, rows, sem, first):
+    copies, at = [], 0
+    for i, part in enumerate(parts):
+        copies.append(pltpu.make_async_copy(part, rows.at[at : at + part.shape[0], :], sem.at[first + i]))
+        at += part.shape[0]
+    return copies
+
+
+def norm_rows(gain_ref, rows, out):
     gain = gain_ref[...]
 
     def step(i, carry):
-        r = pl.multiple_of(i * 16, 16)
-        for start, ref, at in ((0, own, r), (96, own, 96 + r), (192, near, r), (288, far, r)):
-            x = ref[pl.ds(pl.multiple_of(at, 16), 16), :].astype(F32)
-            out[pl.ds(pl.multiple_of(start + r, 16), 16), :] = (x * rms(x) * gain).astype(BF16)
+        for start in (0, 96, 192, 288):
+            at = pl.ds(pl.multiple_of(start + i * 16, 16), 16)
+            x = rows[at, :].astype(F32)
+            out[at, :] = (x * rms(x) * gain).astype(BF16)
         return carry
 
     lax.fori_loop(0, 6, step, 0)
@@ -134,22 +127,24 @@
     return ((0, first), (96, second), (192, 192), (288, 288))
 
 
-def backward_body(k_ref, nb_hbm, own, near, far, w, grads, dgu, gu_acc, dh_acc, left, dy, nb, ordered, out, in_sem, sem):
-    chunks = [slice(j * 512, j * 512 + 512) for j in range(4)]
-    nb_loads = [pltpu.make_async_copy(nb_hbm.at[:, c], nb.at[:, c], in_sem.at[3 + j]) for j, c in enumerate(chunks)]
-    loads = [
-        pltpu.make_async_copy(own, dy.at[0:192, :], in_sem.at[0]),
-        pltpu.make_async_copy(near, dy.at[192:288, :], in_sem.at[1]),
-        pltpu.make_async_copy(far, dy.at[288:384, :], in_sem.at[2]),
-    ]
-    for load in nb_loads + loads:
+def backward_body(k_ref, gain, x_own, y_own, near, far, w, grads, dgu, gu_acc, dh_acc, left, dy, x, nb, out, in_sem, sem):
+    x_loads = row_loads((x_own, near.at[0:96, :], far.at[0:96, :]), x, in_sem, 0)
+    y_loads = row_loads((y_own, near.at[96:192, :], far.at[96:192, :]), dy, in_sem, 3)
+    for load in x_loads + y_loads:
         load.start()
+    for load in x_loads:
+        load.wait()
+    norm_rows(gain, x, nb)
     gu_acc[...] = jnp.zeros_like(gu_acc)
     dh_acc[...] = jnp.zeros_like(dh_acc)
-    for load, d in zip(nb_loads, chunks):
-        load.wait()
+
+    def contract(j, carry):
+        d = pl.ds(pl.multiple_of(j * 512, 512), 512)
         gu_acc[...] += jnp.dot(nb[:, d], w[d, 0:256], preferred_element_type=F32)
-    for load in loads:
+        return carry
+
+    lax.fori_loop(0, 4, contract, 0)
+    for load in y_loads:
         load.wait()
 
     def contract_dy(j, carry):
@@ -185,8 +180,7 @@
 
     lax.fori_loop(0, 8, expand, 0)
     for at, start in blocks(k_ref[0]):
-        ordered[at : at + 96, :] = gu_acc[pl.ds(start, 96), :].astype(BF16)
-    pltpu.sync_copy(ordered, dgu)
+        dgu[at : at + 96, :] = gu_acc[pl.ds(start, 96), :].astype(BF16)
     for j in range(8):
         pair = pl.ds(2 * j, 2)
         pltpu.make_async_copy(out.at[pair], grads.at[pair], sem.at[j]).wait()
@@ -205,20 +199,25 @@
     lax.fori_loop(0, 8, step, 0)
 
 
-def cotangent_body(dgu_hbm, w, keep, send, dgu):
-    pltpu.sync_copy(dgu_hbm, dgu)
+def cotangent_body(dgu, w, keep, send):
     project(dgu, w, 0, 256, keep, send)
 
 
-def forward_body(k_ref, nf_hbm, w, keep, send, gu_acc, hidden, nf, sem):
-    chunks = [slice(j * 512, j * 512 + 512) for j in range(4)]
-    loads = [pltpu.make_async_copy(nf_hbm.at[:, c], nf.at[:, c], sem.at[j]) for j, c in enumerate(chunks)]
+def forward_body(k_ref, gain, x_own, near, far, w, keep, send, gu_acc, hidden, x, nf, sem):
+    loads = row_loads((x_own, near, far), x, sem, 0)
     for load in loads:
         load.start()
-    for j, d in enumerate(chunks):
-        loads[j].wait()
-        part = jnp.dot(nf[:, d], w[d, 0:256], preferred_element_type=F32)
-        gu_acc[...] = part if j == 0 else gu_acc[...] + part
+    for load in loads:
+        load.wait()
+    norm_rows(gain, x, nf)
+    gu_acc[...] = jnp.zeros_like(gu_acc)
+
+    def contract(j, carry):
+        d = pl.ds(pl.multiple_of(j * 512, 512), 512)
+        gu_acc[...] += jnp.dot(nf[:, d], w[d, 0:256], preferred_element_type=F32)
+        return carry
+
+    lax.fori_loop(0, 4, contract, 0)
     for at, start in blocks(k_ref[0]):
         rows = pl.ds(start, 96)
         g, u = gu_acc[rows, 0:128], gu_acc[rows, 128:256]
@@ -266,21 +265,21 @@
     lax.fori_loop(0, 6, step, 0)
 
 
-def rejoin_body(k_ref, *refs):
-    pieces, outs, sem = refs[:4], refs[4:6], refs[6]
+def rejoin_body(k_ref, mine, other, next_rows, back_rows, sem):
     stores = []
-    for i in range(4):
-        at = k_ref[0] if i % 2 == 0 else 1 - k_ref[0]
+    for i, (piece, at) in enumerate(((mine, k_ref[0]), (other, 1 - k_ref[0]))):
         rows = pl.ds(pl.multiple_of(at * 96, 32), 96)
-        stores.append(pltpu.make_async_copy(pieces[i], outs[i // 2].at[rows, :], sem.at[i]))
+        stores.append(pltpu.make_async_copy(piece.at[0:96, :], next_rows.at[rows, :], sem.at[2 * i]))
+        stores.append(pltpu.make_async_copy(piece.at[96:192, :], back_rows.at[rows, :], sem.at[2 * i + 1]))
     for store in stores:
         store.start()
     for store in stores:
         store.wait()
 
 
-def add_body(a, b, out):
-    out[...] = (a[...].astype(F32) + b[...].astype(F32)).astype(BF16)
+def add_body(a, b, c, d, out):
+    out[0:96, :] = (a[...].astype(F32) + b[...].astype(F32)).astype(BF16)
+    out[96:192, :] = (c[...].astype(F32) + d[...].astype(F32)).astype(BF16)
 
 
 def stepped(m, root, grad):
@@ -339,58 +338,51 @@
     def on_chip(x):
         return lax.ppermute(x, "hid", swap)
 
-    def exchange(x):
-        return lax.all_to_all(x, "y", 0, 0, tiled=True)
+    def exchange(x, axes):
+        return lax.all_to_all(x, axes, 0, 0, tiled=True)
 
     def after(x, other):
         return lax.optimization_barrier((x, other))[0]
 
-    tokens, part, piece = struct((384, 2048)), struct((192, 2048)), struct((96, 2048))
+    part, piece = struct((192, 2048)), struct((96, 2048))
+    xh = lax.axis_index("xh")
     quarter = struct((128, 384))
     give, mine = call(
-        predict_body, [quarter, struct((8, 2, 128, 384))],
-        [lags, x_arr, w_in[0], c_in, s_in, w_out[0], c_out, s_out],
+        predict_body, [quarter, quarter],
+        [lags, xh.astype(jnp.int32).reshape(1), w_in[0], c_in, s_in, w_out[0], c_out, s_out],
         scratch=[
             pltpu.VMEM((2, 128, 256), F32), pltpu.VMEM((2, 128, 256), jnp.int32), pltpu.VMEM((4, 128), F32),
             pltpu.VMEM((256, 128), F32), pltpu.VMEM((256, 128), jnp.int32), pltpu.VMEM((2, 128), F32),
-            pltpu.VMEM((2, 128, 384), BF16), pltpu.SemaphoreType.DMA((6,)), pltpu.SemaphoreType.DMA((8,)),
+            pltpu.SemaphoreType.DMA((6,)),
         ],
-        n_smem=2, hbm_in=range(2, 8), hbm_out=(1,),
+        n_smem=2, hbm_in=range(2, 8),
     )
     other = across(give)
-    half_b, half_y, half_f = call(
-        halves_body, [piece, piece, piece], [k_arr, after(x_b, give), dy, x_f],
+    rows = jnp.where(xh == 0, jnp.concatenate([mine, other]), jnp.concatenate([other, mine])).astype(jnp.float16)
+    gathered = lax.all_gather(rows, "y", axis=0, tiled=True)
+    half, half_f = call(
+        halves_body, [part, piece], [k_arr, after(x_b, give), dy, x_f],
         scratch=[pltpu.SemaphoreType.DMA((3,))], n_smem=1, hbm_in=(1, 2, 3),
     )
-    (send,) = call(
-        fill_body, [struct((8, 2, 128, 384))], [x_arr, other, mine],
-        scratch=[pltpu.SemaphoreType.DMA((8,))], n_smem=1, hbm_in=(2,), hbm_out=(0,), alias={2: 0},
-    )
-    weights = exchange(send).reshape(2048, 384)
-
-    near_b = across(half_b)
-    near_y = across(half_y)
-    far_b = on_chip(near_b)
-    far_y = on_chip(near_y)
+
+    near = across(half)
+    near, half_f, gathered = lax.optimization_barrier((near, half_f, gathered))
+    weights = gathered.astype(BF16)
+    far = on_chip(near)
     near_f = across(half_f)
     far_f = on_chip(near_f)
-    (nb,) = call(normed_hbm_body, [tokens], [gain, x_b, near_b, far_b], hbm_out=(0,), scratch=[pltpu.VMEM((384, 2048), BF16)])
-    (nf,) = call(
-        normed_hbm_body, [tokens], [gain, x_f, near_f, far_f],
-        hbm_out=(0,), scratch=[pltpu.VMEM((384, 2048), BF16)],
-    )
 
     grads, dgu = call(
-        backward_body, [struct((16, 384, 128)), struct((384, 256))], [k_arr, nb, dy, near_y, far_y, weights],
+        backward_body, [struct((16, 384, 128)), struct((384, 256))], [k_arr, gain, x_b, dy, near, far, weights],
         scratch=[
             pltpu.VMEM((384, 256), F32), pltpu.VMEM((384, 128), F32),
-            pltpu.VMEM((384, 384), BF16), pltpu.VMEM((384, 2048), BF16),
-            pltpu.VMEM((384, 2048), BF16), pltpu.VMEM((384, 256), BF16),
-            pltpu.VMEM((16, 384, 128), BF16), pltpu.SemaphoreType.DMA((7,)), pltpu.SemaphoreType.DMA((8,)),
+            pltpu.VMEM((384, 384), BF16), pltpu.VMEM((384, 2048), BF16), pltpu.VMEM((384, 2048), BF16),
+            pltpu.VMEM((384, 2048), BF16),
+            pltpu.VMEM((16, 384, 128), BF16), pltpu.SemaphoreType.DMA((6,)), pltpu.SemaphoreType.DMA((8,)),
         ],
-        flops=4 * 384 * 384 * 2048, n_smem=1, hbm_in=(1, 2, 3, 4), hbm_out=(0, 1),
-    )
-    received = exchange(grads.reshape(8, 2, 384, 128))
+        flops=4 * 384 * 384 * 2048, n_smem=1, hbm_in=(2, 3, 4, 5), hbm_out=(0,),
+    )
+    received = exchange(grads.reshape(8, 2, 384, 128), "y")
     own_sum, give = call(
         sum_body, [struct((384, 128), F32), struct((384, 128))], [x_arr, received],
         scratch=[pltpu.VMEM((8, 2, 384, 128), BF16), pltpu.SemaphoreType.DMA((6,))],
@@ -398,36 +390,32 @@
     )
     other_sum = across(give)
 
+    e_keep, e_send = call(cotangent_body, [part, part], [dgu, weights], flops=2 * 384 * 256 * 2048)
+    e_recv = on_chip(e_send)
     q_keep, q_send = call(
-        forward_body, [part, part], [k_arr, after(nf, dgu), weights],
+        forward_body, [part, part], [k_arr, gain, x_f, near_f, after(far_f, e_send), weights],
         scratch=[
             pltpu.VMEM((384, 256), F32), pltpu.VMEM((384, 128), BF16),
-            pltpu.VMEM((384, 2048), BF16), pltpu.SemaphoreType.DMA((4,)),
+            pltpu.VMEM((384, 2048), BF16), pltpu.VMEM((384, 2048), BF16), pltpu.SemaphoreType.DMA((3,)),
         ],
-        flops=2 * 384 * 384 * 2048, n_smem=1, hbm_in=(1,),
+        flops=2 * 384 * 384 * 2048, n_smem=1, hbm_in=(2, 3, 4),
     )
     q_recv = on_chip(q_send)
-    e_keep, e_send = call(
-        cotangent_body, [part, part], [after(dgu, q_send), weights],
-        scratch=[pltpu.VMEM((384, 256), BF16)], flops=2 * 384 * 256 * 2048, hbm_in=(0,),
-    )
-    e_recv = on_chip(e_send)
     ahead = call(ahead_body, [piece, piece], [k_arr, x_f, q_keep, q_recv], n_smem=1)
-    back = call(back_body, [piece, piece], [k_arr, gain, x_b, near_b, dy, e_keep, e_recv], n_smem=1)
+    back = call(back_body, [piece, piece], [k_arr, gain, x_b, near, dy, e_keep, e_recv], n_smem=1)
 
     def relay(pieces, distance):
         moves = [(s, s + distance) for s in range(sections) if 0 <= s + distance < sections]
         same = [(2 * s + h, 2 * t + h) for s, t in moves for h in range(2)]
         cross = [(2 * s + h, 2 * t + 1 - h) for s, t in moves for h in range(2)]
         axes = ("section", "xh")
-        own, pair = lax.ppermute(pieces[0], axes, same), lax.ppermute(pieces[1], axes, cross)
-        (mine,) = call(add_body, [piece], [own, pair])
-        return mine, on_chip(mine)
-
-    next_halves = relay(ahead, 1)
-    back_halves = relay(back, -1)
+        return lax.ppermute(pieces[0], axes, same), lax.ppermute(pieces[1], axes, cross)
+
+    next_parts = relay(ahead, 1)
+    back_parts = relay(back, -1)
+    (joined,) = call(add_body, [part], [*next_parts, *back_parts])
     next_rows, back_rows = call(
-        rejoin_body, [part, part], [k_arr, *next_halves, *back_halves],
+        rejoin_body, [part, part], [k_arr, joined, on_chip(joined)],
         scratch=[pltpu.SemaphoreType.DMA((4,))], n_smem=1, hbm_out=(0, 1),
     )
 

time: 156 us -> 141 us (0.904)
  blocking collectives: 0 us -> 28.9 us
  waiting for transfers between devices: 59.3 us -> 34.6 us
  starting transfers between devices: 66.9 us -> 51 us
  Pallas kernels: 27.5 us -> 22.6 us
  local copies, waits for them, and re-layouts: 0.06 us -> 1.68 us
    all_gather x0 -> x1, blocking collectives: none -> 28.9 us  [tick(): gathered = lax.all_gather(rows, 'y', axis=0, tiled=True)]
    ppermute x5 -> x4, waiting for transfers between devices: 30.3 us -> 14.9 us  [across(): return lax.ppermute(x, 'xh', swap)]
    all_to_all x2 -> x1, waiting for transfers between devices: 11 us -> 0.01 us  [exchange(): return lax.all_to_all(x, axes, 0, 0, tiled=True)]
    all_to_all x2 -> x1, starting transfers between devices: 13.3 us -> 6.96 us  [exchange(): return lax.all_to_all(x, axes, 0, 0, tiled=True)]
    ppermute x2, starting transfers between devices: 15.2 us -> 9.05 us  [relay(): lax.ppermute(pieces[0], axes, same)]
    pallas_call x15 -> x11, Pallas kernels: 27.5 us -> 22.6 us  [call(): pl.pallas_call(body, out_shape=tuple(((pltpu.HBM if i in hbm_out else jax...]
    ppermute x2, starting transfers between devices: 5.89 us -> 10.6 us  [relay(): lax.ppermute(pieces[1], axes, cross)]
    ppermute x5 -> x4, starting transfers between devices: 18.5 us -> 13.9 us  [across(): return lax.ppermute(x, 'xh', swap)]
  transfers between devices with their start and end apart: 18 -> 14, of which waited for: 10 -> 5; matrix products, arithmetic and copies ran while one was open for 0% -> 0% of each run, Pallas kernels for 11% -> 9%
where the time goes in v3:
time: 141 us
  starting transfers between devices  51 us (36%)
  waiting for transfers between devices  34.6 us (25%)
  blocking collectives  28.9 us (20%)
  Pallas kernels  22.6 us (16%)
  local copies, waits for them, and re-layouts  1.68 us (1%)
  between operations  1.66 us (1%)
    all_gather x1, blocking collectives, tick(): gathered = lax.all_gather(rows, 'y', axis=0, tiled=True)  28.9 us
    pallas_call x11, Pallas kernels, call(): pl.pallas_call(body, out_shape=tuple(((pltpu.HBM if i in hbm_out else jax...  22.6 us
    ppermute x2, waiting for transfers between devices, relay(): lax.ppermute(pieces[1], axes, cross)  17.7 us
    ppermute x4, waiting for transfers between devices, across(): return lax.ppermute(x, 'xh', swap)  14.9 us
    ppermute x4, starting transfers between devices, across(): return lax.ppermute(x, 'xh', swap)  13.9 us
    ppermute x2, starting transfers between devices, relay(): lax.ppermute(pieces[1], axes, cross)  10.6 us
    ppermute x5, starting transfers between devices, on_chip(): return lax.ppermute(x, 'hid', swap)  10.5 us
    ppermute x2, starting transfers between devices, relay(): lax.ppermute(pieces[0], axes, same)  9.05 us
  transfers between devices with their start and end apart: 14, of which 5 were waited for; matrix products, arithmetic and copies ran while one was open for 0% of the time, Pallas kernels for 9%

profile of v3, /device:TPU:10, one launch (start us, length us, event | category | flops | bytes accessed | tf_op | source)
XLA Modules:
  0.0 140.7 jit_solution(7706906474926701854)
XLA Ops:
  1.3 1.4 %shard_map.138 = (bf16[128,384]{1,0:T(8,128)(2,1)S(1)}, bf16[128,384]{1,0:T(8,128)(2,1)S(1)}) custom-call(s32[1]{0:T(128)S(6)} %copy.15.lag_ref, s32[1]{0:T(128)} %bitcast.3.x_ref, f32[2,128,256]{2,1,0:T(8,128)} %bitcast.34, s32[2,128,256]{2,1,0:T(8,128)} %bitcast.25, f32[4,128]{1,0:T(4,128)} %bitcast.29, f32[256,128]{1,0:T(8,128)} %bitcast.35, ...), custom_call_target="tpu_custom_call" | custom-call | bytes 986120 | tf_op jit(solution)/shard_map/pallas_call | solution.py:31
  2.7 4.0 %collective-permute-start.1 = (bf16[128,384]{1,0:T(8,128)(2,1)S(1)}, bf16[128,384]{1,0:T(8,128)(2,1)S(1)}, u32[]{:S(2)}, u32[]{:S(2)}) collective-permute-start(bf16[128,384]{1,0:T(8,128)(2,1)S(1)} %get-tuple-element.29), channel_id=1, source_target_pairs={{0,2},{2,0},{1,3},{3,1},{4,6},{6,4},{5,7},{7,5},{8,10},{10,8},{9,1... | collective-permute-start | bytes 294920 | tf_op jit(solution)/shard_map/ppermute | solution.py:336
  6.8 1.3 shard_map.139
  8.0 3.3 %collective-permute-start = (bf16[192,2048]{1,0:T(8,128)(2,1)S(1)}, bf16[192,2048]{1,0:T(8,128)(2,1)S(1)}, u32[]{:S(2)}, u32[]{:S(2)}) collective-permute-start(bf16[192,2048]{1,0:T(8,128)(2,1)S(1)} %get-tuple-element.31), channel_id=1, source_target_pairs={{0,2},{2,0},{1,3},{3,1},{4,6},{6,4},{5,7},{7,5},{8,10},{10,8},{9,1... | collective-permute-start | bytes 2359304 | tf_op jit(solution)/shard_map/ppermute | solution.py:336
  11.4 28.9 %all-gather.1 = f16[2048,384]{1,0:T(8,128)(2,1)S(1)} all-gather(f16[256,384]{1,0:T(8,128)(2,1)S(1)} %fusion), channel_id=1, replica_groups=mesh['section'=16,'y'=8,'xh'=2,'hid'=2] {'y'}, dimensions={0}, use_global_device_ids=true | all-gather | bytes 1769472 | tf_op jit(solution)/shard_map/all_gather | solution.py:362
  40.3 2.1 %collective-permute-start.4 = (bf16[192,2048]{1,0:T(8,128)(2,1)S(1)}, bf16[192,2048]{1,0:T(8,128)(2,1)S(1)}, u32[]{:S(2)}, u32[]{:S(2)}) collective-permute-start(bf16[192,2048]{1,0:T(8,128)(2,1)S(1)} %collective-permute-done.near.x_near), channel_id=1, source_target_pairs={{0,1},{1,0},{2,3},{3,2},{4,5},{5,4},{6,7},{7,6},{8,9},{9,8},{10,11... | collective-permute-start | bytes 2359304 | tf_op jit(solution)/shard_map/ppermute | solution.py:339
  42.4 0.3 convert_element_type.7.w
  42.6 2.0 %collective-permute-done.4.far = bf16[192,2048]{1,0:T(8,128)(2,1)S(1)} collective-permute-done((bf16[192,2048]{1,0:T(8,128)(2,1)S(1)}, bf16[192,2048]{1,0:T(8,128)(2,1)S(1)}, u32[]{:S(2)}, u32[]{:S(2)}) %collective-permute-start.4) | collective-permute-done | bytes 786464 | tf_op jit(solution)/shard_map/ppermute | solution.py:339
  44.6 0.9 copy-done.10
  45.5 7.5 %shard_map.140 = (bf16[16,384,128]{2,1,0:T(8,128)(2,1)}, bf16[384,256]{1,0:T(8,128)(2,1)S(1)}) custom-call(s32[1]{0:T(128)} %bitcast.k_ref, f32[1,2048]{1,0:T(1,128)S(1)} %copy-done.7, bf16[192,2048]{1,0:T(8,128)(2,1)} %bitcast.20, bf16[192,2048]{1,0:T(8,128)(2,1)} %bitcast.23, bf16[192,2048]{1,0:T(8,128)(2,1)} %copy-done.3, bf16[192,2048]{1,0:T(8,128)(2,1)} %copy-done.10, ...), custom_call_target="tpu_custom_call" | custom-call | flops 1207959552 | bytes 6496260 | tf_op jit(solution)/shard_map/pallas_call | solution.py:31
  53.0 7.0 %all-to-all-start = ((bf16[8,2,384,128]{3,2,1,0:T(8,128)(2,1)}), bf16[8,2,384,128]{3,2,1,0:T(8,128)(2,1)}, u32[]{:S(2)}, u32[]{:S(2)}) async-start(bf16[8,2,384,128]{3,2,1,0:T(8,128)(2,1)} %bitcast.33), calls=%async_computation | async-start | bytes 3145728 | tf_op jit(solution)/shard_map/all_to_all | solution.py:342
  60.0 3.7 %collective-permute-start.2 = (bf16[96,2048]{1,0:T(8,128)(2,1)S(1)}, bf16[96,2048]{1,0:T(8,128)(2,1)S(1)}, u32[]{:S(2)}, u32[]{:S(2)}) collective-permute-start(bf16[96,2048]{1,0:T(8,128)(2,1)S(1)} %get-tuple-element.34), channel_id=1, source_target_pairs={{0,2},{2,0},{1,3},{3,1},{4,6},{6,4},{5,7},{7,5},{8,10},{10,8},{9,1... | collective-permute-start | bytes 1179656 | tf_op jit(solution)/shard_map/ppermute | solution.py:336
  63.7 10.3 %collective-permute-done.2.near = bf16[96,2048]{1,0:T(8,128)(2,1)S(1)} collective-permute-done((bf16[96,2048]{1,0:T(8,128)(2,1)S(1)}, bf16[96,2048]{1,0:T(8,128)(2,1)S(1)}, u32[]{:S(2)}, u32[]{:S(2)}) %collective-permute-start.2) | collective-permute-done | bytes 393248 | tf_op jit(solution)/shard_map/ppermute | solution.py:336
  73.9 1.9 %collective-permute-start.3 = (bf16[96,2048]{1,0:T(8,128)(2,1)S(1)}, bf16[96,2048]{1,0:T(8,128)(2,1)S(1)}, u32[]{:S(2)}, u32[]{:S(2)}) collective-permute-start(bf16[96,2048]{1,0:T(8,128)(2,1)S(1)} %collective-permute-done.2.near), channel_id=1, source_target_pairs={{0,1},{1,0},{2,3},{3,2},{4,5},{5,4},{6,7},{7,6},{8,9},{9,8},{10,11... | collective-permute-start | bytes 1179656 | tf_op jit(solution)/shard_map/ppermute | solution.py:339
  75.8 2.0 %shard_map.141 = (bf16[192,2048]{1,0:T(8,128)(2,1)S(1)}, bf16[192,2048]{1,0:T(8,128)(2,1)S(1)}) custom-call(bf16[384,256]{1,0:T(8,128)(2,1)S(1)} %get-tuple-element.37.dgu, bf16[2048,384]{1,0:T(8,128)(2,1)S(1)} %convert_element_type.7.w), custom_call_target="tpu_custom_call" | custom-call | flops 402653184 | bytes 3342336 | tf_op jit(solution)/shard_map/pallas_call | solution.py:31
  77.9 0.7 copy-done.12
  78.6 5.2 %shard_map.142 = (bf16[192,2048]{1,0:T(8,128)(2,1)S(1)}, bf16[192,2048]{1,0:T(8,128)(2,1)S(1)}) custom-call(s32[1]{0:T(128)} %bitcast.k_ref, f32[1,2048]{1,0:T(1,128)S(1)} %copy-done.7, bf16[192,2048]{1,0:T(8,128)(2,1)} %bitcast.17, bf16[96,2048]{1,0:T(8,128)(2,1)} %copy-done.11, bf16[96,2048]{1,0:T(8,128)(2,1)} %copy-done.12, ...), custom_call_target="tpu_custom_call" | custom-call | flops 603979776 | bytes 4726788 | tf_op jit(solution)/shard_map/pallas_call | solution.py:31
  83.9 2.6 %collective-permute-start.5 = (bf16[192,2048]{1,0:T(8,128)(2,1)S(1)}, bf16[192,2048]{1,0:T(8,128)(2,1)S(1)}, u32[]{:S(2)}, u32[]{:S(2)}) collective-permute-start(bf16[192,2048]{1,0:T(8,128)(2,1)S(1)} %get-tuple-element.41), channel_id=1, source_target_pairs={{0,1},{1,0},{2,3},{3,2},{4,5},{5,4},{6,7},{7,6},{8,9},{9,8},{10,11... | collective-permute-start | bytes 2359304 | tf_op jit(solution)/shard_map/ppermute | solution.py:339
  86.4 1.9 %collective-permute-start.8 = (bf16[192,2048]{1,0:T(8,128)(2,1)S(1)}, bf16[192,2048]{1,0:T(8,128)(2,1)S(1)}, u32[]{:S(2)}, u32[]{:S(2)}) collective-permute-start(bf16[192,2048]{1,0:T(8,128)(2,1)S(1)} %get-tuple-element.38), channel_id=1, source_target_pairs={{0,1},{1,0},{2,3},{3,2},{4,5},{5,4},{6,7},{7,6},{8,9},{9,8},{10,11... | collective-permute-start | bytes 2359304 | tf_op jit(solution)/shard_map/ppermute | solution.py:339
  88.7 4.3 %collective-permute-start.6 = (bf16[96,2048]{1,0:T(8,128)(2,1)S(1)}, bf16[96,2048]{1,0:T(8,128)(2,1)S(1)}, u32[]{:S(2)}, u32[]{:S(2)}) collective-permute-start(bf16[96,2048]{1,0:T(8,128)(2,1)S(1)} %get-tuple-element.42), channel_id=1, source_target_pairs={{0,32},{2,34},{32,64},{34,66},{64,96},{66,98},{96,128},{98,130},{1... | collective-permute-start | bytes 1179656 | tf_op jit(solution)/shard_map/ppermute | solution.py:412
  93.0 5.5 %collective-permute-start.7 = (bf16[96,2048]{1,0:T(8,128)(2,1)S(1)}, bf16[96,2048]{1,0:T(8,128)(2,1)S(1)}, u32[]{:S(2)}, u32[]{:S(2)}) collective-permute-start(bf16[96,2048]{1,0:T(8,128)(2,1)S(1)} %get-tuple-element.43), channel_id=1, source_target_pairs={{0,34},{2,32},{32,66},{34,64},{64,98},{66,96},{96,130},{98,128},{1... | collective-permute-start | bytes 1179656 | tf_op jit(solution)/shard_map/ppermute | solution.py:412
  98.5 1.0 shard_map.144
  99.6 4.8 %collective-permute-start.9 = (bf16[96,2048]{1,0:T(8,128)(2,1)S(1)}, bf16[96,2048]{1,0:T(8,128)(2,1)S(1)}, u32[]{:S(2)}, u32[]{:S(2)}) collective-permute-start(bf16[96,2048]{1,0:T(8,128)(2,1)S(1)} %get-tuple-element.45), channel_id=1, source_target_pairs={{32,0},{34,2},{64,32},{66,34},{96,64},{98,66},{128,96},{130,98},{1... | collective-permute-start | bytes 1179656 | tf_op jit(solution)/shard_map/ppermute | solution.py:412
  104.3 5.1 %collective-permute-start.10 = (bf16[96,2048]{1,0:T(8,128)(2,1)S(1)}, bf16[96,2048]{1,0:T(8,128)(2,1)S(1)}, u32[]{:S(2)}, u32[]{:S(2)}) collective-permute-start(bf16[96,2048]{1,0:T(8,128)(2,1)S(1)} %get-tuple-element.46), channel_id=1, source_target_pairs={{32,2},{34,0},{64,34},{66,32},{96,66},{98,64},{128,98},{130,96},{1... | collective-permute-start | bytes 1179656 | tf_op jit(solution)/shard_map/ppermute | solution.py:412
  109.4 13.3 %collective-permute-done.7.b = bf16[96,2048]{1,0:T(8,128)(2,1)S(1)} collective-permute-done((bf16[96,2048]{1,0:T(8,128)(2,1)S(1)}, bf16[96,2048]{1,0:T(8,128)(2,1)S(1)}, u32[]{:S(2)}, u32[]{:S(2)}) %collective-permute-start.7) | collective-permute-done | bytes 393248 | tf_op jit(solution)/shard_map/ppermute | solution.py:412
  122.7 4.5 %collective-permute-done.10.d = bf16[96,2048]{1,0:T(8,128)(2,1)S(1)} collective-permute-done((bf16[96,2048]{1,0:T(8,128)(2,1)S(1)}, bf16[96,2048]{1,0:T(8,128)(2,1)S(1)}, u32[]{:S(2)}, u32[]{:S(2)}) %collective-permute-start.10) | collective-permute-done | bytes 393248 | tf_op jit(solution)/shard_map/ppermute | solution.py:412
  127.4 2.1 %collective-permute-start.11 = (bf16[192,2048]{1,0:T(8,128)(2,1)S(1)}, bf16[192,2048]{1,0:T(8,128)(2,1)S(1)}, u32[]{:S(2)}, u32[]{:S(2)}) collective-permute-start(bf16[192,2048]{1,0:T(8,128)(2,1)S(1)} %shard_map.145.mine), channel_id=1, source_target_pairs={{0,1},{1,0},{2,3},{3,2},{4,5},{5,4},{6,7},{7,6},{8,9},{9,8},{10,11... | collective-permute-start | bytes 2359304 | tf_op jit(solution)/shard_map/ppermute | solution.py:339
  129.5 1.4 %shard_map.147 = (f32[384,128]{1,0:T(8,128)S(1)}, bf16[384,128]{1,0:T(8,128)(2,1)S(1)}) custom-call(s32[1]{0:T(128)} %bitcast.3.x_ref, bf16[8,2,384,128]{3,2,1,0:T(8,128)(2,1)} %all-to-all-done.received), custom_call_target="tpu_custom_call" | custom-call | bytes 1867780 | tf_op jit(solution)/shard_map/pallas_call | solution.py:31
  130.9 2.8 %collective-permute-start.12 = (bf16[384,128]{1,0:T(8,128)(2,1)S(1)}, bf16[384,128]{1,0:T(8,128)(2,1)S(1)}, u32[]{:S(2)}, u32[]{:S(2)}) collective-permute-start(bf16[384,128]{1,0:T(8,128)(2,1)S(1)} %get-tuple-element.51), channel_id=1, source_target_pairs={{0,2},{2,0},{1,3},{3,1},{4,6},{6,4},{5,7},{7,5},{8,10},{10,8},{9,1... | collective-permute-start | bytes 294920 | tf_op jit(solution)/shard_map/ppermute | solution.py:336
  133.8 1.2 shard_map.146
  135.0 4.6 %collective-permute-done.12.other_sum = bf16[384,128]{1,0:T(8,128)(2,1)S(1)} collective-permute-done((bf16[384,128]{1,0:T(8,128)(2,1)S(1)}, bf16[384,128]{1,0:T(8,128)(2,1)S(1)}, u32[]{:S(2)}, u32[]{:S(2)}) %collective-permute-start.12) | collective-permute-done | bytes 98336 | tf_op jit(solution)/shard_map/ppermute | solution.py:336
  139.6 1.2 shard_map.148
  (36 shorter events, 0.6 us)
Async XLA Ops:
  2.7 8.6 %collective-permute-start.1 = (bf16[128,384]{1,0:T(8,128)(2,1)S(1)}, bf16[128,384]{1,0:T(8,128)(2,1)S(1)}, u32[]{:S(2)}, u32[]{:S(2)}) collective-permute-start(bf16[128,384]{1,0:T(8,128)(2,1)S(1)} %get-tuple-element.29), channel_id=1, source_target_pairs={{0,2},{2,0},{1,3},{3,1},{4,6},{6,4},{5,7},{7,5},{8,10},{10,8},{9,1... | collective-permute-start | bytes 294920 | tf_op jit(solution)/shard_map/ppermute | solution.py:336
  8.0 32.3 %collective-permute-start = (bf16[192,2048]{1,0:T(8,128)(2,1)S(1)}, bf16[192,2048]{1,0:T(8,128)(2,1)S(1)}, u32[]{:S(2)}, u32[]{:S(2)}) collective-permute-start(bf16[192,2048]{1,0:T(8,128)(2,1)S(1)} %get-tuple-element.31), channel_id=1, source_target_pairs={{0,2},{2,0},{1,3},{3,1},{4,6},{6,4},{5,7},{7,5},{8,10},{10,8},{9,1... | collective-permute-start | bytes 2359304 | tf_op jit(solution)/shard_map/ppermute | solution.py:336
  40.3 2.3 %copy-start.3 = (bf16[192,2048]{1,0:T(8,128)(2,1)}, bf16[192,2048]{1,0:T(8,128)(2,1)S(1)}, u32[]{:S(2)}) copy-start(bf16[192,2048]{1,0:T(8,128)(2,1)S(1)} %collective-permute-done.near.x_near) | copy-start | bytes 2359300
  40.3 5.2 %copy-start.7 = (f32[1,2048]{1,0:T(1,128)S(1)}, f32[1,2048]{1,0:T(1,128)}, u32[]{:S(2)}) copy-start(f32[1,2048]{1,0:T(1,128)} %gain_ref.1) | copy-start | bytes 24580
  40.3 4.3 %collective-permute-start.4 = (bf16[192,2048]{1,0:T(8,128)(2,1)S(1)}, bf16[192,2048]{1,0:T(8,128)(2,1)S(1)}, u32[]{:S(2)}, u32[]{:S(2)}) collective-permute-start(bf16[192,2048]{1,0:T(8,128)(2,1)S(1)} %collective-permute-done.near.x_near), channel_id=1, source_target_pairs={{0,1},{1,0},{2,3},{3,2},{4,5},{5,4},{6,7},{7,6},{8,9},{9,8},{10,11... | collective-permute-start | bytes 2359304 | tf_op jit(solution)/shard_map/ppermute | solution.py:339
  44.6 0.9 copy-start.10
  53.0 76.5 %all-to-all-start = ((bf16[8,2,384,128]{3,2,1,0:T(8,128)(2,1)}), bf16[8,2,384,128]{3,2,1,0:T(8,128)(2,1)}, u32[]{:S(2)}, u32[]{:S(2)}) async-start(bf16[8,2,384,128]{3,2,1,0:T(8,128)(2,1)} %bitcast.33), calls=%async_computation | async-start | bytes 3145728 | tf_op jit(solution)/shard_map/all_to_all | solution.py:342
  60.0 14.0 %collective-permute-start.2 = (bf16[96,2048]{1,0:T(8,128)(2,1)S(1)}, bf16[96,2048]{1,0:T(8,128)(2,1)S(1)}, u32[]{:S(2)}, u32[]{:S(2)}) collective-permute-start(bf16[96,2048]{1,0:T(8,128)(2,1)S(1)} %get-tuple-element.34), channel_id=1, source_target_pairs={{0,2},{2,0},{1,3},{3,1},{4,6},{6,4},{5,7},{7,5},{8,10},{10,8},{9,1... | collective-permute-start | bytes 1179656 | tf_op jit(solution)/shard_map/ppermute | solution.py:336
  73.9 3.9 %copy-start.11 = (bf16[96,2048]{1,0:T(8,128)(2,1)}, bf16[96,2048]{1,0:T(8,128)(2,1)S(1)}, u32[]{:S(2)}) copy-start(bf16[96,2048]{1,0:T(8,128)(2,1)S(1)} %collective-permute-done.2.near) | copy-start | bytes 1179652
  73.9 3.9 %collective-permute-start.3 = (bf16[96,2048]{1,0:T(8,128)(2,1)S(1)}, bf16[96,2048]{1,0:T(8,128)(2,1)S(1)}, u32[]{:S(2)}, u32[]{:S(2)}) collective-permute-start(bf16[96,2048]{1,0:T(8,128)(2,1)S(1)} %collective-permute-done.2.near), channel_id=1, source_target_pairs={{0,1},{1,0},{2,3},{3,2},{4,5},{5,4},{6,7},{7,6},{8,9},{9,8},{10,11... | collective-permute-start | bytes 1179656 | tf_op jit(solution)/shard_map/ppermute | solution.py:339
  77.8 0.8 copy-start.12
  78.6 9.8 %copy-start = (bf16[1,192,2048]{2,1,0:T(8,128)(2,1)S(1)}, bf16[1,192,2048]{2,1,0:T(8,128)(2,1)}, u32[]{:S(2)}) copy-start(bf16[1,192,2048]{2,1,0:T(8,128)(2,1)} %param.11) | copy-start | bytes 2359300
  83.8 14.7 %copy-start.1 = (bf16[1,192,2048]{2,1,0:T(8,128)(2,1)S(1)}, bf16[1,192,2048]{2,1,0:T(8,128)(2,1)}, u32[]{:S(2)}) copy-start(bf16[1,192,2048]{2,1,0:T(8,128)(2,1)} %param.12) | copy-start | bytes 2359300
  83.9 14.7 %copy-start.2 = (bf16[1,192,2048]{2,1,0:T(8,128)(2,1)S(1)}, bf16[1,192,2048]{2,1,0:T(8,128)(2,1)}, u32[]{:S(2)}) copy-start(bf16[1,192,2048]{2,1,0:T(8,128)(2,1)} %param.13) | copy-start | bytes 2359300
  83.9 14.7 %copy-start.4 = (bf16[192,2048]{1,0:T(8,128)(2,1)S(1)}, bf16[192,2048]{1,0:T(8,128)(2,1)}, u32[]{:S(2)}) copy-start(bf16[192,2048]{1,0:T(8,128)(2,1)} %copy-done.3) | copy-start | bytes 2359300
  83.9 4.5 %collective-permute-start.5 = (bf16[192,2048]{1,0:T(8,128)(2,1)S(1)}, bf16[192,2048]{1,0:T(8,128)(2,1)S(1)}, u32[]{:S(2)}, u32[]{:S(2)}) collective-permute-start(bf16[192,2048]{1,0:T(8,128)(2,1)S(1)} %get-tuple-element.41), channel_id=1, source_target_pairs={{0,1},{1,0},{2,3},{3,2},{4,5},{5,4},{6,7},{7,6},{8,9},{9,8},{10,11... | collective-permute-start | bytes 2359304 | tf_op jit(solution)/shard_map/ppermute | solution.py:339
  86.4 12.1 %collective-permute-start.8 = (bf16[192,2048]{1,0:T(8,128)(2,1)S(1)}, bf16[192,2048]{1,0:T(8,128)(2,1)S(1)}, u32[]{:S(2)}, u32[]{:S(2)}) collective-permute-start(bf16[192,2048]{1,0:T(8,128)(2,1)S(1)} %get-tuple-element.38), channel_id=1, source_target_pairs={{0,1},{1,0},{2,3},{3,2},{4,5},{5,4},{6,7},{7,6},{8,9},{9,8},{10,11... | collective-permute-start | bytes 2359304 | tf_op jit(solution)/shard_map/ppermute | solution.py:339
  88.7 20.8 %collective-permute-start.6 = (bf16[96,2048]{1,0:T(8,128)(2,1)S(1)}, bf16[96,2048]{1,0:T(8,128)(2,1)S(1)}, u32[]{:S(2)}, u32[]{:S(2)}) collective-permute-start(bf16[96,2048]{1,0:T(8,128)(2,1)S(1)} %get-tuple-element.42), channel_id=1, source_target_pairs={{0,32},{2,34},{32,64},{34,66},{64,96},{66,98},{96,128},{98,130},{1... | collective-permute-start | bytes 1179656 | tf_op jit(solution)/shard_map/ppermute | solution.py:412
  93.0 29.8 %collective-permute-start.7 = (bf16[96,2048]{1,0:T(8,128)(2,1)S(1)}, bf16[96,2048]{1,0:T(8,128)(2,1)S(1)}, u32[]{:S(2)}, u32[]{:S(2)}) collective-permute-start(bf16[96,2048]{1,0:T(8,128)(2,1)S(1)} %get-tuple-element.43), channel_id=1, source_target_pairs={{0,34},{2,32},{32,66},{34,64},{64,98},{66,96},{96,130},{98,128},{1... | collective-permute-start | bytes 1179656 | tf_op jit(solution)/shard_map/ppermute | solution.py:412
  99.6 23.2 %collective-permute-start.9 = (bf16[96,2048]{1,0:T(8,128)(2,1)S(1)}, bf16[96,2048]{1,0:T(8,128)(2,1)S(1)}, u32[]{:S(2)}, u32[]{:S(2)}) collective-permute-start(bf16[96,2048]{1,0:T(8,128)(2,1)S(1)} %get-tuple-element.45), channel_id=1, source_target_pairs={{32,0},{34,2},{64,32},{66,34},{96,64},{98,66},{128,96},{130,98},{1... | collective-permute-start | bytes 1179656 | tf_op jit(solution)/shard_map/ppermute | solution.py:412
  104.3 22.9 %collective-permute-start.10 = (bf16[96,2048]{1,0:T(8,128)(2,1)S(1)}, bf16[96,2048]{1,0:T(8,128)(2,1)S(1)}, u32[]{:S(2)}, u32[]{:S(2)}) collective-permute-start(bf16[96,2048]{1,0:T(8,128)(2,1)S(1)} %get-tuple-element.46), channel_id=1, source_target_pairs={{32,2},{34,0},{64,34},{66,32},{96,66},{98,64},{128,98},{130,96},{1... | collective-permute-start | bytes 1179656 | tf_op jit(solution)/shard_map/ppermute | solution.py:412
  127.4 12.2 %copy-start.5 = (s32[1,2,128,256]{3,2,1,0:T(8,128)S(1)}, s32[1,2,128,256]{3,2,1,0:T(8,128)}, u32[]{:S(2)}) copy-start(s32[1,2,128,256]{3,2,1,0:T(8,128)} %param.17) | copy-start | bytes 786436
  127.4 12.2 %copy-start.6 = (s32[1,256,128]{2,1,0:T(8,128)S(1)}, s32[1,256,128]{2,1,0:T(8,128)}, u32[]{:S(2)}) copy-start(s32[1,256,128]{2,1,0:T(8,128)} %param.18) | copy-start | bytes 393220
  127.4 12.1 %copy-start.8 = (f32[1,2,2,128,1]{3,4,2,1,0:T(1,128)S(1)}, f32[1,2,2,128,1]{3,4,2,1,0:T(1,128)}, u32[]{:S(2)}) copy-start(f32[1,2,2,128,1]{3,4,2,1,0:T(1,128)} %param.19) | copy-start | bytes 6148
  127.4 12.1 %copy-start.9 = (f32[1,2,1,128]{3,2,1,0:T(1,128)S(1)}, f32[1,2,1,128]{3,2,1,0:T(1,128)}, u32[]{:S(2)}) copy-start(f32[1,2,1,128]{3,2,1,0:T(1,128)} %param.20) | copy-start | bytes 3076
  127.4 6.3 %collective-permute-start.11 = (bf16[192,2048]{1,0:T(8,128)(2,1)S(1)}, bf16[192,2048]{1,0:T(8,128)(2,1)S(1)}, u32[]{:S(2)}, u32[]{:S(2)}) collective-permute-start(bf16[192,2048]{1,0:T(8,128)(2,1)S(1)} %shard_map.145.mine), channel_id=1, source_target_pairs={{0,1},{1,0},{2,3},{3,2},{4,5},{5,4},{6,7},{7,6},{8,9},{9,8},{10,11... | collective-permute-start | bytes 2359304 | tf_op jit(solution)/shard_map/ppermute | solution.py:339
  130.9 8.6 %collective-permute-start.12 = (bf16[384,128]{1,0:T(8,128)(2,1)S(1)}, bf16[384,128]{1,0:T(8,128)(2,1)S(1)}, u32[]{:S(2)}, u32[]{:S(2)}) collective-permute-start(bf16[384,128]{1,0:T(8,128)(2,1)S(1)} %get-tuple-element.51), channel_id=1, source_target_pairs={{0,2},{2,0},{1,3},{3,1},{4,6},{6,4},{5,7},{7,5},{8,10},{10,8},{9,1... | collective-permute-start | bytes 294920 | tf_op jit(solution)/shard_map/ppermute | solution.py:336

commit v4 on v3

--- a/solution.py
+++ b/solution.py
@@ -244,22 +244,28 @@
     lax.fori_loop(0, 6, step, 0)
 
 
-def back_body(k_ref, gain_ref, x_own, x_near, dy, keep, recv, own_out, pair_out):
+def pair_body(keep, recv, out):
+    def step(i, carry):
+        rows = pl.ds(pl.multiple_of(i * 16, 16), 16)
+        out[rows, :] = total(keep, recv, 96 + i * 16).astype(BF16)
+        return carry
+
+    lax.fori_loop(0, 6, step, 0)
+
+
+def back_body(k_ref, gain_ref, x_own, dy, keep, recv, other, out):
     k = k_ref[0]
     gain = gain_ref[...]
-
-    def through_norm(x, e):
-        r = rms(x)
-        a = gain * e
-        return r * a - x * (r * r * r * jnp.mean(a * x, axis=-1, keepdims=True))
 
     def step(i, carry):
         r = i * 16
         rows = pl.ds(pl.multiple_of(r, 16), 16)
         mine = pl.ds(pl.multiple_of(k * 96 + r, 16), 16)
-        own = through_norm(x_own[mine, :].astype(F32), total(keep, recv, r))
-        own_out[rows, :] = (dy[mine, :].astype(F32) + own).astype(BF16)
-        pair_out[rows, :] = through_norm(x_near[rows, :].astype(F32), total(keep, recv, 96 + r)).astype(BF16)
+        x = x_own[mine, :].astype(F32)
+        inv = rms(x)
+        a = gain * (total(keep, recv, r) + other[rows, :].astype(F32))
+        through = inv * a - x * (inv * inv * inv * jnp.mean(a * x, axis=-1, keepdims=True))
+        out[rows, :] = (dy[mine, :].astype(F32) + through).astype(BF16)
         return carry
 
     lax.fori_loop(0, 6, step, 0)
@@ -277,9 +283,9 @@
         store.wait()
 
 
-def add_body(a, b, c, d, out):
+def add_body(a, b, c, out):
     out[0:96, :] = (a[...].astype(F32) + b[...].astype(F32)).astype(BF16)
-    out[96:192, :] = (c[...].astype(F32) + d[...].astype(F32)).astype(BF16)
+    out[96:192, :] = c[...]
 
 
 def stepped(m, root, grad):
@@ -380,7 +386,7 @@
             pltpu.VMEM((384, 2048), BF16),
             pltpu.VMEM((16, 384, 128), BF16), pltpu.SemaphoreType.DMA((6,)), pltpu.SemaphoreType.DMA((8,)),
         ],
-        flops=4 * 384 * 384 * 2048, n_smem=1, hbm_in=(2, 3, 4, 5), hbm_out=(0,),
+        flops=4 * 384 * 384 * 2048, n_smem=1, hbm_in=(2, 3, 4), hbm_out=(0,),
     )
     received = exchange(grads.reshape(8, 2, 384, 128), "y")
     own_sum, give = call(
@@ -398,22 +404,22 @@
             pltpu.VMEM((384, 256), F32), pltpu.VMEM((384, 128), BF16),
             pltpu.VMEM((384, 2048), BF16), pltpu.VMEM((384, 2048), BF16), pltpu.SemaphoreType.DMA((3,)),
         ],
-        flops=2 * 384 * 384 * 2048, n_smem=1, hbm_in=(2, 3, 4),
+        flops=2 * 384 * 384 * 2048, n_smem=1, hbm_in=(2,),
     )
     q_recv = on_chip(q_send)
     ahead = call(ahead_body, [piece, piece], [k_arr, x_f, q_keep, q_recv], n_smem=1)
-    back = call(back_body, [piece, piece], [k_arr, gain, x_b, near, dy, e_keep, e_recv], n_smem=1)
-
-    def relay(pieces, distance):
+    (e_pair,) = call(pair_body, [piece], [e_keep, e_recv])
+    e_other = across(e_pair)
+    (back,) = call(back_body, [piece], [k_arr, gain, x_b, dy, e_keep, e_recv, e_other], n_smem=1)
+
+    def relay(x, distance, turn):
         moves = [(s, s + distance) for s in range(sections) if 0 <= s + distance < sections]
-        same = [(2 * s + h, 2 * t + h) for s, t in moves for h in range(2)]
-        cross = [(2 * s + h, 2 * t + 1 - h) for s, t in moves for h in range(2)]
         axes = ("section", "xh")
-        return lax.ppermute(pieces[0], axes, same), lax.ppermute(pieces[1], axes, cross)
-
-    next_parts = relay(ahead, 1)
-    back_parts = relay(back, -1)
-    (joined,) = call(add_body, [part], [*next_parts, *back_parts])
+        return lax.ppermute(x, axes, [(2 * s + h, 2 * t + (h ^ turn)) for s, t in moves for h in range(2)])
+
+    next_parts = relay(ahead[0], 1, 0), relay(ahead[1], 1, 1)
+    back_part = relay(back, -1, 0)
+    (joined,) = call(add_body, [part], [*next_parts, back_part])
     next_rows, back_rows = call(
         rejoin_body, [part, part], [k_arr, joined, on_chip(joined)],
         scratch=[pltpu.SemaphoreType.DMA((4,))], n_smem=1, hbm_out=(0, 1),

time: 141 us -> 141 us (level)
  the two profiles are of different devices: /device:TPU:10 before, /device:TPU:1 now
where the time goes in v4:
time: 141 us; the launch traced here: 140 us
  starting transfers between devices  49.5 us (35%)
  waiting for transfers between devices  41.4 us (29%)
  blocking collectives  25.4 us (18%)
  Pallas kernels  22.2 us (16%)
  between operations  1.64 us (1%)
    ppermute x5, waiting for transfers between devices, across(): return lax.ppermute(x, 'xh', swap)  29.4 us
    all_gather x1, blocking collectives, tick(): gathered = lax.all_gather(rows, 'y', axis=0, tiled=True)  25.4 us
    ppermute x5, starting transfers between devices, on_chip(): return lax.ppermute(x, 'hid', swap)  23.2 us
    pallas_call x12, Pallas kernels, call(): pl.pallas_call(body, out_shape=tuple(((pltpu.HBM if i in hbm_out else jax...  22.2 us
    ppermute x5, starting transfers between devices, across(): return lax.ppermute(x, 'xh', swap)  13.3 us
    ppermute x3, waiting for transfers between devices, relay(): lax.ppermute(x, axes, [(2 * s + h, 2 * t + (h ^ turn)) for s, t in moves...  10.4 us
    ppermute x3, starting transfers between devices, relay(): lax.ppermute(x, axes, [(2 * s + h, 2 * t + (h ^ turn)) for s, t in moves...  8.69 us
    all_to_all x1, starting transfers between devices, exchange(): return lax.all_to_all(x, axes, 0, 0, tiled=True)  4.31 us
  transfers between devices with their start and end apart: 14, of which 5 were waited for; matrix products, arithmetic and copies ran while one was open for 0% of the time, Pallas kernels for 9%

profile of v4, /device:TPU:1, one launch (start us, length us, event | category | flops | bytes accessed | tf_op | source)
XLA Modules:
  0.0 140.4 jit_solution(2472065126980651211)
XLA Ops:
  1.3 1.4 %shard_map.138 = (bf16[128,384]{1,0:T(8,128)(2,1)S(1)}, bf16[128,384]{1,0:T(8,128)(2,1)S(1)}) custom-call(s32[1]{0:T(128)S(6)} %copy.15.lag_ref, s32[1]{0:T(128)} %bitcast.3.x_ref, f32[2,128,256]{2,1,0:T(8,128)} %bitcast.34, s32[2,128,256]{2,1,0:T(8,128)} %bitcast.25, f32[4,128]{1,0:T(4,128)} %bitcast.29, f32[256,128]{1,0:T(8,128)} %bitcast.35, ...), custom_call_target="tpu_custom_call" | custom-call | bytes 986120 | tf_op jit(solution)/shard_map/pallas_call | solution.py:31
  2.7 5.5 %collective-permute-start.1 = (bf16[128,384]{1,0:T(8,128)(2,1)S(1)}, bf16[128,384]{1,0:T(8,128)(2,1)S(1)}, u32[]{:S(2)}, u32[]{:S(2)}) collective-permute-start(bf16[128,384]{1,0:T(8,128)(2,1)S(1)} %get-tuple-element.27), channel_id=1, source_target_pairs={{0,2},{2,0},{1,3},{3,1},{4,6},{6,4},{5,7},{7,5},{8,10},{10,8},{9,1... | collective-permute-start | bytes 294920 | tf_op jit(solution)/shard_map/ppermute | solution.py:342
  8.2 1.3 shard_map.139
  9.5 1.9 %collective-permute-start = (bf16[192,2048]{1,0:T(8,128)(2,1)S(1)}, bf16[192,2048]{1,0:T(8,128)(2,1)S(1)}, u32[]{:S(2)}, u32[]{:S(2)}) collective-permute-start(bf16[192,2048]{1,0:T(8,128)(2,1)S(1)} %get-tuple-element.29), channel_id=1, source_target_pairs={{0,2},{2,0},{1,3},{3,1},{4,6},{6,4},{5,7},{7,5},{8,10},{10,8},{9,1... | collective-permute-start | bytes 2359304 | tf_op jit(solution)/shard_map/ppermute | solution.py:342
  11.5 25.4 %all-gather.1 = f16[2048,384]{1,0:T(8,128)(2,1)S(1)} all-gather(f16[256,384]{1,0:T(8,128)(2,1)S(1)} %fusion), channel_id=1, replica_groups=mesh['section'=16,'y'=8,'xh'=2,'hid'=2] {'y'}, dimensions={0}, use_global_device_ids=true | all-gather | bytes 1769472 | tf_op jit(solution)/shard_map/all_gather | solution.py:368
  36.8 12.0 %collective-permute-start.4 = (bf16[192,2048]{1,0:T(8,128)(2,1)S(1)}, bf16[192,2048]{1,0:T(8,128)(2,1)S(1)}, u32[]{:S(2)}, u32[]{:S(2)}) collective-permute-start(bf16[192,2048]{1,0:T(8,128)(2,1)S(1)} %collective-permute-done.near), channel_id=1, source_target_pairs={{0,1},{1,0},{2,3},{3,2},{4,5},{5,4},{6,7},{7,6},{8,9},{9,8},{10,11... | collective-permute-start | bytes 2359304 | tf_op jit(solution)/shard_map/ppermute | solution.py:345
  48.8 0.3 convert_element_type.7.w
  49.1 1.6 %collective-permute-done.4.far = bf16[192,2048]{1,0:T(8,128)(2,1)S(1)} collective-permute-done((bf16[192,2048]{1,0:T(8,128)(2,1)S(1)}, bf16[192,2048]{1,0:T(8,128)(2,1)S(1)}, u32[]{:S(2)}, u32[]{:S(2)}) %collective-permute-start.4) | collective-permute-done | bytes 786464 | tf_op jit(solution)/shard_map/ppermute | solution.py:345
  50.7 7.4 %shard_map.140 = (bf16[16,384,128]{2,1,0:T(8,128)(2,1)}, bf16[384,256]{1,0:T(8,128)(2,1)S(1)}) custom-call(s32[1]{0:T(128)} %bitcast.k_ref, f32[1,2048]{1,0:T(1,128)S(1)} %copy-done.5, bf16[192,2048]{1,0:T(8,128)(2,1)} %bitcast.20, bf16[192,2048]{1,0:T(8,128)(2,1)} %bitcast.23, bf16[192,2048]{1,0:T(8,128)(2,1)} %copy-done.8, ...), custom_call_target="tpu_custom_call" | custom-call | flops 1207959552 | bytes 6496260 | tf_op jit(solution)/shard_map/pallas_call | solution.py:31
  58.1 4.3 %all-to-all-start = ((bf16[8,2,384,128]{3,2,1,0:T(8,128)(2,1)}), bf16[8,2,384,128]{3,2,1,0:T(8,128)(2,1)}, u32[]{:S(2)}, u32[]{:S(2)}) async-start(bf16[8,2,384,128]{3,2,1,0:T(8,128)(2,1)} %bitcast.33), calls=%async_computation | async-start | bytes 3145728 | tf_op jit(solution)/shard_map/all_to_all | solution.py:348
  62.4 1.9 %collective-permute-start.2 = (bf16[96,2048]{1,0:T(8,128)(2,1)S(1)}, bf16[96,2048]{1,0:T(8,128)(2,1)S(1)}, u32[]{:S(2)}, u32[]{:S(2)}) collective-permute-start(bf16[96,2048]{1,0:T(8,128)(2,1)S(1)} %get-tuple-element.32), channel_id=1, source_target_pairs={{0,2},{2,0},{1,3},{3,1},{4,6},{6,4},{5,7},{7,5},{8,10},{10,8},{9,1... | collective-permute-start | bytes 1179656 | tf_op jit(solution)/shard_map/ppermute | solution.py:342
  64.4 11.9 %collective-permute-done.2.near = bf16[96,2048]{1,0:T(8,128)(2,1)S(1)} collective-permute-done((bf16[96,2048]{1,0:T(8,128)(2,1)S(1)}, bf16[96,2048]{1,0:T(8,128)(2,1)S(1)}, u32[]{:S(2)}, u32[]{:S(2)}) %collective-permute-start.2) | collective-permute-done | bytes 393248 | tf_op jit(solution)/shard_map/ppermute | solution.py:342
  76.2 3.0 %collective-permute-start.3 = (bf16[96,2048]{1,0:T(8,128)(2,1)S(1)}, bf16[96,2048]{1,0:T(8,128)(2,1)S(1)}, u32[]{:S(2)}, u32[]{:S(2)}) collective-permute-start(bf16[96,2048]{1,0:T(8,128)(2,1)S(1)} %collective-permute-done.2.near), channel_id=1, source_target_pairs={{0,1},{1,0},{2,3},{3,2},{4,5},{5,4},{6,7},{7,6},{8,9},{9,8},{10,11... | collective-permute-start | bytes 1179656 | tf_op jit(solution)/shard_map/ppermute | solution.py:345
  79.3 2.0 %shard_map.141 = (bf16[192,2048]{1,0:T(8,128)(2,1)S(1)}, bf16[192,2048]{1,0:T(8,128)(2,1)S(1)}) custom-call(bf16[384,256]{1,0:T(8,128)(2,1)S(1)} %get-tuple-element.35.dgu, bf16[2048,384]{1,0:T(8,128)(2,1)S(1)} %convert_element_type.7.w), custom_call_target="tpu_custom_call" | custom-call | flops 402653184 | bytes 3342336 | tf_op jit(solution)/shard_map/pallas_call | solution.py:31
  81.3 1.9 %collective-permute-start.8 = (bf16[192,2048]{1,0:T(8,128)(2,1)S(1)}, bf16[192,2048]{1,0:T(8,128)(2,1)S(1)}, u32[]{:S(2)}, u32[]{:S(2)}) collective-permute-start(bf16[192,2048]{1,0:T(8,128)(2,1)S(1)} %get-tuple-element.36), channel_id=1, source_target_pairs={{0,1},{1,0},{2,3},{3,2},{4,5},{5,4},{6,7},{7,6},{8,9},{9,8},{10,11... | collective-permute-start | bytes 2359304 | tf_op jit(solution)/shard_map/ppermute | solution.py:345
  83.2 4.9 %shard_map.142 = (bf16[192,2048]{1,0:T(8,128)(2,1)S(1)}, bf16[192,2048]{1,0:T(8,128)(2,1)S(1)}) custom-call(s32[1]{0:T(128)} %bitcast.k_ref, f32[1,2048]{1,0:T(1,128)S(1)} %copy-done.5, bf16[192,2048]{1,0:T(8,128)(2,1)} %bitcast.17, bf16[96,2048]{1,0:T(8,128)(2,1)S(1)} %collective-permute-done.2.near, bf16[96,2048]{1,0:T(8,128)(2,1)S(1)} %collective-permute-done.3.far, ...), custom_call_target="tpu_custom_call" | custom-call | flops 603979776 | bytes 4726788 | tf_op jit(solution)/shard_map/pallas_call | solution.py:31
  88.2 2.6 %collective-permute-start.5 = (bf16[192,2048]{1,0:T(8,128)(2,1)S(1)}, bf16[192,2048]{1,0:T(8,128)(2,1)S(1)}, u32[]{:S(2)}, u32[]{:S(2)}) collective-permute-start(bf16[192,2048]{1,0:T(8,128)(2,1)S(1)} %get-tuple-element.39), channel_id=1, source_target_pairs={{0,1},{1,0},{2,3},{3,2},{4,5},{5,4},{6,7},{7,6},{8,9},{9,8},{10,11... | collective-permute-start | bytes 2359304 | tf_op jit(solution)/shard_map/ppermute | solution.py:345
  90.7 0.1 shard_map.144
  90.9 2.1 %collective-permute-start.9 = (bf16[96,2048]{1,0:T(8,128)(2,1)S(1)}, bf16[96,2048]{1,0:T(8,128)(2,1)S(1)}, u32[]{:S(2)}, u32[]{:S(2)}) collective-permute-start(bf16[96,2048]{1,0:T(8,128)(2,1)S(1)} %shard_map.144), channel_id=1, source_target_pairs={{0,2},{2,0},{1,3},{3,1},{4,6},{6,4},{5,7},{7,5},{8,10},{10,8},{9,1... | collective-permute-start | bytes 1179656 | tf_op jit(solution)/shard_map/ppermute | solution.py:342
  93.0 0.3 shard_map.143
  93.3 3.7 %collective-permute-start.6 = (bf16[96,2048]{1,0:T(8,128)(2,1)S(1)}, bf16[96,2048]{1,0:T(8,128)(2,1)S(1)}, u32[]{:S(2)}, u32[]{:S(2)}) collective-permute-start(bf16[96,2048]{1,0:T(8,128)(2,1)S(1)} %get-tuple-element.40), channel_id=1, source_target_pairs={{0,32},{2,34},{32,64},{34,66},{64,96},{66,98},{96,128},{98,130},{1... | collective-permute-start | bytes 1179656 | tf_op jit(solution)/shard_map/ppermute | solution.py:418
  96.9 3.7 %collective-permute-start.7 = (bf16[96,2048]{1,0:T(8,128)(2,1)S(1)}, bf16[96,2048]{1,0:T(8,128)(2,1)S(1)}, u32[]{:S(2)}, u32[]{:S(2)}) collective-permute-start(bf16[96,2048]{1,0:T(8,128)(2,1)S(1)} %get-tuple-element.41), channel_id=1, source_target_pairs={{0,34},{2,32},{32,66},{34,64},{64,98},{66,96},{96,130},{98,128},{1... | collective-permute-start | bytes 1179656 | tf_op jit(solution)/shard_map/ppermute | solution.py:418
  100.7 12.8 %collective-permute-done.9.other = bf16[96,2048]{1,0:T(8,128)(2,1)S(1)} collective-permute-done((bf16[96,2048]{1,0:T(8,128)(2,1)S(1)}, bf16[96,2048]{1,0:T(8,128)(2,1)S(1)}, u32[]{:S(2)}, u32[]{:S(2)}) %collective-permute-start.9) | collective-permute-done | bytes 393248 | tf_op jit(solution)/shard_map/ppermute | solution.py:342
  113.5 0.9 shard_map.145
  114.4 1.3 collective-permute-start.10
  115.7 10.4 %collective-permute-done.10.c = bf16[96,2048]{1,0:T(8,128)(2,1)S(1)} collective-permute-done((bf16[96,2048]{1,0:T(8,128)(2,1)S(1)}, bf16[96,2048]{1,0:T(8,128)(2,1)S(1)}, u32[]{:S(2)}, u32[]{:S(2)}) %collective-permute-start.10) | collective-permute-done | bytes 393248 | tf_op jit(solution)/shard_map/ppermute | solution.py:418
  126.3 3.8 %collective-permute-start.11 = (bf16[192,2048]{1,0:T(8,128)(2,1)S(1)}, bf16[192,2048]{1,0:T(8,128)(2,1)S(1)}, u32[]{:S(2)}, u32[]{:S(2)}) collective-permute-start(bf16[192,2048]{1,0:T(8,128)(2,1)S(1)} %shard_map.146.mine), channel_id=1, source_target_pairs={{0,1},{1,0},{2,3},{3,2},{4,5},{5,4},{6,7},{7,6},{8,9},{9,8},{10,11... | collective-permute-start | bytes 2359304 | tf_op jit(solution)/shard_map/ppermute | solution.py:345
  130.0 1.4 %shard_map.148 = (f32[384,128]{1,0:T(8,128)S(1)}, bf16[384,128]{1,0:T(8,128)(2,1)S(1)}) custom-call(s32[1]{0:T(128)} %bitcast.3.x_ref, bf16[8,2,384,128]{3,2,1,0:T(8,128)(2,1)} %all-to-all-done.received), custom_call_target="tpu_custom_call" | custom-call | bytes 1867780 | tf_op jit(solution)/shard_map/pallas_call | solution.py:31
  131.5 1.9 %collective-permute-start.12 = (bf16[384,128]{1,0:T(8,128)(2,1)S(1)}, bf16[384,128]{1,0:T(8,128)(2,1)S(1)}, u32[]{:S(2)}, u32[]{:S(2)}) collective-permute-start(bf16[384,128]{1,0:T(8,128)(2,1)S(1)} %get-tuple-element.47), channel_id=1, source_target_pairs={{0,2},{2,0},{1,3},{3,1},{4,6},{6,4},{5,7},{7,5},{8,10},{10,8},{9,1... | collective-permute-start | bytes 294920 | tf_op jit(solution)/shard_map/ppermute | solution.py:342
  133.4 1.2 shard_map.147
  134.6 4.6 %collective-permute-done.12.other_sum = bf16[384,128]{1,0:T(8,128)(2,1)S(1)} collective-permute-done((bf16[384,128]{1,0:T(8,128)(2,1)S(1)}, bf16[384,128]{1,0:T(8,128)(2,1)S(1)}, u32[]{:S(2)}, u32[]{:S(2)}) %collective-permute-start.12) | collective-permute-done | bytes 98336 | tf_op jit(solution)/shard_map/ppermute | solution.py:342
  139.3 1.2 shard_map.149
  (29 shorter events, 0.2 us)
Async XLA Ops:
  2.7 8.7 %collective-permute-start.1 = (bf16[128,384]{1,0:T(8,128)(2,1)S(1)}, bf16[128,384]{1,0:T(8,128)(2,1)S(1)}, u32[]{:S(2)}, u32[]{:S(2)}) collective-permute-start(bf16[128,384]{1,0:T(8,128)(2,1)S(1)} %get-tuple-element.27), channel_id=1, source_target_pairs={{0,2},{2,0},{1,3},{3,1},{4,6},{6,4},{5,7},{7,5},{8,10},{10,8},{9,1... | collective-permute-start | bytes 294920 | tf_op jit(solution)/shard_map/ppermute | solution.py:342
  9.5 27.4 %collective-permute-start = (bf16[192,2048]{1,0:T(8,128)(2,1)S(1)}, bf16[192,2048]{1,0:T(8,128)(2,1)S(1)}, u32[]{:S(2)}, u32[]{:S(2)}) collective-permute-start(bf16[192,2048]{1,0:T(8,128)(2,1)S(1)} %get-tuple-element.29), channel_id=1, source_target_pairs={{0,2},{2,0},{1,3},{3,1},{4,6},{6,4},{5,7},{7,5},{8,10},{10,8},{9,1... | collective-permute-start | bytes 2359304 | tf_op jit(solution)/shard_map/ppermute | solution.py:342
  36.8 12.3 %copy-start.8 = (bf16[192,2048]{1,0:T(8,128)(2,1)}, bf16[192,2048]{1,0:T(8,128)(2,1)S(1)}, u32[]{:S(2)}) copy-start(bf16[192,2048]{1,0:T(8,128)(2,1)S(1)} %collective-permute-done.near) | copy-start | bytes 2359300
  36.8 13.9 %copy-start.5 = (f32[1,2048]{1,0:T(1,128)S(1)}, f32[1,2048]{1,0:T(1,128)}, u32[]{:S(2)}) copy-start(f32[1,2048]{1,0:T(1,128)} %gain_ref.1) | copy-start | bytes 24580
  36.8 13.9 %collective-permute-start.4 = (bf16[192,2048]{1,0:T(8,128)(2,1)S(1)}, bf16[192,2048]{1,0:T(8,128)(2,1)S(1)}, u32[]{:S(2)}, u32[]{:S(2)}) collective-permute-start(bf16[192,2048]{1,0:T(8,128)(2,1)S(1)} %collective-permute-done.near), channel_id=1, source_target_pairs={{0,1},{1,0},{2,3},{3,2},{4,5},{5,4},{6,7},{7,6},{8,9},{9,8},{10,11... | collective-permute-start | bytes 2359304 | tf_op jit(solution)/shard_map/ppermute | solution.py:345
  58.1 71.9 %all-to-all-start = ((bf16[8,2,384,128]{3,2,1,0:T(8,128)(2,1)}), bf16[8,2,384,128]{3,2,1,0:T(8,128)(2,1)}, u32[]{:S(2)}, u32[]{:S(2)}) async-start(bf16[8,2,384,128]{3,2,1,0:T(8,128)(2,1)} %bitcast.33), calls=%async_computation | async-start | bytes 3145728 | tf_op jit(solution)/shard_map/all_to_all | solution.py:348
  62.4 13.8 %collective-permute-start.2 = (bf16[96,2048]{1,0:T(8,128)(2,1)S(1)}, bf16[96,2048]{1,0:T(8,128)(2,1)S(1)}, u32[]{:S(2)}, u32[]{:S(2)}) collective-permute-start(bf16[96,2048]{1,0:T(8,128)(2,1)S(1)} %get-tuple-element.32), channel_id=1, source_target_pairs={{0,2},{2,0},{1,3},{3,1},{4,6},{6,4},{5,7},{7,5},{8,10},{10,8},{9,1... | collective-permute-start | bytes 1179656 | tf_op jit(solution)/shard_map/ppermute | solution.py:342
  76.2 6.9 %collective-permute-start.3 = (bf16[96,2048]{1,0:T(8,128)(2,1)S(1)}, bf16[96,2048]{1,0:T(8,128)(2,1)S(1)}, u32[]{:S(2)}, u32[]{:S(2)}) collective-permute-start(bf16[96,2048]{1,0:T(8,128)(2,1)S(1)} %collective-permute-done.2.near), channel_id=1, source_target_pairs={{0,1},{1,0},{2,3},{3,2},{4,5},{5,4},{6,7},{7,6},{8,9},{9,8},{10,11... | collective-permute-start | bytes 1179656 | tf_op jit(solution)/shard_map/ppermute | solution.py:345
  81.3 9.5 %collective-permute-start.8 = (bf16[192,2048]{1,0:T(8,128)(2,1)S(1)}, bf16[192,2048]{1,0:T(8,128)(2,1)S(1)}, u32[]{:S(2)}, u32[]{:S(2)}) collective-permute-start(bf16[192,2048]{1,0:T(8,128)(2,1)S(1)} %get-tuple-element.36), channel_id=1, source_target_pairs={{0,1},{1,0},{2,3},{3,2},{4,5},{5,4},{6,7},{7,6},{8,9},{9,8},{10,11... | collective-permute-start | bytes 2359304 | tf_op jit(solution)/shard_map/ppermute | solution.py:345
  88.1 4.8 %copy-start = (bf16[1,192,2048]{2,1,0:T(8,128)(2,1)S(1)}, bf16[1,192,2048]{2,1,0:T(8,128)(2,1)}, u32[]{:S(2)}) copy-start(bf16[1,192,2048]{2,1,0:T(8,128)(2,1)} %param.11) | copy-start | bytes 2359300
  88.2 4.8 %collective-permute-start.5 = (bf16[192,2048]{1,0:T(8,128)(2,1)S(1)}, bf16[192,2048]{1,0:T(8,128)(2,1)S(1)}, u32[]{:S(2)}, u32[]{:S(2)}) collective-permute-start(bf16[192,2048]{1,0:T(8,128)(2,1)S(1)} %get-tuple-element.39), channel_id=1, source_target_pairs={{0,1},{1,0},{2,3},{3,2},{4,5},{5,4},{6,7},{7,6},{8,9},{9,8},{10,11... | collective-permute-start | bytes 2359304 | tf_op jit(solution)/shard_map/ppermute | solution.py:345
  90.9 22.6 %copy-start.1 = (bf16[1,192,2048]{2,1,0:T(8,128)(2,1)S(1)}, bf16[1,192,2048]{2,1,0:T(8,128)(2,1)}, u32[]{:S(2)}) copy-start(bf16[1,192,2048]{2,1,0:T(8,128)(2,1)} %param.12) | copy-start | bytes 2359300
  90.9 22.6 %copy-start.2 = (bf16[1,192,2048]{2,1,0:T(8,128)(2,1)S(1)}, bf16[1,192,2048]{2,1,0:T(8,128)(2,1)}, u32[]{:S(2)}) copy-start(bf16[1,192,2048]{2,1,0:T(8,128)(2,1)} %param.13) | copy-start | bytes 2359300
  90.9 22.6 %collective-permute-start.9 = (bf16[96,2048]{1,0:T(8,128)(2,1)S(1)}, bf16[96,2048]{1,0:T(8,128)(2,1)S(1)}, u32[]{:S(2)}, u32[]{:S(2)}) collective-permute-start(bf16[96,2048]{1,0:T(8,128)(2,1)S(1)} %shard_map.144), channel_id=1, source_target_pairs={{0,2},{2,0},{1,3},{3,1},{4,6},{6,4},{5,7},{7,5},{8,10},{10,8},{9,1... | collective-permute-start | bytes 1179656 | tf_op jit(solution)/shard_map/ppermute | solution.py:342
  93.3 22.5 %collective-permute-start.6 = (bf16[96,2048]{1,0:T(8,128)(2,1)S(1)}, bf16[96,2048]{1,0:T(8,128)(2,1)S(1)}, u32[]{:S(2)}, u32[]{:S(2)}) collective-permute-start(bf16[96,2048]{1,0:T(8,128)(2,1)S(1)} %get-tuple-element.40), channel_id=1, source_target_pairs={{0,32},{2,34},{32,64},{34,66},{64,96},{66,98},{96,128},{98,130},{1... | collective-permute-start | bytes 1179656 | tf_op jit(solution)/shard_map/ppermute | solution.py:418
  96.9 18.8 %collective-permute-start.7 = (bf16[96,2048]{1,0:T(8,128)(2,1)S(1)}, bf16[96,2048]{1,0:T(8,128)(2,1)S(1)}, u32[]{:S(2)}, u32[]{:S(2)}) collective-permute-start(bf16[96,2048]{1,0:T(8,128)(2,1)S(1)} %get-tuple-element.41), channel_id=1, source_target_pairs={{0,34},{2,32},{32,66},{34,64},{64,98},{66,96},{96,130},{98,128},{1... | collective-permute-start | bytes 1179656 | tf_op jit(solution)/shard_map/ppermute | solution.py:418
  114.4 11.7 %collective-permute-start.10 = (bf16[96,2048]{1,0:T(8,128)(2,1)S(1)}, bf16[96,2048]{1,0:T(8,128)(2,1)S(1)}, u32[]{:S(2)}, u32[]{:S(2)}) collective-permute-start(bf16[96,2048]{1,0:T(8,128)(2,1)S(1)} %shard_map.145), channel_id=1, source_target_pairs={{32,0},{34,2},{64,32},{66,34},{96,64},{98,66},{128,96},{130,98},{1... | collective-permute-start | bytes 1179656 | tf_op jit(solution)/shard_map/ppermute | solution.py:418
  126.2 13.0 %copy-start.3 = (s32[1,2,128,256]{3,2,1,0:T(8,128)S(1)}, s32[1,2,128,256]{3,2,1,0:T(8,128)}, u32[]{:S(2)}) copy-start(s32[1,2,128,256]{3,2,1,0:T(8,128)} %param.17) | copy-start | bytes 786436
  126.2 13.0 %copy-start.4 = (s32[1,256,128]{2,1,0:T(8,128)S(1)}, s32[1,256,128]{2,1,0:T(8,128)}, u32[]{:S(2)}) copy-start(s32[1,256,128]{2,1,0:T(8,128)} %param.18) | copy-start | bytes 393220
  126.2 13.0 %copy-start.6 = (f32[1,2,2,128,1]{3,4,2,1,0:T(1,128)S(1)}, f32[1,2,2,128,1]{3,4,2,1,0:T(1,128)}, u32[]{:S(2)}) copy-start(f32[1,2,2,128,1]{3,4,2,1,0:T(1,128)} %param.19) | copy-start | bytes 6148
  126.2 13.0 %copy-start.7 = (f32[1,2,1,128]{3,2,1,0:T(1,128)S(1)}, f32[1,2,1,128]{3,2,1,0:T(1,128)}, u32[]{:S(2)}) copy-start(f32[1,2,1,128]{3,2,1,0:T(1,128)} %param.20) | copy-start | bytes 3076
  126.3 7.2 %collective-permute-start.11 = (bf16[192,2048]{1,0:T(8,128)(2,1)S(1)}, bf16[192,2048]{1,0:T(8,128)(2,1)S(1)}, u32[]{:S(2)}, u32[]{:S(2)}) collective-permute-start(bf16[192,2048]{1,0:T(8,128)(2,1)S(1)} %shard_map.146.mine), channel_id=1, source_target_pairs={{0,1},{1,0},{2,3},{3,2},{4,5},{5,4},{6,7},{7,6},{8,9},{9,8},{10,11... | collective-permute-start | bytes 2359304 | tf_op jit(solution)/shard_map/ppermute | solution.py:345
  131.5 7.7 %collective-permute-start.12 = (bf16[384,128]{1,0:T(8,128)(2,1)S(1)}, bf16[384,128]{1,0:T(8,128)(2,1)S(1)}, u32[]{:S(2)}, u32[]{:S(2)}) collective-permute-start(bf16[384,128]{1,0:T(8,128)(2,1)S(1)} %get-tuple-element.47), channel_id=1, source_target_pairs={{0,2},{2,0},{1,3},{3,1},{4,6},{6,4},{5,7},{7,5},{8,10},{10,8},{9,1... | collective-permute-start | bytes 294920 | tf_op jit(solution)/shard_map/ppermute | solution.py:342

commit v5 on v4

--- a/solution.py
+++ b/solution.py
@@ -135,24 +135,11 @@
     for load in x_loads:
         load.wait()
     norm_rows(gain, x, nb)
-    gu_acc[...] = jnp.zeros_like(gu_acc)
-    dh_acc[...] = jnp.zeros_like(dh_acc)
-
-    def contract(j, carry):
-        d = pl.ds(pl.multiple_of(j * 512, 512), 512)
-        gu_acc[...] += jnp.dot(nb[:, d], w[d, 0:256], preferred_element_type=F32)
-        return carry
-
-    lax.fori_loop(0, 4, contract, 0)
+    gu_acc[...] = jnp.dot(nb[...], w[:, 0:256], preferred_element_type=F32)
     for load in y_loads:
         load.wait()
 
-    def contract_dy(j, carry):
-        d = pl.ds(pl.multiple_of(j * 512, 512), 512)
-        dh_acc[...] += jnp.dot(dy[:, d], w[d, 256:384], preferred_element_type=F32)
-        return carry
-
-    lax.fori_loop(0, 4, contract_dy, 0)
+    dh_acc[...] = jnp.dot(dy[...], w[:, 256:384], preferred_element_type=F32)
     for b in range(3):
         rows = slice(b * 128, b * 128 + 128)
         g, u, dh = gu_acc[rows, 0:128], gu_acc[rows, 128:256], dh_acc[rows, :]
@@ -178,7 +165,7 @@
         pltpu.make_async_copy(out.at[pair], grads.at[pair], sem.at[j]).start()
         return carry
 
-    lax.fori_loop(0, 8, expand, 0)
+    lax.fori_loop(0, 8, expand, 0, unroll=4)
     for at, start in blocks(k_ref[0]):
         dgu[at : at + 96, :] = gu_acc[pl.ds(start, 96), :].astype(BF16)
     for j in range(8):
@@ -196,7 +183,7 @@
         send[96:192, d] = r[288:384]
         return carry
 
-    lax.fori_loop(0, 8, step, 0)
+    lax.fori_loop(0, 8, step, 0, unroll=4)
 
 
 def cotangent_body(dgu, w, keep, send):
@@ -210,14 +197,7 @@
     for load in loads:
         load.wait()
     norm_rows(gain, x, nf)
-    gu_acc[...] = jnp.zeros_like(gu_acc)
-
-    def contract(j, carry):
-        d = pl.ds(pl.multiple_of(j * 512, 512), 512)
-        gu_acc[...] += jnp.dot(nf[:, d], w[d, 0:256], preferred_element_type=F32)
-        return carry
-
-    lax.fori_loop(0, 4, contract, 0)
+    gu_acc[...] = jnp.dot(nf[...], w[:, 0:256], preferred_element_type=F32)
     for at, start in blocks(k_ref[0]):
         rows = pl.ds(start, 96)
         g, u = gu_acc[rows, 0:128], gu_acc[rows, 128:256]

time: 141 us -> 137 us (0.972)
  Pallas kernels: 22.2 us -> 18.3 us
    pallas_call x12, Pallas kernels: 22.2 us -> 18.3 us  [call(): pl.pallas_call(body, out_shape=tuple(((pltpu.HBM if i in hbm_out else jax...]
  transfers between devices with their start and end apart: 14 -> 14, of which waited for: 5 -> 5; matrix products, arithmetic and copies ran while one was open for 0% -> 0% of each run, Pallas kernels for 9% -> 7%
where the time goes in v5:
time: 137 us
  starting transfers between devices  49.5 us (36%)
  waiting for transfers between devices  41.3 us (30%)
  blocking collectives  25.4 us (19%)
  Pallas kernels  18.3 us (13%)
  between operations  1.65 us (1%)
    ppermute x5, waiting for transfers between devices, across(): return lax.ppermute(x, 'xh', swap)  29.3 us
    all_gather x1, blocking collectives, tick(): gathered = lax.all_gather(rows, 'y', axis=0, tiled=True)  25.4 us
    ppermute x5, starting transfers between devices, on_chip(): return lax.ppermute(x, 'hid', swap)  23.2 us
    pallas_call x12, Pallas kernels, call(): pl.pallas_call(body, out_shape=tuple(((pltpu.HBM if i in hbm_out else jax...  18.3 us
    ppermute x5, starting transfers between devices, across(): return lax.ppermute(x, 'xh', swap)  13.3 us
    ppermute x3, waiting for transfers between devices, relay(): lax.ppermute(x, axes, [(2 * s + h, 2 * t + (h ^ turn)) for s, t in moves...  10.4 us
    ppermute x3, starting transfers between devices, relay(): lax.ppermute(x, axes, [(2 * s + h, 2 * t + (h ^ turn)) for s, t in moves...  8.71 us
    all_to_all x1, starting transfers between devices, exchange(): return lax.all_to_all(x, axes, 0, 0, tiled=True)  4.31 us
  transfers between devices with their start and end apart: 14, of which 5 were waited for; matrix products, arithmetic and copies ran while one was open for 0% of the time, Pallas kernels for 7%

profile of v5, /device:TPU:1, one launch (start us, length us, event | category | flops | bytes accessed | tf_op | source)
XLA Modules:
  0.0 136.6 jit_solution(10372080934368041990)
XLA Ops:
  1.3 1.4 %shard_map.138 = (bf16[128,384]{1,0:T(8,128)(2,1)S(1)}, bf16[128,384]{1,0:T(8,128)(2,1)S(1)}) custom-call(s32[1]{0:T(128)S(6)} %copy.15.lag_ref, s32[1]{0:T(128)} %bitcast.3.x_ref, f32[2,128,256]{2,1,0:T(8,128)} %bitcast.34, s32[2,128,256]{2,1,0:T(8,128)} %bitcast.25, f32[4,128]{1,0:T(4,128)} %bitcast.29, f32[256,128]{1,0:T(8,128)} %bitcast.35, ...), custom_call_target="tpu_custom_call" | custom-call | bytes 986120 | tf_op jit(solution)/shard_map/pallas_call | solution.py:31
  2.7 5.5 %collective-permute-start.1 = (bf16[128,384]{1,0:T(8,128)(2,1)S(1)}, bf16[128,384]{1,0:T(8,128)(2,1)S(1)}, u32[]{:S(2)}, u32[]{:S(2)}) collective-permute-start(bf16[128,384]{1,0:T(8,128)(2,1)S(1)} %get-tuple-element.27), channel_id=1, source_target_pairs={{0,2},{2,0},{1,3},{3,1},{4,6},{6,4},{5,7},{7,5},{8,10},{10,8},{9,1... | collective-permute-start | bytes 294920 | tf_op jit(solution)/shard_map/ppermute | solution.py:322
  8.2 1.3 shard_map.139
  9.5 1.9 %collective-permute-start = (bf16[192,2048]{1,0:T(8,128)(2,1)S(1)}, bf16[192,2048]{1,0:T(8,128)(2,1)S(1)}, u32[]{:S(2)}, u32[]{:S(2)}) collective-permute-start(bf16[192,2048]{1,0:T(8,128)(2,1)S(1)} %get-tuple-element.29), channel_id=1, source_target_pairs={{0,2},{2,0},{1,3},{3,1},{4,6},{6,4},{5,7},{7,5},{8,10},{10,8},{9,1... | collective-permute-start | bytes 2359304 | tf_op jit(solution)/shard_map/ppermute | solution.py:322
  11.5 25.4 %all-gather.1 = f16[2048,384]{1,0:T(8,128)(2,1)S(1)} all-gather(f16[256,384]{1,0:T(8,128)(2,1)S(1)} %fusion), channel_id=1, replica_groups=mesh['section'=16,'y'=8,'xh'=2,'hid'=2] {'y'}, dimensions={0}, use_global_device_ids=true | all-gather | bytes 1769472 | tf_op jit(solution)/shard_map/all_gather | solution.py:348
  36.8 12.0 %collective-permute-start.4 = (bf16[192,2048]{1,0:T(8,128)(2,1)S(1)}, bf16[192,2048]{1,0:T(8,128)(2,1)S(1)}, u32[]{:S(2)}, u32[]{:S(2)}) collective-permute-start(bf16[192,2048]{1,0:T(8,128)(2,1)S(1)} %collective-permute-done.near), channel_id=1, source_target_pairs={{0,1},{1,0},{2,3},{3,2},{4,5},{5,4},{6,7},{7,6},{8,9},{9,8},{10,11... | collective-permute-start | bytes 2359304 | tf_op jit(solution)/shard_map/ppermute | solution.py:325
  48.8 0.3 convert_element_type.7.w
  49.1 1.6 %collective-permute-done.4.far = bf16[192,2048]{1,0:T(8,128)(2,1)S(1)} collective-permute-done((bf16[192,2048]{1,0:T(8,128)(2,1)S(1)}, bf16[192,2048]{1,0:T(8,128)(2,1)S(1)}, u32[]{:S(2)}, u32[]{:S(2)}) %collective-permute-start.4) | collective-permute-done | bytes 786464 | tf_op jit(solution)/shard_map/ppermute | solution.py:325
  50.7 6.2 %shard_map.140 = (bf16[16,384,128]{2,1,0:T(8,128)(2,1)}, bf16[384,256]{1,0:T(8,128)(2,1)S(1)}) custom-call(s32[1]{0:T(128)} %bitcast.k_ref, f32[1,2048]{1,0:T(1,128)S(1)} %copy-done.5, bf16[192,2048]{1,0:T(8,128)(2,1)} %bitcast.20, bf16[192,2048]{1,0:T(8,128)(2,1)} %bitcast.23, bf16[192,2048]{1,0:T(8,128)(2,1)} %copy-done.8, ...), custom_call_target="tpu_custom_call" | custom-call | flops 1207959552 | bytes 6496260 | tf_op jit(solution)/shard_map/pallas_call | solution.py:31
  56.9 4.3 %all-to-all-start = ((bf16[8,2,384,128]{3,2,1,0:T(8,128)(2,1)}), bf16[8,2,384,128]{3,2,1,0:T(8,128)(2,1)}, u32[]{:S(2)}, u32[]{:S(2)}) async-start(bf16[8,2,384,128]{3,2,1,0:T(8,128)(2,1)} %bitcast.33), calls=%async_computation | async-start | bytes 3145728 | tf_op jit(solution)/shard_map/all_to_all | solution.py:328
  61.2 1.9 %collective-permute-start.2 = (bf16[96,2048]{1,0:T(8,128)(2,1)S(1)}, bf16[96,2048]{1,0:T(8,128)(2,1)S(1)}, u32[]{:S(2)}, u32[]{:S(2)}) collective-permute-start(bf16[96,2048]{1,0:T(8,128)(2,1)S(1)} %get-tuple-element.32), channel_id=1, source_target_pairs={{0,2},{2,0},{1,3},{3,1},{4,6},{6,4},{5,7},{7,5},{8,10},{10,8},{9,1... | collective-permute-start | bytes 1179656 | tf_op jit(solution)/shard_map/ppermute | solution.py:322
  63.1 11.9 %collective-permute-done.2.near = bf16[96,2048]{1,0:T(8,128)(2,1)S(1)} collective-permute-done((bf16[96,2048]{1,0:T(8,128)(2,1)S(1)}, bf16[96,2048]{1,0:T(8,128)(2,1)S(1)}, u32[]{:S(2)}, u32[]{:S(2)}) %collective-permute-start.2) | collective-permute-done | bytes 393248 | tf_op jit(solution)/shard_map/ppermute | solution.py:322
  75.0 3.0 %collective-permute-start.3 = (bf16[96,2048]{1,0:T(8,128)(2,1)S(1)}, bf16[96,2048]{1,0:T(8,128)(2,1)S(1)}, u32[]{:S(2)}, u32[]{:S(2)}) collective-permute-start(bf16[96,2048]{1,0:T(8,128)(2,1)S(1)} %collective-permute-done.2.near), channel_id=1, source_target_pairs={{0,1},{1,0},{2,3},{3,2},{4,5},{5,4},{6,7},{7,6},{8,9},{9,8},{10,11... | collective-permute-start | bytes 1179656 | tf_op jit(solution)/shard_map/ppermute | solution.py:325
  78.0 0.8 shard_map.141
  78.9 1.9 %collective-permute-start.8 = (bf16[192,2048]{1,0:T(8,128)(2,1)S(1)}, bf16[192,2048]{1,0:T(8,128)(2,1)S(1)}, u32[]{:S(2)}, u32[]{:S(2)}) collective-permute-start(bf16[192,2048]{1,0:T(8,128)(2,1)S(1)} %get-tuple-element.36), channel_id=1, source_target_pairs={{0,1},{1,0},{2,3},{3,2},{4,5},{5,4},{6,7},{7,6},{8,9},{9,8},{10,11... | collective-permute-start | bytes 2359304 | tf_op jit(solution)/shard_map/ppermute | solution.py:325
  80.8 3.5 %shard_map.142 = (bf16[192,2048]{1,0:T(8,128)(2,1)S(1)}, bf16[192,2048]{1,0:T(8,128)(2,1)S(1)}) custom-call(s32[1]{0:T(128)} %bitcast.k_ref, f32[1,2048]{1,0:T(1,128)S(1)} %copy-done.5, bf16[192,2048]{1,0:T(8,128)(2,1)} %bitcast.17, bf16[96,2048]{1,0:T(8,128)(2,1)S(1)} %collective-permute-done.2.near, bf16[96,2048]{1,0:T(8,128)(2,1)S(1)} %collective-permute-done.3.far, ...), custom_call_target="tpu_custom_call" | custom-call | flops 603979776 | bytes 4726788 | tf_op jit(solution)/shard_map/pallas_call | solution.py:31
  84.3 2.5 %collective-permute-start.5 = (bf16[192,2048]{1,0:T(8,128)(2,1)S(1)}, bf16[192,2048]{1,0:T(8,128)(2,1)S(1)}, u32[]{:S(2)}, u32[]{:S(2)}) collective-permute-start(bf16[192,2048]{1,0:T(8,128)(2,1)S(1)} %get-tuple-element.39), channel_id=1, source_target_pairs={{0,1},{1,0},{2,3},{3,2},{4,5},{5,4},{6,7},{7,6},{8,9},{9,8},{10,11... | collective-permute-start | bytes 2359304 | tf_op jit(solution)/shard_map/ppermute | solution.py:325
  86.9 0.1 shard_map.144
  87.1 2.1 %collective-permute-start.9 = (bf16[96,2048]{1,0:T(8,128)(2,1)S(1)}, bf16[96,2048]{1,0:T(8,128)(2,1)S(1)}, u32[]{:S(2)}, u32[]{:S(2)}) collective-permute-start(bf16[96,2048]{1,0:T(8,128)(2,1)S(1)} %shard_map.144), channel_id=1, source_target_pairs={{0,2},{2,0},{1,3},{3,1},{4,6},{6,4},{5,7},{7,5},{8,10},{10,8},{9,1... | collective-permute-start | bytes 1179656 | tf_op jit(solution)/shard_map/ppermute | solution.py:322
  89.1 0.3 shard_map.143
  89.4 3.7 %collective-permute-start.6 = (bf16[96,2048]{1,0:T(8,128)(2,1)S(1)}, bf16[96,2048]{1,0:T(8,128)(2,1)S(1)}, u32[]{:S(2)}, u32[]{:S(2)}) collective-permute-start(bf16[96,2048]{1,0:T(8,128)(2,1)S(1)} %get-tuple-element.40), channel_id=1, source_target_pairs={{0,32},{2,34},{32,64},{34,66},{64,96},{66,98},{96,128},{98,130},{1... | collective-permute-start | bytes 1179656 | tf_op jit(solution)/shard_map/ppermute | solution.py:398
  93.1 3.7 %collective-permute-start.7 = (bf16[96,2048]{1,0:T(8,128)(2,1)S(1)}, bf16[96,2048]{1,0:T(8,128)(2,1)S(1)}, u32[]{:S(2)}, u32[]{:S(2)}) collective-permute-start(bf16[96,2048]{1,0:T(8,128)(2,1)S(1)} %get-tuple-element.41), channel_id=1, source_target_pairs={{0,34},{2,32},{32,66},{34,64},{64,98},{66,96},{96,130},{98,128},{1... | collective-permute-start | bytes 1179656 | tf_op jit(solution)/shard_map/ppermute | solution.py:398
  96.8 12.8 %collective-permute-done.9.other = bf16[96,2048]{1,0:T(8,128)(2,1)S(1)} collective-permute-done((bf16[96,2048]{1,0:T(8,128)(2,1)S(1)}, bf16[96,2048]{1,0:T(8,128)(2,1)S(1)}, u32[]{:S(2)}, u32[]{:S(2)}) %collective-permute-start.9) | collective-permute-done | bytes 393248 | tf_op jit(solution)/shard_map/ppermute | solution.py:322
  109.7 0.9 shard_map.145
  110.6 1.3 collective-permute-start.10
  111.9 10.4 %collective-permute-done.10.c = bf16[96,2048]{1,0:T(8,128)(2,1)S(1)} collective-permute-done((bf16[96,2048]{1,0:T(8,128)(2,1)S(1)}, bf16[96,2048]{1,0:T(8,128)(2,1)S(1)}, u32[]{:S(2)}, u32[]{:S(2)}) %collective-permute-start.10) | collective-permute-done | bytes 393248 | tf_op jit(solution)/shard_map/ppermute | solution.py:398
  122.4 3.8 %collective-permute-start.11 = (bf16[192,2048]{1,0:T(8,128)(2,1)S(1)}, bf16[192,2048]{1,0:T(8,128)(2,1)S(1)}, u32[]{:S(2)}, u32[]{:S(2)}) collective-permute-start(bf16[192,2048]{1,0:T(8,128)(2,1)S(1)} %shard_map.146.mine), channel_id=1, source_target_pairs={{0,1},{1,0},{2,3},{3,2},{4,5},{5,4},{6,7},{7,6},{8,9},{9,8},{10,11... | collective-permute-start | bytes 2359304 | tf_op jit(solution)/shard_map/ppermute | solution.py:325
  126.2 1.4 %shard_map.148 = (f32[384,128]{1,0:T(8,128)S(1)}, bf16[384,128]{1,0:T(8,128)(2,1)S(1)}) custom-call(s32[1]{0:T(128)} %bitcast.3.x_ref, bf16[8,2,384,128]{3,2,1,0:T(8,128)(2,1)} %all-to-all-done.received), custom_call_target="tpu_custom_call" | custom-call | bytes 1867780 | tf_op jit(solution)/shard_map/pallas_call | solution.py:31
  127.7 1.9 %collective-permute-start.12 = (bf16[384,128]{1,0:T(8,128)(2,1)S(1)}, bf16[384,128]{1,0:T(8,128)(2,1)S(1)}, u32[]{:S(2)}, u32[]{:S(2)}) collective-permute-start(bf16[384,128]{1,0:T(8,128)(2,1)S(1)} %get-tuple-element.47), channel_id=1, source_target_pairs={{0,2},{2,0},{1,3},{3,1},{4,6},{6,4},{5,7},{7,5},{8,10},{10,8},{9,1... | collective-permute-start | bytes 294920 | tf_op jit(solution)/shard_map/ppermute | solution.py:322
  129.6 1.2 shard_map.147
  130.8 4.6 %collective-permute-done.12.other_sum = bf16[384,128]{1,0:T(8,128)(2,1)S(1)} collective-permute-done((bf16[384,128]{1,0:T(8,128)(2,1)S(1)}, bf16[384,128]{1,0:T(8,128)(2,1)S(1)}, u32[]{:S(2)}, u32[]{:S(2)}) %collective-permute-start.12) | collective-permute-done | bytes 98336 | tf_op jit(solution)/shard_map/ppermute | solution.py:322
  135.4 1.2 shard_map.149
  (29 shorter events, 0.2 us)
Async XLA Ops:
  2.7 8.7 %collective-permute-start.1 = (bf16[128,384]{1,0:T(8,128)(2,1)S(1)}, bf16[128,384]{1,0:T(8,128)(2,1)S(1)}, u32[]{:S(2)}, u32[]{:S(2)}) collective-permute-start(bf16[128,384]{1,0:T(8,128)(2,1)S(1)} %get-tuple-element.27), channel_id=1, source_target_pairs={{0,2},{2,0},{1,3},{3,1},{4,6},{6,4},{5,7},{7,5},{8,10},{10,8},{9,1... | collective-permute-start | bytes 294920 | tf_op jit(solution)/shard_map/ppermute | solution.py:322
  9.5 27.4 %collective-permute-start = (bf16[192,2048]{1,0:T(8,128)(2,1)S(1)}, bf16[192,2048]{1,0:T(8,128)(2,1)S(1)}, u32[]{:S(2)}, u32[]{:S(2)}) collective-permute-start(bf16[192,2048]{1,0:T(8,128)(2,1)S(1)} %get-tuple-element.29), channel_id=1, source_target_pairs={{0,2},{2,0},{1,3},{3,1},{4,6},{6,4},{5,7},{7,5},{8,10},{10,8},{9,1... | collective-permute-start | bytes 2359304 | tf_op jit(solution)/shard_map/ppermute | solution.py:322
  36.8 12.3 %copy-start.8 = (bf16[192,2048]{1,0:T(8,128)(2,1)}, bf16[192,2048]{1,0:T(8,128)(2,1)S(1)}, u32[]{:S(2)}) copy-start(bf16[192,2048]{1,0:T(8,128)(2,1)S(1)} %collective-permute-done.near) | copy-start | bytes 2359300
  36.8 13.9 %copy-start.5 = (f32[1,2048]{1,0:T(1,128)S(1)}, f32[1,2048]{1,0:T(1,128)}, u32[]{:S(2)}) copy-start(f32[1,2048]{1,0:T(1,128)} %gain_ref.1) | copy-start | bytes 24580
  36.8 13.9 %collective-permute-start.4 = (bf16[192,2048]{1,0:T(8,128)(2,1)S(1)}, bf16[192,2048]{1,0:T(8,128)(2,1)S(1)}, u32[]{:S(2)}, u32[]{:S(2)}) collective-permute-start(bf16[192,2048]{1,0:T(8,128)(2,1)S(1)} %collective-permute-done.near), channel_id=1, source_target_pairs={{0,1},{1,0},{2,3},{3,2},{4,5},{5,4},{6,7},{7,6},{8,9},{9,8},{10,11... | collective-permute-start | bytes 2359304 | tf_op jit(solution)/shard_map/ppermute | solution.py:325
  56.9 69.3 %all-to-all-start = ((bf16[8,2,384,128]{3,2,1,0:T(8,128)(2,1)}), bf16[8,2,384,128]{3,2,1,0:T(8,128)(2,1)}, u32[]{:S(2)}, u32[]{:S(2)}) async-start(bf16[8,2,384,128]{3,2,1,0:T(8,128)(2,1)} %bitcast.33), calls=%async_computation | async-start | bytes 3145728 | tf_op jit(solution)/shard_map/all_to_all | solution.py:328
  61.2 13.8 %collective-permute-start.2 = (bf16[96,2048]{1,0:T(8,128)(2,1)S(1)}, bf16[96,2048]{1,0:T(8,128)(2,1)S(1)}, u32[]{:S(2)}, u32[]{:S(2)}) collective-permute-start(bf16[96,2048]{1,0:T(8,128)(2,1)S(1)} %get-tuple-element.32), channel_id=1, source_target_pairs={{0,2},{2,0},{1,3},{3,1},{4,6},{6,4},{5,7},{7,5},{8,10},{10,8},{9,1... | collective-permute-start | bytes 1179656 | tf_op jit(solution)/shard_map/ppermute | solution.py:322
  75.0 5.8 %collective-permute-start.3 = (bf16[96,2048]{1,0:T(8,128)(2,1)S(1)}, bf16[96,2048]{1,0:T(8,128)(2,1)S(1)}, u32[]{:S(2)}, u32[]{:S(2)}) collective-permute-start(bf16[96,2048]{1,0:T(8,128)(2,1)S(1)} %collective-permute-done.2.near), channel_id=1, source_target_pairs={{0,1},{1,0},{2,3},{3,2},{4,5},{5,4},{6,7},{7,6},{8,9},{9,8},{10,11... | collective-permute-start | bytes 1179656 | tf_op jit(solution)/shard_map/ppermute | solution.py:325
  78.9 8.0 %collective-permute-start.8 = (bf16[192,2048]{1,0:T(8,128)(2,1)S(1)}, bf16[192,2048]{1,0:T(8,128)(2,1)S(1)}, u32[]{:S(2)}, u32[]{:S(2)}) collective-permute-start(bf16[192,2048]{1,0:T(8,128)(2,1)S(1)} %get-tuple-element.36), channel_id=1, source_target_pairs={{0,1},{1,0},{2,3},{3,2},{4,5},{5,4},{6,7},{7,6},{8,9},{9,8},{10,11... | collective-permute-start | bytes 2359304 | tf_op jit(solution)/shard_map/ppermute | solution.py:325
  84.3 4.8 %copy-start = (bf16[1,192,2048]{2,1,0:T(8,128)(2,1)S(1)}, bf16[1,192,2048]{2,1,0:T(8,128)(2,1)}, u32[]{:S(2)}) copy-start(bf16[1,192,2048]{2,1,0:T(8,128)(2,1)} %param.11) | copy-start | bytes 2359300
  84.3 4.8 %collective-permute-start.5 = (bf16[192,2048]{1,0:T(8,128)(2,1)S(1)}, bf16[192,2048]{1,0:T(8,128)(2,1)S(1)}, u32[]{:S(2)}, u32[]{:S(2)}) collective-permute-start(bf16[192,2048]{1,0:T(8,128)(2,1)S(1)} %get-tuple-element.39), channel_id=1, source_target_pairs={{0,1},{1,0},{2,3},{3,2},{4,5},{5,4},{6,7},{7,6},{8,9},{9,8},{10,11... | collective-permute-start | bytes 2359304 | tf_op jit(solution)/shard_map/ppermute | solution.py:325
  87.0 22.6 %copy-start.1 = (bf16[1,192,2048]{2,1,0:T(8,128)(2,1)S(1)}, bf16[1,192,2048]{2,1,0:T(8,128)(2,1)}, u32[]{:S(2)}) copy-start(bf16[1,192,2048]{2,1,0:T(8,128)(2,1)} %param.12) | copy-start | bytes 2359300
  87.0 22.6 %copy-start.2 = (bf16[1,192,2048]{2,1,0:T(8,128)(2,1)S(1)}, bf16[1,192,2048]{2,1,0:T(8,128)(2,1)}, u32[]{:S(2)}) copy-start(bf16[1,192,2048]{2,1,0:T(8,128)(2,1)} %param.13) | copy-start | bytes 2359300
  87.1 22.6 %collective-permute-start.9 = (bf16[96,2048]{1,0:T(8,128)(2,1)S(1)}, bf16[96,2048]{1,0:T(8,128)(2,1)S(1)}, u32[]{:S(2)}, u32[]{:S(2)}) collective-permute-start(bf16[96,2048]{1,0:T(8,128)(2,1)S(1)} %shard_map.144), channel_id=1, source_target_pairs={{0,2},{2,0},{1,3},{3,1},{4,6},{6,4},{5,7},{7,5},{8,10},{10,8},{9,1... | collective-permute-start | bytes 1179656 | tf_op jit(solution)/shard_map/ppermute | solution.py:322
  89.4 22.5 %collective-permute-start.6 = (bf16[96,2048]{1,0:T(8,128)(2,1)S(1)}, bf16[96,2048]{1,0:T(8,128)(2,1)S(1)}, u32[]{:S(2)}, u32[]{:S(2)}) collective-permute-start(bf16[96,2048]{1,0:T(8,128)(2,1)S(1)} %get-tuple-element.40), channel_id=1, source_target_pairs={{0,32},{2,34},{32,64},{34,66},{64,96},{66,98},{96,128},{98,130},{1... | collective-permute-start | bytes 1179656 | tf_op jit(solution)/shard_map/ppermute | solution.py:398
  93.1 18.8 %collective-permute-start.7 = (bf16[96,2048]{1,0:T(8,128)(2,1)S(1)}, bf16[96,2048]{1,0:T(8,128)(2,1)S(1)}, u32[]{:S(2)}, u32[]{:S(2)}) collective-permute-start(bf16[96,2048]{1,0:T(8,128)(2,1)S(1)} %get-tuple-element.41), channel_id=1, source_target_pairs={{0,34},{2,32},{32,66},{34,64},{64,98},{66,96},{96,130},{98,128},{1... | collective-permute-start | bytes 1179656 | tf_op jit(solution)/shard_map/ppermute | solution.py:398
  110.6 11.7 %collective-permute-start.10 = (bf16[96,2048]{1,0:T(8,128)(2,1)S(1)}, bf16[96,2048]{1,0:T(8,128)(2,1)S(1)}, u32[]{:S(2)}, u32[]{:S(2)}) collective-permute-start(bf16[96,2048]{1,0:T(8,128)(2,1)S(1)} %shard_map.145), channel_id=1, source_target_pairs={{32,0},{34,2},{64,32},{66,34},{96,64},{98,66},{128,96},{130,98},{1... | collective-permute-start | bytes 1179656 | tf_op jit(solution)/shard_map/ppermute | solution.py:398
  122.4 13.0 %copy-start.3 = (s32[1,2,128,256]{3,2,1,0:T(8,128)S(1)}, s32[1,2,128,256]{3,2,1,0:T(8,128)}, u32[]{:S(2)}) copy-start(s32[1,2,128,256]{3,2,1,0:T(8,128)} %param.17) | copy-start | bytes 786436
  122.4 13.0 %copy-start.4 = (s32[1,256,128]{2,1,0:T(8,128)S(1)}, s32[1,256,128]{2,1,0:T(8,128)}, u32[]{:S(2)}) copy-start(s32[1,256,128]{2,1,0:T(8,128)} %param.18) | copy-start | bytes 393220
  122.4 13.0 %copy-start.6 = (f32[1,2,2,128,1]{3,4,2,1,0:T(1,128)S(1)}, f32[1,2,2,128,1]{3,4,2,1,0:T(1,128)}, u32[]{:S(2)}) copy-start(f32[1,2,2,128,1]{3,4,2,1,0:T(1,128)} %param.19) | copy-start | bytes 6148
  122.4 13.0 %copy-start.7 = (f32[1,2,1,128]{3,2,1,0:T(1,128)S(1)}, f32[1,2,1,128]{3,2,1,0:T(1,128)}, u32[]{:S(2)}) copy-start(f32[1,2,1,128]{3,2,1,0:T(1,128)} %param.20) | copy-start | bytes 3076
  122.4 7.2 %collective-permute-start.11 = (bf16[192,2048]{1,0:T(8,128)(2,1)S(1)}, bf16[192,2048]{1,0:T(8,128)(2,1)S(1)}, u32[]{:S(2)}, u32[]{:S(2)}) collective-permute-start(bf16[192,2048]{1,0:T(8,128)(2,1)S(1)} %shard_map.146.mine), channel_id=1, source_target_pairs={{0,1},{1,0},{2,3},{3,2},{4,5},{5,4},{6,7},{7,6},{8,9},{9,8},{10,11... | collective-permute-start | bytes 2359304 | tf_op jit(solution)/shard_map/ppermute | solution.py:325
  127.7 7.7 %collective-permute-start.12 = (bf16[384,128]{1,0:T(8,128)(2,1)S(1)}, bf16[384,128]{1,0:T(8,128)(2,1)S(1)}, u32[]{:S(2)}, u32[]{:S(2)}) collective-permute-start(bf16[384,128]{1,0:T(8,128)(2,1)S(1)} %get-tuple-element.47), channel_id=1, source_target_pairs={{0,2},{2,0},{1,3},{3,1},{4,6},{6,4},{5,7},{7,5},{8,10},{10,8},{9,1... | collective-permute-start | bytes 294920 | tf_op jit(solution)/shard_map/ppermute | solution.py:322
